TPU v7x, 128 devices: a whole 4x4x4 slice. The times are simulated.
128 devices in a mesh: visit: 8 (over x, core), fp: 16 (over y, z).
Axes of the slice: x: 4, y: 4, z: 4, core: 2. Of those that a mesh axis runs over, the one named last changes fastest.
Arguments:
- image: bfloat16 [8, 4096, 4096], P('visit', 'fp'), may hold values from -6 to 6
- inv_var: bfloat16 [8, 4096, 4096], P('visit', 'fp'), may hold values from 0.25 to 4
- bg_grid: float32 [8, 16, 16, 128], P('visit', 'fp'), may hold values from -6 to 6
- bg_mix: float32 [16, 16], replicated, may hold values from -1.5 to 1.5
- psf_taps: float32 [8, 16, 21], P('visit', 'fp'), may hold values from 0.05 to 1
- warp_shift: int32 [8, 16], P('visit', 'fp'), may hold values from 0 to 63
- bad_cols: int32 [16, 32], P('fp'), may hold values from 0 to 4095
- piece_patch: int32 [8, 256, 1], P('visit', 'fp'), may hold values from 0 to 15; in each aligned block of 16 rows (0 to 15, 16 to 31, ..., all dimensions but the last counted through in order) at most 2 rows name the same one
- piece_pos: int32 [8, 256], P('visit', 'fp'), may hold values from 0 to 440
- band_of_visit: int32 [8], replicated, may hold values from 0 to 3, as said below
Outputs:
- flux_sum: float32 [4, 16, 456, 4096], P(None, 'fp', None, 'visit')
- weight_sum: float32 [4, 16, 456, 4096], P(None, 'fp', None, 'visit')
Inputs may be any that keep to these rules, and one draw needn't show every extreme that they name: `piece_patch`: among the 16 pieces of one CCD group in one visit, at most 2 name the same patch; some group names a patch exactly 2 times. `band_of_visit`: each band is named by exactly 2 visits.
All inputs are finite; a program needn't handle non-finite values.
Results may differ from a plain program's by a relative error of at most 0.0055.
Values may be sent and summed in bfloat16 or wider, within the bound.
No kernel may reach another device: no remote copies, remote signals or barrier semaphores. Data moves between devices by JAX's collectives and lax.ppermute only.
A program may use at most 192 MiB of HBM per device.

v0:
```python
import jax
import jax.numpy as jnp
from jax import lax
from jax.sharding import PartitionSpec as P

ROW_PIX = 4096
BANDS = 4
CCD_ROWS = 256
MOST = 2
BORDER = 100
BLOCK = 256
TAPS_HALF = 10
FRAME = 456
HALF = 16
WINDOW = 288


def extended(shard, sides, width):
    for axis, dim in sides:
        peers, length = (lax.axis_size(axis), shard.shape[dim])
        up = [(i, (i + 1) % peers) for i in range(peers - 1)]
        down = [(j, i) for i, j in up]
        last = lax.slice_in_dim(shard, length - width, length, axis=dim)
        leading = lax.slice_in_dim(shard, 0, width, axis=dim)
        before = lax.ppermute(last, axis, up)
        after = lax.ppermute(leading, axis, down)
        shard = jnp.concatenate([before, shard, after], axis=dim)
    return shard


def make_kernel(tap_vals, shift):
    tap_vals = tap_vals / jnp.sum(tap_vals)
    offset = shift.astype(jnp.float32) / 16.0
    tap_steps = jnp.arange(-2, 7, dtype=jnp.int32).astype(jnp.float32)
    lag_values = offset - tap_steps
    lanczos = jnp.where(
        jnp.abs(lag_values) < 3.0, jnp.sinc(lag_values) * jnp.sinc(lag_values / 3.0), 0.0
    )
    lanczos = lanczos / jnp.sum(lanczos)
    kernel = jnp.zeros((2 * HALF + 1,), jnp.float32)
    for position in range(9):
        tap_start = position - 2 - TAPS_HALF + HALF
        kernel = kernel + lanczos[position] * jnp.pad(
            tap_vals, (tap_start, 2 * HALF + 1 - tap_start - tap_vals.shape[0])
        )
    return kernel


def banded(kernels):
    lag_grid = (
        jnp.arange(WINDOW, dtype=jnp.int32)[:, None] - jnp.arange(BLOCK, dtype=jnp.int32)[None, :]
    )
    offsets = jnp.arange(2 * HALF + 1, dtype=jnp.int32)
    pick_table = (lag_grid[:, :, None] == offsets[None, None, :]).astype(jnp.bfloat16)
    return jnp.einsum(
        "iog,...g->...io", pick_table, kernels, preferred_element_type=jnp.float32
    ).astype(jnp.bfloat16)


def convolve_rows(pixel_rows, matrices):
    lead_dims = pixel_rows.shape[:-1]
    block_count = ROW_PIX // BLOCK
    padded = jnp.pad(pixel_rows, [(0, 0)] * (pixel_rows.ndim - 1) + [(HALF, BLOCK - HALF)])
    tile_rows = padded.reshape(lead_dims + (block_count + 1, BLOCK))
    windows = jnp.concatenate(
        [tile_rows[..., :block_count, :], tile_rows[..., 1:, : 2 * HALF]], axis=-1
    )
    result = jnp.einsum(
        "...cnbi,...cio->...cnbo", windows, matrices, preferred_element_type=jnp.float32
    )
    return result.reshape(pixel_rows.shape).astype(jnp.bfloat16)


def shards(
    image,
    inv_var,
    bg_grid,
    bg_mix,
    psf_taps,
    warp_shift,
    bad_cols,
    piece_patch,
    piece_pos,
    band_of_visit,
):
    all_grids = lax.all_gather(bg_grid, "fp", axis=1, tiled=True)[0]
    mix_row = lax.dynamic_slice_in_dim(bg_mix, lax.axis_index("fp"), 1, 0)
    bg_model = jnp.einsum("ck,kab->cab", mix_row, all_grids, precision=lax.Precision.HIGHEST)[0]
    grid_count, bin_count = bg_model.shape
    backdrop = jnp.broadcast_to(
        bg_model[:, None, :, None],
        (grid_count, CCD_ROWS // grid_count, bin_count, ROW_PIX // bin_count),
    ).reshape(CCD_ROWS, ROW_PIX)
    columns = jnp.arange(ROW_PIX, dtype=jnp.int32)
    good_cols = 1.0 - jnp.any(bad_cols[0][:, None] == columns[None, :], axis=0).astype(jnp.float32)
    flux_in = ((image[0].astype(jnp.float32) - backdrop) * good_cols).astype(jnp.bfloat16)
    ivar_in = (inv_var[0].astype(jnp.float32) * good_cols).astype(jnp.bfloat16)
    kernel = make_kernel(psf_taps[0, 0], warp_shift[0, 0])
    taps_pair = jnp.stack([kernel.astype(jnp.bfloat16), jnp.abs(kernel).astype(jnp.bfloat16)])
    patches = piece_patch[0, :, 0]
    starts = piece_pos[0]
    piece_count = patches.shape[0]
    piece_rows = CCD_ROWS // piece_count
    owner_count = lax.axis_size("fp")
    piece_ids = jnp.arange(piece_count, dtype=jnp.int32)
    earlier = piece_ids[:, None] > piece_ids[None, :]
    same_patch = patches[:, None] == patches[None, :]
    slot_rank = jnp.sum((earlier & same_patch).astype(jnp.int32), axis=1)
    chooser = (
        patches[None, None, :] == jnp.arange(owner_count, dtype=jnp.int32)[:, None, None]
    ) & (slot_rank[None, None, :] == jnp.arange(MOST, dtype=jnp.int32)[None, :, None])
    slot_used = jnp.any(chooser, axis=2)
    slot_start = jnp.where(
        slot_used, jnp.sum(jnp.where(chooser, starts[None, None, :], 0), axis=2), FRAME
    )
    chooser_bf = chooser.astype(jnp.bfloat16)
    warped = convolve_rows(jnp.stack([flux_in, ivar_in]), banded(taps_pair))
    grouped = warped.reshape(2, piece_count, piece_rows, ROW_PIX)
    received = lax.all_to_all(
        jnp.einsum(
            "dsj,cjpw->dcspw", chooser_bf, grouped, preferred_element_type=jnp.float32
        ).astype(jnp.bfloat16),
        "fp",
        split_axis=0,
        concat_axis=0,
        tiled=True,
    )
    arrived_start = lax.all_to_all(slot_start, "fp", split_axis=0, concat_axis=0, tiled=True)
    products = received.astype(jnp.float32)
    flux_term = products[:, 1] * products[:, 0]
    weight_term = products[:, 1]
    dest_rows = arrived_start[:, :, None] + jnp.arange(piece_rows, dtype=jnp.int32)[None, None, :]
    frame_terms = jnp.stack([flux_term, weight_term]).reshape(2, -1, ROW_PIX)
    frame_sums = (
        jnp.zeros((2, FRAME, ROW_PIX), jnp.float32)
        .at[:, dest_rows.reshape(-1)]
        .add(frame_terms, mode="drop")
    )
    partial_value = frame_sums.astype(jnp.bfloat16)
    edge_rows = 2 * BORDER
    band_onehot = (band_of_visit[:, None] == jnp.arange(BANDS, dtype=jnp.int32)[None, :]).astype(
        jnp.float32
    )
    framed = extended(partial_value, (("fp", 1),), edge_rows).astype(jnp.float32)
    summed = partial_value.astype(jnp.float32)
    summed = summed.at[:, :edge_rows].add(framed[:, :edge_rows])
    summed = summed.at[:, FRAME - edge_rows :].add(framed[:, FRAME + edge_rows :])
    shares = lax.all_to_all(summed[None], "visit", split_axis=3, concat_axis=0, tiled=True)
    band_totals = jnp.einsum("vb,vcew->bcew", band_onehot, shares, precision=lax.Precision.HIGHEST)
    return (band_totals[:, 0][:, None], band_totals[:, 1][:, None])


def solution(mesh):
    placed = (
        P("visit", "fp", None),
        P("visit", "fp", None),
        P("visit", "fp", None, None),
        P(),
        P("visit", "fp", None),
        P("visit", "fp"),
        P("fp", None),
        P("visit", "fp", None),
        P("visit", "fp"),
        P(),
    )
    return jax.shard_map(
        shards,
        mesh=mesh,
        in_specs=placed,
        out_specs=(P(None, "fp", None, "visit"), P(None, "fp", None, "visit")),
        check_vma=False,
    )
```

profile of v0, /device:TPU:104, one launch (start us, length us, event | category | flops | bytes accessed | tf_op | source)
XLA Modules:
  0.0 819.6 jit_solution(14045676072112319958)
XLA Ops:
  3.8 7.0 all-to-all-start
  11.7 22.0 %all_gather.3 = f32[1,16,16,128]{3,2,0,1:T(8,128)S(1)} all-gather(f32[1,1,16,128]{3,2,0,1:T(8,128)} %bitcast.83), channel_id=1, replica_groups=mesh['visit'=8,'fp'=16] {'fp'}, dimensions={1}, use_global_device_ids=true | all-gather | bytes 139264 | tf_op jit(solution)/shard_map/all_gather | solution.py:86
  34.0 7.9 broadcast_in_dim.60
  41.9 13.3 %reshape.241 = f32[1,256,4096]{2,1,0:T(8,128)} reshape(f32[16,16,128,32]{3,2,1,0:T(8,128)} %broadcast_in_dim.60) | data formatting | bytes 8388608 | tf_op jit(solution)/shard_map/reshape | solution.py:93
  93.7 7.8 convert_element_type.105
  107.0 16.2 %copy.65 = bf16[16,2,2,16,4096]{4,2,3,1,0:T(2,128)(2,1)} copy(bf16[16,2,2,16,4096]{4,0,2,3,1:T(8,128)(2,1)S(1)} %convert_bitcast_fusion) | data formatting | bytes 16777216 | tf_op jit(solution)/shard_map/convert_element_type | solution.py:122
  123.2 6.9 all-to-all-start.1
  130.3 95.6 %all-to-all-done.1 = bf16[16,2,2,16,4096]{4,2,3,1,0:T(2,128)(2,1)} async-done(((bf16[16,2,2,16,4096]{4,2,3,1,0:T(2,128)(2,1)}), bf16[16,2,2,16,4096]{4,2,3,1,0:T(2,128)(2,1)}, u32[]{:S(2)}, u32[]{:S(2)}) %all-to-all-start.1) | async-done | bytes 8388640 | tf_op jit(solution)/shard_map/all_to_all | solution.py:119
  225.9 26.0 %copy_convert_fusion = f32[16,2,2,16,4096]{4,3,2,0,1:T(8,128)} fusion(bf16[16,2,2,16,4096]{4,2,3,1,0:T(2,128)(2,1)} %all-to-all-done.1), kind=kLoop, calls=%fused_computation.7 | loop fusion | flops 4194304 | bytes 25165824 | tf_op jit(solution)/shard_map/convert_element_type | solution.py:129
  251.9 11.0 %fusion.45 = (f32[16,1,2,16,4096]{4,3,2,0,1:T(8,128)}, f32[16,1,2,16,4096]{4,3,2,0,1:T(8,128)}) fusion(f32[16,2,2,16,4096]{4,3,2,0,1:T(8,128)} %copy_convert_fusion), kind=kLoop, calls=%fused_computation.94 | loop fusion | bytes 33554432 | tf_op jit(solution)/shard_map/slice | solution.py:130
  262.9 11.1 %bitcast_multiply_fusion = f32[1,512,4096]{2,1,0:T(8,128)} fusion(f32[16,1,2,16,4096]{4,3,2,0,1:T(8,128)} %get-tuple-element.41, f32[16,1,2,16,4096]{4,3,2,0,1:T(8,128)} %get-tuple-element.42), kind=kLoop, calls=%fused_computation.6 | loop fusion | flops 2097152 | bytes 25165824 | tf_op jit(solution)/shard_map/mul | solution.py:130
  274.1 6.6 maximum_bitcast_fusion
  280.7 18.9 %copy.67 = f32[512,2,4096]{2,1,0:T(2,128)} copy(f32[512,2,4096]{2,0,1:T(8,128)S(1)} %maximum_bitcast_fusion) | data formatting | bytes 33554432 | tf_op jit(solution)/shard_map/stack | solution.py:133
  299.5 8.0 broadcast_in_dim.33
  307.5 103.4 %scatter_fusion = f32[2,456,4096]{2,0,1:T(2,128)} fusion(f32[2,456,4096]{2,0,1:T(2,128)} %broadcast_in_dim.33, s32[512]{0:T(512)S(1)} %bitcast.82, f32[512,2,4096]{2,1,0:T(2,128)} %copy.67), kind=kCustom, calls=%fused_computation | custom fusion | flops 4194304 | bytes 50333696 | tf_op jit(solution)/shard_map/scatter-add | solution.py:137
  411.0 12.2 %fusion.44 = (f32[2,456,4096]{2,0,1:T(2,128)S(1)}, bf16[2,456,4096]{2,0,1:T(2,128)(2,1)}) fusion(f32[2,456,4096]{2,0,1:T(2,128)} %scatter_fusion), kind=kLoop, calls=%fused_computation.93 | loop fusion | flops 7471104 | bytes 37355520 | tf_op jit(solution)/shard_map/convert_element_type | solution.py:145
  423.2 9.2 %fusion.47 = (bf16[2,200,4096]{2,0,1:T(2,128)(2,1)S(1)}, bf16[2,200,4096]{2,0,1:T(2,128)(2,1)S(1)}) fusion(bf16[2,456,4096]{2,0,1:T(2,128)(2,1)} %get-tuple-element.38), kind=kLoop, calls=%fused_computation.96 | loop fusion | bytes 13107200 | tf_op jit(solution)/shard_map/slice | solution.py:23
  438.3 68.0 %collective-permute-done = bf16[2,200,4096]{2,0,1:T(2,128)(2,1)S(1)} collective-permute-done((bf16[2,200,4096]{2,0,1:T(2,128)(2,1)S(1)}, bf16[2,200,4096]{2,0,1:T(2,128)(2,1)S(1)}, u32[]{:S(2)}, u32[]{:S(2)}) %collective-permute-start) | collective-permute-done | bytes 3276832 | tf_op jit(solution)/shard_map/ppermute | solution.py:25
  510.3 21.3 %fusion.5 = f32[2,456,4096]{2,0,1:T(2,128)S(1)} fusion(f32[2,456,4096]{2,0,1:T(2,128)S(1)} %get-tuple-element.37, bf16[2,200,4096]{2,0,1:T(2,128)(2,1)S(1)} %collective-permute-done.1, bf16[2,456,4096]{2,0,1:T(2,128)(2,1)S(1)} %copy-done.2, bf16[2,200,4096]{2,0,1:T(2,128)(2,1)S(1)} %collective-permute-done), kind=kLoop, calls=%fused_computation.13 | loop fusion | flops 11468800 | bytes 27131904 | tf_op jit(solution)/shard_map/scatter-add | solution.py:146
  536.9 19.9 %fusion.4 = f32[1,2,456,4096]{3,1,2,0:T(2,128)} fusion(f32[1,2,456,4096]{3,1,2,0:T(2,128)} %copy.94, f32[2,456,4096]{2,0,1:T(2,128)S(1)} %fusion.5, bf16[2,200,4096]{2,0,1:T(2,128)(2,1)} %copy-done.3, bf16[2,456,4096]{2,0,1:T(2,128)(2,1)} %get-tuple-element.38, bf16[2,200,4096]{2,0,1:T(2,128)(2,1)S(1)} %collective-permute-done), kind=kLoop, calls=%fused_computation.11 | loop fusion | flops 11468800 | bytes 27131904 | tf_op jit(solution)/shard_map/scatter-add | solution.py:147
  556.9 30.6 %copy.68 = f32[1,2,456,4096]{2,1,0,3:T(2,128)} copy(f32[1,2,456,4096]{3,1,2,0:T(2,128)} %fusion.4) | data formatting | bytes 29884416 | tf_op jit(solution)/shard_map/scatter-add | solution.py:147
  587.5 194.9 %all_to_all.29 = f32[1,2,456,4096]{2,1,0,3:T(2,128)} all-to-all(f32[1,2,456,4096]{2,1,0,3:T(2,128)} %copy.68), channel_id=1, replica_groups=mesh['visit'=8,'fp'=16] {'visit'}, dimensions={3} | all-to-all | bytes 29884416 | tf_op jit(solution)/shard_map/all_to_all | solution.py:148
  782.4 19.0 %copy.83 = f32[1,2,456,8,512]{4,3,2,1,0:T(8,128)} copy(f32[1,2,456,8,512]{2,1,4,3,0:T(2,128)} %bitcast.75) | data formatting | bytes 29884416 | tf_op jit(solution)/shard_map/all_to_all | solution.py:148
  801.5 10.5 %fusion = f32[4,2,456,512]{3,0,2,1:T(4,128)S(1)} fusion(f32[1,2,456,8,512]{4,3,2,1,0:T(8,128)} %copy.83, s32[8]{0:T(128)S(1)} %copy-done.5), kind=kOutput, calls=%fused_computation.2 | convolution fusion | flops 179306528 | bytes 22413344 | tf_op jit(solution)/shard_map/vb,vcew->bcew/dot_general | solution.py:149
  (52 shorter events, 70.2 us)
Async XLA Ops:
  0.6 33.1 %copy-start = (f32[16,16]{1,0:T(8,128)S(1)}, f32[16,16]{1,0:T(8,128)}, u32[]{:S(2)}) copy-start(f32[16,16]{1,0:T(8,128)} %param.18) | copy-start | bytes 3076
  3.8 119.4 %all-to-all-start = ((s32[16,1,2]{2,1,0:T(1,128)}), s32[16,1,2]{2,1,0:T(1,128)S(1)}, u32[]{:S(2)}, u32[]{:S(2)}) async-start(s32[16,1,2]{2,1,0:T(1,128)} %copy.57), calls=%async_computation | async-start | bytes 16384 | tf_op jit(solution)/shard_map/all_to_all | solution.py:128
  41.9 13.3 %copy-start.4 = (bf16[1,256,4096]{2,1,0:T(8,128)(2,1)S(1)}, bf16[1,256,4096]{2,1,0:T(8,128)(2,1)}, u32[]{:S(2)}) copy-start(bf16[1,256,4096]{2,1,0:T(8,128)(2,1)} %param.15) | copy-start | bytes 6291460
  70.4 4.4 copy-start.6
  123.2 102.7 %all-to-all-start.1 = ((bf16[16,2,2,16,4096]{4,2,3,1,0:T(2,128)(2,1)}), bf16[16,2,2,16,4096]{4,2,3,1,0:T(2,128)(2,1)}, u32[]{:S(2)}, u32[]{:S(2)}) async-start(bf16[16,2,2,16,4096]{4,2,3,1,0:T(2,128)(2,1)} %copy.65), calls=%async_computation.1 | async-start | bytes 16777216 | tf_op jit(solution)/shard_map/all_to_all | solution.py:119
  423.2 87.2 %copy-start.2 = (bf16[2,456,4096]{2,0,1:T(2,128)(2,1)S(1)}, bf16[2,456,4096]{2,0,1:T(2,128)(2,1)}, u32[]{:S(2)}) copy-start(bf16[2,456,4096]{2,0,1:T(2,128)(2,1)} %get-tuple-element.38) | copy-start | bytes 22413316
  432.4 73.9 %collective-permute-start = (bf16[2,200,4096]{2,0,1:T(2,128)(2,1)S(1)}, bf16[2,200,4096]{2,0,1:T(2,128)(2,1)S(1)}, u32[]{:S(2)}, u32[]{:S(2)}) collective-permute-start(bf16[2,200,4096]{2,0,1:T(2,128)(2,1)S(1)} %get-tuple-element.45), channel_id=1, source_target_pairs={{0,1},{1,2},{2,3},{3,4},{4,5},{5,6},{6,7},{7,8},{8,9},{9,10},{10,1... | collective-permute-start | bytes 9830408 | tf_op jit(solution)/shard_map/ppermute | solution.py:25
  434.4 76.0 %collective-permute-start.1 = (bf16[2,200,4096]{2,0,1:T(2,128)(2,1)S(1)}, bf16[2,200,4096]{2,0,1:T(2,128)(2,1)S(1)}, u32[]{:S(2)}, u32[]{:S(2)}) collective-permute-start(bf16[2,200,4096]{2,0,1:T(2,128)(2,1)S(1)} %get-tuple-element.46), channel_id=1, source_target_pairs={{1,0},{2,1},{3,2},{4,3},{5,4},{6,5},{7,6},{8,7},{9,8},{10,9},{11,1... | collective-permute-start | bytes 9830408 | tf_op jit(solution)/shard_map/ppermute | solution.py:26
  510.3 21.3 %copy-start.3 = (bf16[2,200,4096]{2,0,1:T(2,128)(2,1)}, bf16[2,200,4096]{2,0,1:T(2,128)(2,1)S(1)}, u32[]{:S(2)}) copy-start(bf16[2,200,4096]{2,0,1:T(2,128)(2,1)S(1)} %collective-permute-done.1) | copy-start | bytes 9830404
  782.4 19.1 %copy-start.5 = (s32[8]{0:T(128)S(1)}, s32[8]{0:T(128)}, u32[]{:S(2)}) copy-start(s32[8]{0:T(128)} %param.24) | copy-start | bytes 100
  813.3 6.0 copy-start.1
where the time goes:
time: 825 us; the launch traced here: 820 us
  other arithmetic  219 us (27%)
  blocking collectives  217 us (26%)
  local copies, waits for them, and re-layouts  172 us (21%)
  waiting for transfers between devices  168 us (20%)
  matrix products  23.2 us (3%)
  starting transfers between devices  19.8 us (2%)
    all_to_all x1, blocking collectives, shards(): lax.all_to_all(summed[None], 'visit', split_axis=3, concat_axis=0, tiled=...  195 us
    scatter-add x1, other arithmetic, shards(): frame_sums = jnp.zeros((2, FRAME, ROW_PIX), jnp.float32).at[:, dest_rows....  103 us
    all_to_all x1, waiting for transfers between devices, shards(): lax.all_to_all(jnp.einsum('dsj,cjpw->dcspw', chooser_bf, grouped, preferr...  95.6 us
    ppermute x1, waiting for transfers between devices, extended(): before = lax.ppermute(last, axis, up)  68 us
    scatter-add x1, local copies, waits for them, and re-layouts, shards(): summed = summed.at[:, FRAME - edge_rows:].add(framed[:, FRAME + edge_rows:])  30.6 us
    convert_element_type x1, other arithmetic, shards(): products = received.astype(jnp.float32)  26 us
    all_gather x1, blocking collectives, shards(): all_grids = lax.all_gather(bg_grid, 'fp', axis=1, tiled=True)[0]  22 us
    scatter-add x1, other arithmetic, shards(): summed = summed.at[:, :edge_rows].add(framed[:, :edge_rows])  21.3 us
  transfers between devices with their start and end apart: 4, of which 3 were waited for; matrix products, arithmetic and copies ran while one was open for 11% of the time, Pallas kernels for 0%

commit v1 on v0

v1 whole, which is shorter than its diff:
```python
import jax
import jax.numpy as jnp
from jax import lax
from jax.experimental import pallas as pl
from jax.experimental.pallas import tpu as pltpu
from jax.sharding import PartitionSpec as P

ROW_PIX = 4096
BANDS = 4
CCD_ROWS = 256
MOST = 2
BORDER = 100
EDGE = 2 * BORDER
TAPS_HALF = 10
FRAME = 456
HALF = 16
TAPS = 2 * HALF + 1
PIECES = 16
PIECE_ROWS = 16
BINS = 128
BIN_PIX = ROW_PIX // BINS
PATCHES = 16
VISITS = 8
SPAN = ROW_PIX // VISITS
BLOCK = 256
PAD = 128
WINDOW = BLOCK + 2 * PAD
UNUSED = 1 << 20
VMEM_LIMIT = 48 << 20


def make_kernel(tap_vals, shift):
    tap_vals = tap_vals / jnp.sum(tap_vals)
    offset = shift.astype(jnp.float32) / 16.0
    tap_steps = jnp.arange(-2, 7, dtype=jnp.int32).astype(jnp.float32)
    lag_values = offset - tap_steps
    lanczos = jnp.where(
        jnp.abs(lag_values) < 3.0, jnp.sinc(lag_values) * jnp.sinc(lag_values / 3.0), 0.0
    )
    lanczos = lanczos / jnp.sum(lanczos)
    kernel = jnp.zeros((TAPS,), jnp.float32)
    for position in range(9):
        tap_start = position - 2 - TAPS_HALF + HALF
        kernel = kernel + lanczos[position] * jnp.pad(
            tap_vals, (tap_start, TAPS - tap_start - tap_vals.shape[0])
        )
    return kernel


def fill_band(taps_ref, band_ref, absolute):
    lag = lax.broadcasted_iota(jnp.int32, (128, 128), 0) - lax.broadcasted_iota(
        jnp.int32, (128, 128), 1
    )
    zero = jnp.zeros((128, 128), jnp.bfloat16)
    tiles = []
    for k in (-1, 0, 1):
        tile = jnp.zeros((128, 128), jnp.float32)
        for d in range(-HALF, HALF + 1):
            want = d - 128 * k
            if -128 < want < 128:
                value = taps_ref[d + HALF]
                value = jnp.abs(value) if absolute else value
                tile = jnp.where(lag == want, value, tile)
        tiles.append(tile.astype(jnp.bfloat16))
    for i in range(WINDOW // 128):
        for o in range(BLOCK // 128):
            k = i - o - 1
            band_ref[128 * i : 128 * (i + 1), 128 * o : 128 * (o + 1)] = (
                tiles[k + 1] if -1 <= k <= 1 else zero
            )


def good_columns(bad_ref):
    columns = lax.broadcasted_iota(jnp.int32, (1, ROW_PIX), 1)
    hit = bad_ref[...] == columns
    return 1.0 - jnp.max(hit.astype(jnp.float32), axis=0, keepdims=True)


def fill_padded(padded_ref, rows, values):
    padded_ref[rows, 0:PAD] = jnp.zeros((values.shape[0], PAD), jnp.bfloat16)
    padded_ref[rows, PAD : PAD + ROW_PIX] = values
    padded_ref[rows, PAD + ROW_PIX :] = jnp.zeros((values.shape[0], PAD), jnp.bfloat16)


def convolve_span(padded_ref, band_ref, span):
    start = pl.multiple_of(span * SPAN, 128)
    parts = [
        jnp.dot(
            padded_ref[:, pl.ds(pl.multiple_of(start + BLOCK * n, 128), WINDOW)],
            band_ref[...],
            preferred_element_type=jnp.float32,
        )
        for n in range(SPAN // BLOCK)
    ]
    return jnp.concatenate(parts, axis=1)


def send_pieces(patch_ref, out_ref, values):
    out_ref[...] = jnp.zeros(out_ref.shape, out_ref.dtype)
    patches = [patch_ref[j] for j in range(PIECES)]
    for j in range(PIECES):
        rank = jnp.int32(0)
        for k in range(j):
            rank = rank + (patches[k] == patches[j]).astype(jnp.int32)
        slot = patches[j] * MOST + jnp.minimum(rank, MOST - 1)
        out_ref[0, slot] = values[PIECE_ROWS * j : PIECE_ROWS * (j + 1)]


def weight_body(taps_ref, patch_ref, ivar_ref, bad_ref, send_ref, weight_ref, padded_ref, band_ref):
    span = pl.program_id(0)

    @pl.when(span == 0)
    def _():
        good = good_columns(bad_ref).astype(jnp.bfloat16)
        fill_padded(padded_ref, slice(0, CCD_ROWS), ivar_ref[...] * good)
        fill_band(taps_ref, band_ref, True)

    weight = convolve_span(padded_ref, band_ref, span).astype(jnp.bfloat16)
    weight_ref[...] = weight
    send_pieces(patch_ref, send_ref, weight)


def flux_body(
    taps_ref, patch_ref, mix_ref, image_ref, bad_ref, grids_ref, weight_ref, send_ref, padded_ref, band_ref
):
    span = pl.program_id(0)

    @pl.when(span == 0)
    def _():
        good = good_columns(bad_ref)
        fill_padded(padded_ref, slice(0, CCD_ROWS), image_ref[...] * good.astype(jnp.bfloat16))
        model = mix_ref[0] * grids_ref[0]
        for k in range(1, PIECES):
            model = model + mix_ref[k] * grids_ref[k]
        upper = model.astype(jnp.bfloat16)
        lower = (model - upper.astype(jnp.float32)).astype(jnp.bfloat16)
        both = jnp.concatenate([upper, lower], axis=0)
        spread = (
            lax.broadcasted_iota(jnp.int32, (BINS, ROW_PIX), 1) // BIN_PIX
            == lax.broadcasted_iota(jnp.int32, (BINS, ROW_PIX), 0)
        ).astype(jnp.bfloat16)
        expanded = jnp.dot(both, spread, preferred_element_type=jnp.float32) * good
        fill_padded(
            padded_ref, slice(CCD_ROWS, CCD_ROWS + 2 * PIECES), expanded.astype(jnp.bfloat16)
        )
        fill_band(taps_ref, band_ref, False)

    warped = convolve_span(padded_ref, band_ref, span)
    backdrop = (
        warped[CCD_ROWS : CCD_ROWS + PIECES] + warped[CCD_ROWS + PIECES : CCD_ROWS + 2 * PIECES]
    )
    backdrop = jnp.broadcast_to(backdrop[:, None, :], (PIECES, PIECE_ROWS, SPAN)).reshape(
        CCD_ROWS, SPAN
    )
    flux = warped[:CCD_ROWS] - backdrop
    send_pieces(
        patch_ref, send_ref, (flux * weight_ref[...].astype(jnp.float32)).astype(jnp.bfloat16)
    )


def scatter_body(band_ref, rows_ref, received_ref, total_ref, low_ref, high_ref):
    visit = pl.program_id(0)

    @pl.when(visit == 0)
    def _():
        total_ref[...] = jnp.zeros(total_ref.shape, total_ref.dtype)

    slots = rows_ref.shape[-1]
    place = lax.broadcasted_iota(jnp.int32, (FRAME, slots), 0) == rows_ref[0]
    frames = jnp.dot(
        place.astype(jnp.bfloat16), received_ref[0], preferred_element_type=jnp.float32
    )
    band = band_ref[visit]
    total_ref[band] = total_ref[band] + frames

    @pl.when(visit == pl.num_programs(0) - 1)
    def _():
        low_ref[...] = total_ref[:, :EDGE].astype(jnp.bfloat16)
        high_ref[...] = total_ref[:, FRAME - EDGE :].astype(jnp.bfloat16)


def merge_body(total_ref, before_ref, after_ref, out_ref):
    total = total_ref[0]
    out_ref[0, :EDGE] = total[:EDGE] + before_ref[0].astype(jnp.float32)
    out_ref[0, EDGE : FRAME - EDGE] = total[EDGE : FRAME - EDGE]
    out_ref[0, FRAME - EDGE :] = total[FRAME - EDGE :] + after_ref[0].astype(jnp.float32)


SMEM = pl.BlockSpec(memory_space=pltpu.SMEM)


def whole(shape):
    zeros = (0,) * len(shape)
    return pl.BlockSpec(shape, lambda i: zeros)


PARAMS = pltpu.CompilerParams(
    dimension_semantics=("arbitrary",), vmem_limit_bytes=VMEM_LIMIT
)
SEND_SHAPE = (VISITS, PATCHES * MOST, PIECE_ROWS, SPAN)
SEND_BLOCK = pl.BlockSpec((1, PATCHES * MOST, PIECE_ROWS, SPAN), lambda i: (i, 0, 0, 0))
SPAN_BLOCK = pl.BlockSpec((CCD_ROWS, SPAN), lambda i: (0, i))


def send_weight(taps, patches, inv_var, bad):
    return pl.pallas_call(
        weight_body,
        grid=(VISITS,),
        in_specs=[SMEM, SMEM, whole(inv_var.shape), whole(bad.shape)],
        out_specs=[SEND_BLOCK, SPAN_BLOCK],
        out_shape=[
            jax.ShapeDtypeStruct(SEND_SHAPE, jnp.bfloat16),
            jax.ShapeDtypeStruct((CCD_ROWS, ROW_PIX), jnp.bfloat16),
        ],
        scratch_shapes=[
            pltpu.VMEM((CCD_ROWS, ROW_PIX + 2 * PAD), jnp.bfloat16),
            pltpu.VMEM((WINDOW, BLOCK), jnp.bfloat16),
        ],
        compiler_params=PARAMS,
        name="send_weight",
    )(taps, patches, inv_var, bad)


def send_flux(taps, patches, mix_row, image, bad, grids, weight):
    return pl.pallas_call(
        flux_body,
        grid=(VISITS,),
        in_specs=[
            SMEM,
            SMEM,
            SMEM,
            whole(image.shape),
            whole(bad.shape),
            whole(grids.shape),
            SPAN_BLOCK,
        ],
        out_specs=SEND_BLOCK,
        out_shape=jax.ShapeDtypeStruct(SEND_SHAPE, jnp.bfloat16),
        scratch_shapes=[
            pltpu.VMEM((CCD_ROWS + 2 * PIECES, ROW_PIX + 2 * PAD), jnp.bfloat16),
            pltpu.VMEM((WINDOW, BLOCK), jnp.bfloat16),
        ],
        compiler_params=PARAMS,
        name="send_flux",
    )(taps, patches, mix_row, image, bad, grids, weight)


def exchange(pieces):
    sent = pieces.reshape(VISITS * PATCHES, MOST, PIECE_ROWS, SPAN)
    return lax.all_to_all(sent, ("visit", "fp"), split_axis=0, concat_axis=0, tiled=True)


def scatter(band_of_visit, dest_rows, received):
    slots = PATCHES * MOST * PIECE_ROWS
    return pl.pallas_call(
        scatter_body,
        grid=(VISITS,),
        in_specs=[
            SMEM,
            pl.BlockSpec((1, 1, slots), lambda i: (i, 0, 0)),
            pl.BlockSpec((1, slots, SPAN), lambda i: (i, 0, 0)),
        ],
        out_specs=[
            whole((BANDS, FRAME, SPAN)),
            whole((BANDS, EDGE, SPAN)),
            whole((BANDS, EDGE, SPAN)),
        ],
        out_shape=[
            jax.ShapeDtypeStruct((BANDS, FRAME, SPAN), jnp.float32),
            jax.ShapeDtypeStruct((BANDS, EDGE, SPAN), jnp.bfloat16),
            jax.ShapeDtypeStruct((BANDS, EDGE, SPAN), jnp.bfloat16),
        ],
        compiler_params=PARAMS,
        name="scatter",
    )(band_of_visit, dest_rows, received.reshape(VISITS, slots, SPAN))


def merge(total, before, after):
    edge = pl.BlockSpec((1, EDGE, SPAN), lambda i: (i, 0, 0))
    frame = pl.BlockSpec((1, FRAME, SPAN), lambda i: (i, 0, 0))
    return pl.pallas_call(
        merge_body,
        grid=(BANDS,),
        in_specs=[frame, edge, edge],
        out_specs=frame,
        out_shape=jax.ShapeDtypeStruct((BANDS, FRAME, SPAN), jnp.float32),
        compiler_params=PARAMS,
        name="merge",
    )(total, before, after)


def borders(total, low, high):
    peers = lax.axis_size("fp")
    up = [(i, i + 1) for i in range(peers - 1)]
    down = [(j, i) for i, j in up]
    return merge(total, lax.ppermute(high, "fp", up), lax.ppermute(low, "fp", down))


def slot_rows(patches, starts):
    piece_ids = jnp.arange(PIECES, dtype=jnp.int32)
    earlier = piece_ids[:, None] > piece_ids[None, :]
    rank = jnp.sum((earlier & (patches[:, None] == patches[None, :])).astype(jnp.int32), axis=1)
    slot = patches * MOST + rank
    chosen = slot[None, :] == jnp.arange(PATCHES * MOST, dtype=jnp.int32)[:, None]
    start = jnp.sum(jnp.where(chosen, starts[None, :] - UNUSED, 0), axis=1) + UNUSED
    everywhere = jnp.broadcast_to(start.reshape(1, PATCHES, MOST), (VISITS, PATCHES, MOST))
    arrived = lax.all_to_all(
        everywhere.reshape(VISITS * PATCHES, MOST),
        ("visit", "fp"),
        split_axis=0,
        concat_axis=0,
        tiled=True,
    )
    rows = arrived[:, :, None] + jnp.arange(PIECE_ROWS, dtype=jnp.int32)
    return rows.reshape(VISITS, 1, PATCHES * MOST * PIECE_ROWS)


def shards(
    image,
    inv_var,
    bg_grid,
    bg_mix,
    psf_taps,
    warp_shift,
    bad_cols,
    piece_patch,
    piece_pos,
    band_of_visit,
):
    grids = lax.all_gather(bg_grid, "fp", axis=1, tiled=True)[0]
    mix_row = lax.dynamic_slice_in_dim(bg_mix, lax.axis_index("fp"), 1, 0)[0]
    patches = piece_patch[0, :, 0]
    dest_rows = slot_rows(patches, piece_pos[0])
    taps = make_kernel(psf_taps[0, 0], warp_shift[0, 0])
    bad = bad_cols.reshape(-1, 1)
    weight_pieces, weight = send_weight(taps, patches, inv_var[0], bad)
    weight_arrived = exchange(weight_pieces)
    flux_pieces = send_flux(taps, patches, mix_row, image[0], bad, grids, weight)
    flux_arrived = exchange(flux_pieces)
    weight_out = borders(*scatter(band_of_visit, dest_rows, weight_arrived))
    flux_out = borders(*scatter(band_of_visit, dest_rows, flux_arrived))
    return (flux_out[:, None], weight_out[:, None])


def solution(mesh):
    placed = (
        P("visit", "fp", None),
        P("visit", "fp", None),
        P("visit", "fp", None, None),
        P(),
        P("visit", "fp", None),
        P("visit", "fp"),
        P("fp", None),
        P("visit", "fp", None),
        P("visit", "fp"),
        P(),
    )
    return jax.shard_map(
        shards,
        mesh=mesh,
        in_specs=placed,
        out_specs=(P(None, "fp", None, "visit"), P(None, "fp", None, "visit")),
        check_vma=False,
    )
```

time: 825 us -> 217 us (0.26)
  the two profiles are of different devices: /device:TPU:104 before, /device:TPU:0 now
where the time goes in v1:
time: 217 us; the launch traced here: 213 us
  blocking collectives  63.3 us (29%)
  waiting for transfers between devices  55.3 us (25%)
  starting transfers between devices  40 us (18%)
  Pallas kernels  31.7 us (15%)
  other arithmetic  12 us (6%)
  local copies, waits for them, and re-layouts  9.39 us (4%)
    all_gather x1, blocking collectives, shards(): grids = lax.all_gather(bg_grid, 'fp', axis=1, tiled=True)[0]  63.3 us
    all_to_all x2, waiting for transfers between devices, exchange(): lax.all_to_all(sent, ('visit', 'fp'), split_axis=0, concat_axis=0, tiled=...  38.7 us
    all_to_all x2, starting transfers between devices, exchange(): lax.all_to_all(sent, ('visit', 'fp'), split_axis=0, concat_axis=0, tiled=...  20.9 us
    pallas_call x2, Pallas kernels, scatter(): pl.pallas_call(scatter_body, grid=(VISITS,), in_specs=[SMEM, pl.BlockSpec...  13.9 us
    ppermute x2, waiting for transfers between devices, borders(): lax.ppermute(high, 'fp', up)  13.3 us
    all_to_all x1, starting transfers between devices, slot_rows(): lax.all_to_all(everywhere.reshape(VISITS * PATCHES, MOST), ('visit', 'fp'...  11.1 us
    pallas_call x1, Pallas kernels, send_flux(): pl.pallas_call(flux_body, grid=(VISITS,), in_specs=[SMEM, SMEM, SMEM, who...  7.06 us
    unnamed x22, local copies, waits for them, and re-layouts  7.03 us
  transfers between devices with their start and end apart: 7, of which 4 were waited for; matrix products, arithmetic and copies ran while one was open for 5% of the time, Pallas kernels for 14%

profile of v1, /device:TPU:0, one launch (start us, length us, event | category | flops | bytes accessed | tf_op | source)
XLA Modules:
  0.0 213.1 jit_solution(1248721987179765297)
XLA Ops:
  3.7 11.1 %all-to-all-start = ((s32[128,1,2]{2,1,0:T(1,128)}), s32[128,1,2]{2,1,0:T(1,128)S(1)}, u32[]{:S(2)}, u32[]{:S(2)}) async-start(s32[128,1,2]{2,1,0:T(1,128)} %bitcast.2), calls=%async_computation | async-start | bytes 131072 | tf_op jit(solution)/shard_map/all_to_all | solution.py:307
  16.7 1.3 reduce_sum.39
  18.0 1.3 divide_bitcast_fusion
  20.0 5.6 %multiply_add_fusion.2.taps_ref = f32[33]{0:T(128)S(1)} fusion(f32[21]{0:T(128)S(1)} %divide_bitcast_fusion, f32[]{:T(128)} %bitcast.14, f32[]{:T(128)} %bitcast.13, f32[]{:T(128)} %bitcast.12, f32[]{:T(128)} %bitcast.11, f32[]{:T(128)} %bitcast.10, f32[]{:T(128)} %bitcast.9, f32[]{:T(128)} %bitcast.8, f32[]{:T(128)} %bitcast.7, f32[]{:T(128)} %bitcast.5), kind=kLoop, calls=%fused_computation.35 | loop fusion | flops 561 | bytes 252 | tf_op jit(solution)/shard_map/add | solution.py:44
  26.4 1.6 copy-done.6
  28.6 6.0 %send_weight.1 = (bf16[8,32,16,512]{3,2,1,0:T(8,128)(2,1)}, bf16[256,4096]{1,0:T(8,128)(2,1)S(1)}) custom-call(f32[33]{0:T(128)S(1)} %multiply_add_fusion.2.taps_ref, s32[16]{0:T(128)S(1)} %bitcast.39, bf16[256,4096]{1,0:T(8,128)(2,1)S(1)} %bitcast.36, s32[32,1]{1,0:T(8,128)S(1)} %copy.31.bad_ref), custom_call_target="tpu_custom_call" | custom-call | tf_op jit(solution)/shard_map/send_weight/pallas_call | solution.py:206
  34.6 1.3 copy-done.4
  36.0 10.3 %all-to-all-start.2 = ((bf16[128,2,16,512]{3,2,1,0:T(8,128)(2,1)}), bf16[128,2,16,512]{3,2,1,0:T(8,128)(2,1)}, u32[]{:S(2)}, u32[]{:S(2)}) async-start(bf16[128,2,16,512]{3,2,1,0:T(8,128)(2,1)} %bitcast.42), calls=%async_computation.2 | async-start | bytes 8388608 | tf_op jit(solution)/shard_map/all_to_all | solution.py:250
  46.3 63.3 %all_gather.3 = f32[1,16,16,128]{3,2,0,1:T(8,128)S(1)} all-gather(f32[1,1,16,128]{3,2,0,1:T(8,128)S(1)} %bitcast.46), channel_id=1, replica_groups=mesh['visit'=8,'fp'=16] {'fp'}, dimensions={1}, use_global_device_ids=true | all-gather | bytes 139264 | tf_op jit(solution)/shard_map/all_gather | solution.py:330
  109.7 1.6 copy-done.5
  111.3 7.1 %send_flux.1 = bf16[8,32,16,512]{3,2,1,0:T(8,128)(2,1)} custom-call(f32[33]{0:T(128)S(1)} %multiply_add_fusion.2.taps_ref, s32[16]{0:T(128)S(1)} %bitcast.40, f32[16]{0:T(128)S(1)} %dynamic-slice_bitcast_fusion.mix_ref, bf16[256,4096]{1,0:T(8,128)(2,1)S(1)} %bitcast.35, s32[32,1]{1,0:T(8,128)S(1)} %copy.31.bad_ref, f32[16,16,128]{2,1,0:T(8,128)S(1)} %bitcast.37, ...), custom_call_target="tpu_custom_call" | custom-call | tf_op jit(solution)/shard_map/send_flux/pallas_call | solution.py:225
  118.3 10.6 %all-to-all-start.1 = ((bf16[128,2,16,512]{3,2,1,0:T(8,128)(2,1)}), bf16[128,2,16,512]{3,2,1,0:T(8,128)(2,1)}, u32[]{:S(2)}, u32[]{:S(2)}) async-start(bf16[128,2,16,512]{3,2,1,0:T(8,128)(2,1)} %bitcast.41), calls=%async_computation.1 | async-start | bytes 8388608 | tf_op jit(solution)/shard_map/all_to_all | solution.py:250
  129.3 6.9 %scatter.3 = (f32[4,456,512]{2,1,0:T(8,128)S(1)}, bf16[4,200,512]{2,1,0:T(8,128)(2,1)S(1)}, bf16[4,200,512]{2,1,0:T(8,128)(2,1)S(1)}) custom-call(s32[8]{0:T(128)S(1)} %copy-done.7, s32[8,1,512]{2,1,0:T(1,128)S(1)} %add.155.rows_ref, bf16[8,512,512]{2,1,0:T(8,128)(2,1)} %bitcast.26.received_ref), custom_call_target="tpu_custom_call" | custom-call | tf_op jit(solution)/shard_map/scatter/pallas_call | solution.py:255
  136.2 1.8 copy-done.1
  138.1 2.9 %collective-permute-start.2 = (bf16[4,200,512]{2,1,0:T(8,128)(2,1)S(1)}, bf16[4,200,512]{2,1,0:T(8,128)(2,1)S(1)}, u32[]{:S(2)}, u32[]{:S(2)}) collective-permute-start(bf16[4,200,512]{2,1,0:T(8,128)(2,1)S(1)} %get-tuple-element.17), channel_id=1, source_target_pairs={{0,1},{1,2},{2,3},{3,4},{4,5},{5,6},{6,7},{7,8},{8,9},{9,10},{10,1... | collective-permute-start | bytes 2457608 | tf_op jit(solution)/shard_map/ppermute | solution.py:296
  141.0 1.3 collective-permute-start.3
  142.3 38.7 %all-to-all-done.1 = bf16[128,2,16,512]{3,2,1,0:T(8,128)(2,1)} async-done(((bf16[128,2,16,512]{3,2,1,0:T(8,128)(2,1)}), bf16[128,2,16,512]{3,2,1,0:T(8,128)(2,1)}, u32[]{:S(2)}, u32[]{:S(2)}) %all-to-all-start.1) | async-done | bytes 4194336 | tf_op jit(solution)/shard_map/all_to_all | solution.py:250
  181.1 7.0 %scatter.2 = (f32[4,456,512]{2,1,0:T(8,128)S(1)}, bf16[4,200,512]{2,1,0:T(8,128)(2,1)S(1)}, bf16[4,200,512]{2,1,0:T(8,128)(2,1)S(1)}) custom-call(s32[8]{0:T(128)S(1)} %copy-done.7, s32[8,1,512]{2,1,0:T(1,128)S(1)} %add.155.rows_ref, bf16[8,512,512]{2,1,0:T(8,128)(2,1)} %bitcast.22.received_ref), custom_call_target="tpu_custom_call" | custom-call | tf_op jit(solution)/shard_map/scatter/pallas_call | solution.py:255
  188.1 2.4 %collective-permute-start = (bf16[4,200,512]{2,1,0:T(8,128)(2,1)S(1)}, bf16[4,200,512]{2,1,0:T(8,128)(2,1)S(1)}, u32[]{:S(2)}, u32[]{:S(2)}) collective-permute-start(bf16[4,200,512]{2,1,0:T(8,128)(2,1)S(1)} %get-tuple-element.13), channel_id=1, source_target_pairs={{0,1},{1,2},{2,3},{3,4},{4,5},{5,6},{6,7},{7,8},{8,9},{9,10},{10,1... | collective-permute-start | bytes 2457608 | tf_op jit(solution)/shard_map/ppermute | solution.py:296
  190.5 1.3 collective-permute-start.1
  192.8 2.4 %merge.3 = f32[4,456,512]{2,1,0:T(8,128)} custom-call(f32[4,456,512]{2,1,0:T(8,128)S(1)} %copy-done.2, bf16[4,200,512]{2,1,0:T(8,128)(2,1)S(1)} %collective-permute-done.2.before_ref, bf16[4,200,512]{2,1,0:T(8,128)(2,1)S(1)} %collective-permute-done.3.after_ref), custom_call_target="tpu_custom_call" | custom-call | tf_op jit(solution)/shard_map/merge/pallas_call | solution.py:281
  195.1 13.3 %collective-permute-done.before_ref = bf16[4,200,512]{2,1,0:T(8,128)(2,1)S(1)} collective-permute-done((bf16[4,200,512]{2,1,0:T(8,128)(2,1)S(1)}, bf16[4,200,512]{2,1,0:T(8,128)(2,1)S(1)}, u32[]{:S(2)}, u32[]{:S(2)}) %collective-permute-start) | collective-permute-done | bytes 819232 | tf_op jit(solution)/shard_map/ppermute | solution.py:296
  208.4 2.4 %collective-permute-done.1.after_ref = bf16[4,200,512]{2,1,0:T(8,128)(2,1)S(1)} collective-permute-done((bf16[4,200,512]{2,1,0:T(8,128)(2,1)S(1)}, bf16[4,200,512]{2,1,0:T(8,128)(2,1)S(1)}, u32[]{:S(2)}, u32[]{:S(2)}) %collective-permute-start.1) | collective-permute-done | bytes 819232 | tf_op jit(solution)/shard_map/ppermute | solution.py:296
  210.8 2.3 %merge.2 = f32[4,456,512]{2,1,0:T(8,128)} custom-call(f32[4,456,512]{2,1,0:T(8,128)S(1)} %get-tuple-element.12.total_ref, bf16[4,200,512]{2,1,0:T(8,128)(2,1)S(1)} %collective-permute-done.before_ref, bf16[4,200,512]{2,1,0:T(8,128)(2,1)S(1)} %collective-permute-done.1.after_ref), custom_call_target="tpu_custom_call" | custom-call | tf_op jit(solution)/shard_map/merge/pallas_call | solution.py:281
  (36 shorter events, 7.7 us)
Async XLA Ops:
  0.6 109.0 %copy-start = (f32[16,16]{1,0:T(8,128)S(1)}, f32[16,16]{1,0:T(8,128)}, u32[]{:S(2)}) copy-start(f32[16,16]{1,0:T(8,128)} %param.14) | copy-start | bytes 3076
  3.7 32.2 %all-to-all-start = ((s32[128,1,2]{2,1,0:T(1,128)}), s32[128,1,2]{2,1,0:T(1,128)S(1)}, u32[]{:S(2)}, u32[]{:S(2)}) async-start(s32[128,1,2]{2,1,0:T(1,128)} %bitcast.2), calls=%async_computation | async-start | bytes 131072 | tf_op jit(solution)/shard_map/all_to_all | solution.py:307
  26.4 1.6 copy-start.6
  28.0 0.7 copy-start.8
  34.6 1.3 copy-start.4
  36.0 10.3 %copy-start.10 = (f32[1,1,16,128]{3,2,1,0:T(8,128)S(1)}, f32[1,1,16,128]{3,2,1,0:T(8,128)}, u32[]{:S(2)}) copy-start(f32[1,1,16,128]{3,2,1,0:T(8,128)} %param.13) | copy-start | bytes 24580
  36.0 73.7 %copy-start.3 = (bf16[1,256,4096]{2,1,0:T(8,128)(2,1)S(1)}, bf16[1,256,4096]{2,1,0:T(8,128)(2,1)}, u32[]{:S(2)}) copy-start(bf16[1,256,4096]{2,1,0:T(8,128)(2,1)} %param.11) | copy-start | bytes 6291460
  36.0 73.7 %copy-start.9 = (s32[1,16,1]{1,2,0:T(1,128)S(1)}, s32[1,16,1]{1,2,0:T(1,128)}, u32[]{:S(2)}) copy-start(s32[1,16,1]{1,2,0:T(1,128)} %param.18) | copy-start | bytes 196
  36.0 82.4 %all-to-all-start.2 = ((bf16[128,2,16,512]{3,2,1,0:T(8,128)(2,1)}), bf16[128,2,16,512]{3,2,1,0:T(8,128)(2,1)}, u32[]{:S(2)}, u32[]{:S(2)}) async-start(bf16[128,2,16,512]{3,2,1,0:T(8,128)(2,1)} %bitcast.42), calls=%async_computation.2 | async-start | bytes 8388608 | tf_op jit(solution)/shard_map/all_to_all | solution.py:250
  109.7 1.6 copy-start.5
  118.3 11.0 %copy-start.7 = (s32[8]{0:T(128)S(1)}, s32[8]{0:T(128)}, u32[]{:S(2)}) copy-start(s32[8]{0:T(128)} %band_ref.3) | copy-start | bytes 100
  118.3 62.7 %all-to-all-start.1 = ((bf16[128,2,16,512]{3,2,1,0:T(8,128)(2,1)}), bf16[128,2,16,512]{3,2,1,0:T(8,128)(2,1)}, u32[]{:S(2)}, u32[]{:S(2)}) async-start(bf16[128,2,16,512]{3,2,1,0:T(8,128)(2,1)} %bitcast.41), calls=%async_computation.1 | async-start | bytes 8388608 | tf_op jit(solution)/shard_map/all_to_all | solution.py:250
  136.2 1.9 copy-start.1
  138.1 53.7 %collective-permute-start.2 = (bf16[4,200,512]{2,1,0:T(8,128)(2,1)S(1)}, bf16[4,200,512]{2,1,0:T(8,128)(2,1)S(1)}, u32[]{:S(2)}, u32[]{:S(2)}) collective-permute-start(bf16[4,200,512]{2,1,0:T(8,128)(2,1)S(1)} %get-tuple-element.17), channel_id=1, source_target_pairs={{0,1},{1,2},{2,3},{3,4},{4,5},{5,6},{6,7},{7,8},{8,9},{9,10},{10,1... | collective-permute-start | bytes 2457608 | tf_op jit(solution)/shard_map/ppermute | solution.py:296
  141.0 51.7 %collective-permute-start.3 = (bf16[4,200,512]{2,1,0:T(8,128)(2,1)S(1)}, bf16[4,200,512]{2,1,0:T(8,128)(2,1)S(1)}, u32[]{:S(2)}, u32[]{:S(2)}) collective-permute-start(bf16[4,200,512]{2,1,0:T(8,128)(2,1)S(1)} %get-tuple-element.18), channel_id=1, source_target_pairs={{1,0},{2,1},{3,2},{4,3},{5,4},{6,5},{7,6},{8,7},{9,8},{10,9},{11,1... | collective-permute-start | bytes 2457608 | tf_op jit(solution)/shard_map/ppermute | solution.py:296
  181.1 11.7 %copy-start.2 = (f32[4,456,512]{2,1,0:T(8,128)S(1)}, f32[4,456,512]{2,1,0:T(8,128)}, u32[]{:S(2)}) copy-start(f32[4,456,512]{2,1,0:T(8,128)} %copy-done.1) | copy-start | bytes 11206660
  188.1 20.3 %collective-permute-start = (bf16[4,200,512]{2,1,0:T(8,128)(2,1)S(1)}, bf16[4,200,512]{2,1,0:T(8,128)(2,1)S(1)}, u32[]{:S(2)}, u32[]{:S(2)}) collective-permute-start(bf16[4,200,512]{2,1,0:T(8,128)(2,1)S(1)} %get-tuple-element.13), channel_id=1, source_target_pairs={{0,1},{1,2},{2,3},{3,4},{4,5},{5,6},{6,7},{7,8},{8,9},{9,10},{10,1... | collective-permute-start | bytes 2457608 | tf_op jit(solution)/shard_map/ppermute | solution.py:296
  190.5 20.3 %collective-permute-start.1 = (bf16[4,200,512]{2,1,0:T(8,128)(2,1)S(1)}, bf16[4,200,512]{2,1,0:T(8,128)(2,1)S(1)}, u32[]{:S(2)}, u32[]{:S(2)}) collective-permute-start(bf16[4,200,512]{2,1,0:T(8,128)(2,1)S(1)} %get-tuple-element.14), channel_id=1, source_target_pairs={{1,0},{2,1},{3,2},{4,3},{5,4},{6,5},{7,6},{8,7},{9,8},{10,9},{11,1... | collective-permute-start | bytes 2457608 | tf_op jit(solution)/shard_map/ppermute | solution.py:296

commit v2 on v1

v2 whole, which is shorter than its diff:
```python
import functools

import jax
import jax.numpy as jnp
from jax import lax
from jax.experimental import pallas as pl
from jax.experimental.pallas import tpu as pltpu
from jax.sharding import PartitionSpec as P

ROW_PIX = 4096
BANDS = 4
CCD_ROWS = 256
MOST = 2
BORDER = 100
EDGE = 2 * BORDER
TAPS_HALF = 10
FRAME = 456
HALF = 16
TAPS = 2 * HALF + 1
PIECES = 16
PIECE_ROWS = 16
BINS = 128
BIN_PIX = ROW_PIX // BINS
PATCHES = 16
VISITS = 8
GROUPS = 16
GRID_ROWS = 16
PACKED = GRID_ROWS + 8
SPAN = ROW_PIX // VISITS
CHUNKS = 1
BLOCK = 256
PAD = 128
WINDOW = BLOCK + 2 * PAD
UNUSED = 1 << 20
WIDTH = SPAN // CHUNKS


def fill_band(psf_ref, shift_ref, band_ref, absolute):
    shape = (16, WINDOW)
    step = lax.broadcasted_iota(jnp.int32, shape, 0) - 2
    lag = 3 * PAD - lax.broadcasted_iota(jnp.int32, shape, 1) - step
    offset = (shift_ref[0, 0] - 16 * step).astype(jnp.float32) / 16.0
    angle = offset * jnp.float32(jnp.pi)
    safe = jnp.where(offset == 0.0, 1.0, angle)
    lanczos = jnp.where(
        offset == 0.0, 1.0, 3.0 * jnp.sin(safe) * jnp.sin(safe / 3.0) / (safe * safe)
    )
    lanczos = jnp.where((jnp.abs(offset) < 3.0) & (step < 7), lanczos, 0.0)
    lanczos = lanczos / jnp.sum(lanczos, axis=0, keepdims=True)
    taps = jnp.zeros(shape, jnp.float32)
    total = psf_ref[0, 0, 0]
    for e in range(2 * TAPS_HALF + 1):
        value = psf_ref[0, 0, e]
        taps = jnp.where(lag == e - TAPS_HALF, value, taps)
        total = total + value if e else total
    combined = jnp.sum(lanczos * (taps / total), axis=0, keepdims=True)
    combined = jnp.abs(combined) if absolute else combined
    rolled = pltpu.roll(
        jnp.broadcast_to(combined, (128, WINDOW)), 0, axis=1, stride=1, stride_axis=0
    ).astype(jnp.bfloat16)
    for i in range(WINDOW // 128):
        for o in range(BLOCK // 128):
            tile = (o - i) % (WINDOW // 128)
            band_ref[128 * i : 128 * (i + 1), 128 * o : 128 * (o + 1)] = rolled[
                :, 128 * tile : 128 * (tile + 1)
            ]


def fill_good(bad_ref, good_ref):
    columns = lax.broadcasted_iota(jnp.int32, good_ref.shape, 1) - PAD
    good = (columns >= 0) & (columns < ROW_PIX)
    for k in range(bad_ref.shape[-1]):
        good = good & (columns != bad_ref[0, k])
    good_ref[...] = good.astype(jnp.float32)


def convolve(window, band_ref, width):
    parts = [
        jnp.dot(
            window[:, BLOCK * n : BLOCK * n + WINDOW],
            band_ref[...],
            preferred_element_type=jnp.float32,
        )
        for n in range(width // BLOCK)
    ]
    return parts[0] if len(parts) == 1 else jnp.concatenate(parts, axis=1)


def send_pieces(patch_ref, out_ref, values):
    out_ref[...] = jnp.zeros(out_ref.shape, out_ref.dtype)
    patches = [patch_ref[j] for j in range(PIECES)]
    for j in range(PIECES):
        rank = jnp.int32(0)
        for k in range(j):
            rank = rank + (patches[k] == patches[j]).astype(jnp.int32)
        slot = patches[j] * MOST + jnp.minimum(rank, MOST - 1)
        out_ref[0, slot] = values[PIECE_ROWS * j : PIECE_ROWS * (j + 1)]


def pack_body(where_ref, mix_ref, patch_ref, pos_ref, grid_ref, out_ref):
    group = where_ref[1]
    shape = (PATCHES, BINS)
    patch = lax.broadcasted_iota(jnp.int32, shape, 0)
    slot = lax.broadcasted_iota(jnp.int32, shape, 1)
    first = jnp.full(shape, UNUSED, jnp.int32)
    patches = [patch_ref[j] for j in range(PIECES)]
    for j in range(PIECES):
        rank = jnp.int32(0)
        for k in range(j):
            rank = rank + (patches[k] == patches[j]).astype(jnp.int32)
        first = jnp.where((patch == patches[j]) & (slot == rank), pos_ref[0, j], first)
    first = first.astype(jnp.float32)
    for q in range(PATCHES):
        out_ref[q, :GRID_ROWS] = grid_ref[0, 0] * mix_ref[q, group]
        out_ref[q, GRID_ROWS:] = jnp.broadcast_to(first[q : q + 1], (PACKED - GRID_ROWS, BINS))


def masked_window(chunk, good_ref, left_ref, mid_ref, right_ref):
    width = mid_ref.shape[-1]
    start = pl.multiple_of(pl.program_id(0) * SPAN + chunk * width, 128)
    good = good_ref[:, pl.ds(start, width + 2 * PAD)]
    window = jnp.concatenate([left_ref[0], mid_ref[0], right_ref[0]], axis=1)
    return start, good, window * good.astype(jnp.bfloat16)


def weight_body(
    chunk,
    psf_ref,
    shift_ref,
    patch_ref,
    bad_ref,
    left_ref,
    mid_ref,
    right_ref,
    send_ref,
    weight_ref,
    good_ref,
    band_ref,
):
    @pl.when(pl.program_id(0) == 0)
    def _():
        fill_good(bad_ref, good_ref)
        fill_band(psf_ref, shift_ref, band_ref, True)

    _, _, window = masked_window(chunk, good_ref, left_ref, mid_ref, right_ref)
    weight = convolve(window, band_ref, mid_ref.shape[-1]).astype(jnp.bfloat16)
    weight_ref[0] = weight
    send_pieces(patch_ref, send_ref, weight)


def flux_body(
    chunk,
    psf_ref,
    shift_ref,
    patch_ref,
    bad_ref,
    left_ref,
    mid_ref,
    right_ref,
    packed_ref,
    weight_ref,
    send_ref,
    good_ref,
    band_ref,
    model_ref,
):
    @pl.when(pl.program_id(0) == 0)
    def _():
        fill_good(bad_ref, good_ref)
        fill_band(psf_ref, shift_ref, band_ref, False)
        model = packed_ref[0, :GRID_ROWS]
        for k in range(1, GROUPS):
            model = model + packed_ref[k, :GRID_ROWS]
        upper = model.astype(jnp.bfloat16)
        model_ref[:GRID_ROWS] = upper
        model_ref[GRID_ROWS:] = (model - upper.astype(jnp.float32)).astype(jnp.bfloat16)

    width = mid_ref.shape[-1]
    start, good, window = masked_window(chunk, good_ref, left_ref, mid_ref, right_ref)
    shape = (BINS, width + 2 * PAD)
    first = lax.broadcasted_iota(jnp.int32, shape, 0) * BIN_PIX
    column = lax.broadcasted_iota(jnp.int32, shape, 1) + (start - PAD)
    spread = ((column >= first) & (column < first + BIN_PIX)).astype(jnp.bfloat16)
    expanded = jnp.dot(model_ref[...], spread, preferred_element_type=jnp.float32) * good
    warped = convolve(
        jnp.concatenate([window, expanded.astype(jnp.bfloat16)], axis=0), band_ref, width
    )
    backdrop = warped[CCD_ROWS : CCD_ROWS + GRID_ROWS] + warped[CCD_ROWS + GRID_ROWS :]
    backdrop = jnp.broadcast_to(
        backdrop[:, None, :], (GRID_ROWS, CCD_ROWS // GRID_ROWS, width)
    ).reshape(CCD_ROWS, width)
    flux = warped[:CCD_ROWS] - backdrop
    send_pieces(
        patch_ref, send_ref, (flux * weight_ref[0].astype(jnp.float32)).astype(jnp.bfloat16)
    )


def scatter_body(where_ref, band_ref, rows_ref, received_ref, total_ref, low_ref, high_ref):
    visit = pl.program_id(0)

    @pl.when(visit == 0)
    def _():
        total_ref[...] = jnp.zeros(total_ref.shape, total_ref.dtype)

    slots = rows_ref.shape[-1]
    place = lax.broadcasted_iota(jnp.int32, (FRAME, slots), 0) == rows_ref[0]
    frames = jnp.dot(
        place.astype(jnp.bfloat16), received_ref[0], preferred_element_type=jnp.float32
    )
    band = band_ref[visit]
    total_ref[band] = total_ref[band] + frames

    @pl.when(visit == pl.num_programs(0) - 1)
    def _():
        low_ref[...] = total_ref[:, :EDGE].astype(jnp.bfloat16)
        high_ref[...] = total_ref[:, FRAME - EDGE :].astype(jnp.bfloat16)


def merge_body(total_ref, before_ref, after_ref, *refs):
    out_ref = refs[-1]
    total = total_ref[0]
    out_ref[0, :EDGE] = total[:EDGE] + before_ref[0].astype(jnp.float32)
    out_ref[0, EDGE : FRAME - EDGE] = total[EDGE : FRAME - EDGE]
    out_ref[0, FRAME - EDGE :] = total[FRAME - EDGE :] + after_ref[0].astype(jnp.float32)


SMEM = pl.BlockSpec(memory_space=pltpu.SMEM)


def whole(shape):
    zeros = (0,) * len(shape)
    return pl.BlockSpec(shape, lambda i, *_: zeros)


def params(mebibytes):
    return pltpu.CompilerParams(
        dimension_semantics=("arbitrary",), vmem_limit_bytes=mebibytes << 20
    )


def window_specs(chunk):
    per = SPAN // WIDTH
    tiles = WIDTH // 128
    last = ROW_PIX // 128 - 1
    left = pl.BlockSpec(
        (1, CCD_ROWS, 128),
        lambda i, *_: (0, 0, jnp.maximum((per * i + chunk) * tiles - 1, 0)),
    )
    mid = pl.BlockSpec((1, CCD_ROWS, WIDTH), lambda i, *_: (0, 0, per * i + chunk))
    right = pl.BlockSpec(
        (1, CCD_ROWS, 128),
        lambda i, *_: (0, 0, jnp.minimum((per * i + chunk + 1) * tiles, last)),
    )
    return [left, mid, right]


SEND_SHAPE = (VISITS, PATCHES * MOST, PIECE_ROWS, WIDTH)
SEND_BLOCK = pl.BlockSpec((1,) + SEND_SHAPE[1:], lambda i, *_: (i, 0, 0, 0))
WEIGHT_BLOCK = pl.BlockSpec((1, CCD_ROWS, WIDTH), lambda i, *_: (i, 0, 0))
GOOD_SCRATCH = pltpu.VMEM((1, ROW_PIX + 2 * PAD), jnp.float32)
BAND_SCRATCH = pltpu.VMEM((WINDOW, BLOCK), jnp.bfloat16)


def send_weight(chunk, psf, shift, patches, bad, inv_var):
    return pl.pallas_call(
        functools.partial(weight_body, chunk),
        grid=(VISITS,),
        in_specs=[SMEM] * 4 + window_specs(chunk),
        out_specs=[SEND_BLOCK, WEIGHT_BLOCK],
        out_shape=[
            jax.ShapeDtypeStruct(SEND_SHAPE, jnp.bfloat16),
            jax.ShapeDtypeStruct((VISITS, CCD_ROWS, WIDTH), jnp.bfloat16),
        ],
        scratch_shapes=[GOOD_SCRATCH, BAND_SCRATCH],
        compiler_params=params(48),
        name="send_weight",
    )(psf, shift, patches, bad, inv_var, inv_var, inv_var)


def pack(where, mix, patches, starts, grid):
    return pl.pallas_call(
        pack_body,
        in_specs=[SMEM] * 4 + [pl.BlockSpec(memory_space=pltpu.VMEM)],
        out_specs=pl.BlockSpec(memory_space=pltpu.VMEM),
        out_shape=jax.ShapeDtypeStruct((PATCHES, PACKED, BINS), jnp.float32),
        name="pack",
    )(where, mix, patches, starts, grid)


def send_flux(chunk, psf, shift, patches, bad, image, packed, weight):
    return pl.pallas_call(
        functools.partial(flux_body, chunk),
        grid=(VISITS,),
        in_specs=[SMEM] * 4 + window_specs(chunk) + [whole(packed.shape), WEIGHT_BLOCK],
        out_specs=SEND_BLOCK,
        out_shape=jax.ShapeDtypeStruct(SEND_SHAPE, jnp.bfloat16),
        scratch_shapes=[
            GOOD_SCRATCH,
            BAND_SCRATCH,
            pltpu.VMEM((2 * GRID_ROWS, BINS), jnp.bfloat16),
        ],
        compiler_params=params(48),
        name="send_flux",
    )(psf, shift, patches, bad, image, image, image, packed, weight)


def exchange(pieces):
    sent = pieces.reshape(VISITS * PATCHES, MOST, PIECE_ROWS, WIDTH)
    return lax.all_to_all(sent, ("visit", "fp"), split_axis=0, concat_axis=0, tiled=True)


def scatter(where, band_of_visit, dest_rows, received):
    slots = PATCHES * MOST * PIECE_ROWS
    shapes = [
        jax.ShapeDtypeStruct((BANDS, FRAME, WIDTH), jnp.float32),
        jax.ShapeDtypeStruct((BANDS, EDGE, WIDTH), jnp.bfloat16),
        jax.ShapeDtypeStruct((BANDS, EDGE, WIDTH), jnp.bfloat16),
    ]
    return pl.pallas_call(
        scatter_body,
        grid_spec=pltpu.PrefetchScalarGridSpec(
            num_scalar_prefetch=1,
            grid=(VISITS,),
            in_specs=[
                SMEM,
                pl.BlockSpec((1, 1, slots), lambda i, at: ((at[0] - i) & (VISITS - 1), 0, 0)),
                pl.BlockSpec((1, slots, WIDTH), lambda i, at: (i, 0, 0)),
            ],
            out_specs=[whole(shape.shape) for shape in shapes],
        ),
        out_shape=shapes,
        compiler_params=params(20),
        name="scatter",
    )(where, band_of_visit, dest_rows, received.reshape(VISITS, slots, WIDTH))


def merge(chunk, total, before, after, earlier):
    edge = pl.BlockSpec((1, EDGE, WIDTH), lambda i: (i, 0, 0))
    frame = pl.BlockSpec((1, FRAME, WIDTH), lambda i: (i, 0, 0))
    return pl.pallas_call(
        merge_body,
        grid=(BANDS,),
        in_specs=[frame, edge, edge] + [pl.BlockSpec(memory_space=pl.ANY)] * len(earlier),
        out_specs=pl.BlockSpec((1, FRAME, WIDTH), lambda i: (i, 0, chunk)),
        out_shape=jax.ShapeDtypeStruct((BANDS, FRAME, SPAN), jnp.float32),
        input_output_aliases={3: 0} if earlier else {},
        compiler_params=params(16),
        name="merge",
    )(total, before, after, *earlier)


def swap_borders(low, high):
    peers = lax.axis_size("fp")
    up = [(i, i + 1) for i in range(peers - 1)]
    down = [(j, i) for i, j in up]
    return lax.ppermute(high, "fp", up), lax.ppermute(low, "fp", down)


def slot_rows(first):
    first = first.reshape(1, GROUPS * MOST)
    blocks = [first]
    for k in range(1, VISITS):
        blocks.append(lax.ppermute(first, "visit", [(i, (i + k) % VISITS) for i in range(VISITS)]))
    first = jnp.concatenate(blocks).astype(jnp.int32)
    rows = first[:, :, None] + jnp.arange(PIECE_ROWS, dtype=jnp.int32)
    return rows.reshape(VISITS, 1, GROUPS * MOST * PIECE_ROWS)


def shards(
    image,
    inv_var,
    bg_grid,
    bg_mix,
    psf_taps,
    warp_shift,
    bad_cols,
    piece_patch,
    piece_pos,
    band_of_visit,
):
    where = jnp.stack([lax.axis_index("visit"), lax.axis_index("fp")]).astype(jnp.int32)
    patches = piece_patch[0, :, 0]
    packed = pack(where, bg_mix, patches, piece_pos, bg_grid)
    packed = lax.all_to_all(packed, "fp", split_axis=0, concat_axis=0, tiled=True)
    common = (psf_taps, warp_shift, patches, bad_cols)
    chunks = range(SPAN // WIDTH)
    weights, arrived = [], []
    for chunk in chunks:
        pieces, weight = send_weight(chunk, *common, inv_var)
        weights.append(weight)
        arrived.append(exchange(pieces))
    for chunk in chunks:
        arrived.append(
            exchange(send_flux(chunk, *common, image, packed, weights[chunk]))
        )
    dest_rows = slot_rows(packed[:, GRID_ROWS, :MOST])
    outs = [[], []]
    for turn, received in enumerate(arrived):
        total, low, high = scatter(where, band_of_visit, dest_rows, received)
        kind, chunk = divmod(turn, len(chunks))
        outs[kind] = [merge(chunk, total, *swap_borders(low, high), outs[kind])]
    return (outs[1][0][:, None], outs[0][0][:, None])


def solution(mesh):
    placed = (
        P("visit", "fp", None),
        P("visit", "fp", None),
        P("visit", "fp", None, None),
        P(),
        P("visit", "fp", None),
        P("visit", "fp"),
        P("fp", None),
        P("visit", "fp", None),
        P("visit", "fp"),
        P(),
    )
    return jax.shard_map(
        shards,
        mesh=mesh,
        in_specs=placed,
        out_specs=(P(None, "fp", None, "visit"), P(None, "fp", None, "visit")),
        check_vma=False,
    )
```

time: 217 us -> 198 us (0.912); the launches traced: 213 us -> 197 us
  blocking collectives: 63.3 us -> 0 us
  waiting for transfers between devices: 55.3 us -> 105 us
  other arithmetic: 12 us -> 0.64 us
  starting transfers between devices: 40 us -> 45.3 us
  Pallas kernels: 31.7 us -> 35.7 us
    all_gather x1 -> x0, blocking collectives: 63.3 us -> none  [shards(): grids = lax.all_gather(bg_grid, 'fp', axis=1, tiled=True)[0]]
    ppermute x4 -> x11, waiting for transfers between devices: 16.6 us -> 62.5 us  [the longest x7 40.5 us: slot_rows(): lax.ppermute(first, 'visit', [(i, (i + k) % VISITS) for i in range(VISITS)])]
    ppermute x4 -> x11, starting transfers between devices: 7.97 us -> 20.5 us  [the longest x4 11.4 us: swap_borders(): return (lax.ppermute(high, 'fp', up), lax.ppermute(low, 'fp', down))]
    add x4 -> x1, other arithmetic: 6.51 us -> 0.01 us  [slot_rows(): rows = first[:, :, None] + jnp.arange(PIECE_ROWS, dtype=jnp.int32)]
    all_to_all x2, starting transfers between devices: 20.9 us -> 16.7 us  [exchange(): lax.all_to_all(sent, ('visit', 'fp'), split_axis=0, concat_axis=0, tiled=...]
    all_to_all x2, waiting for transfers between devices: 38.7 us -> 42.8 us  [exchange(): lax.all_to_all(sent, ('visit', 'fp'), split_axis=0, concat_axis=0, tiled=...]
    pallas_call x6 -> x7, Pallas kernels: 31.7 us -> 35.7 us  [the longest x2 15.1 us: scatter(): pl.pallas_call(scatter_body, grid_spec=pltpu.PrefetchScalarGridSpec(num_s...]
    all_to_all x1, starting transfers between devices: 11.1 us -> 8.13 us  [shards(): lax.all_to_all(packed, 'fp', split_axis=0, concat_axis=0, tiled=True)]
  transfers between devices with their start and end apart: 7 -> 14, of which waited for: 4 -> 10; matrix products, arithmetic and copies ran while one was open for 5% -> 0% of each run, Pallas kernels for 14% -> 16%
where the time goes in v2:
time: 198 us; the launch traced here: 197 us
  waiting for transfers between devices  105 us (53%)
  starting transfers between devices  45.3 us (23%)
  Pallas kernels  35.7 us (18%)
  local copies, waits for them, and re-layouts  8.76 us (4%)
    all_to_all x2, waiting for transfers between devices, exchange(): lax.all_to_all(sent, ('visit', 'fp'), split_axis=0, concat_axis=0, tiled=...  42.8 us
    ppermute x7, waiting for transfers between devices, slot_rows(): lax.ppermute(first, 'visit', [(i, (i + k) % VISITS) for i in range(VISITS)])  40.5 us
    ppermute x4, waiting for transfers between devices, swap_borders(): return (lax.ppermute(high, 'fp', up), lax.ppermute(low, 'fp', down))  22 us
    all_to_all x2, starting transfers between devices, exchange(): lax.all_to_all(sent, ('visit', 'fp'), split_axis=0, concat_axis=0, tiled=...  16.7 us
    pallas_call x2, Pallas kernels, scatter(): pl.pallas_call(scatter_body, grid_spec=pltpu.PrefetchScalarGridSpec(num_s...  15.1 us
    ppermute x4, starting transfers between devices, swap_borders(): return (lax.ppermute(high, 'fp', up), lax.ppermute(low, 'fp', down))  11.4 us
    ppermute x7, starting transfers between devices, slot_rows(): lax.ppermute(first, 'visit', [(i, (i + k) % VISITS) for i in range(VISITS)])  9.11 us
    unnamed x28, local copies, waits for them, and re-layouts  8.34 us
  transfers between devices with their start and end apart: 14, of which 10 were waited for; matrix products, arithmetic and copies ran while one was open for 0% of the time, Pallas kernels for 16%

profile of v2, /device:TPU:0, one launch (start us, length us, event | category | flops | bytes accessed | tf_op | source)
XLA Modules:
  0.0 197.2 jit_solution(16515773714297721507)
XLA Ops:
  1.3 1.7 pack.1
  2.9 8.1 %all-to-all-start = ((f32[16,24,128]{2,1,0:T(8,128)}), f32[16,24,128]{2,1,0:T(8,128)S(1)}, u32[]{:S(2)}, u32[]{:S(2)}) async-start(f32[16,24,128]{2,1,0:T(8,128)} %pack.1), calls=%async_computation | async-start | bytes 393216 | tf_op jit(solution)/shard_map/all_to_all | solution.py:384
  11.7 1.6 copy-done
  15.3 6.4 %send_weight.1 = (bf16[8,32,16,512]{3,2,1,0:T(8,128)(2,1)}, bf16[8,256,512]{2,1,0:T(8,128)(2,1)S(1)}) custom-call(f32[1,1,21]{2,1,0:T(1,128)S(1)} %copy-done.9, s32[1,1]{1,0:T(1,128)S(6)} %copy.17.shift_ref, s32[16]{0:T(128)S(1)} %bitcast.14, s32[1,32]{1,0:T(1,128)S(1)} %copy-done.11, bf16[1,256,4096]{2,1,0:T(8,128)(2,1)S(1)} %copy-done, ...), custom_call_target="tpu_custom_call" | custom-call | tf_op jit(solution)/shard_map/send_weight/pallas_call | solution.py:265
  23.0 10.8 %all-to-all-start.2 = ((bf16[128,2,16,512]{3,2,1,0:T(8,128)(2,1)}), bf16[128,2,16,512]{3,2,1,0:T(8,128)(2,1)}, u32[]{:S(2)}, u32[]{:S(2)}) async-start(bf16[128,2,16,512]{3,2,1,0:T(8,128)(2,1)} %bitcast.17), calls=%async_computation.2 | async-start | bytes 8388608 | tf_op jit(solution)/shard_map/all_to_all | solution.py:309
  35.5 7.7 %send_flux.1 = bf16[8,32,16,512]{3,2,1,0:T(8,128)(2,1)} custom-call(f32[1,1,21]{2,1,0:T(1,128)S(1)} %copy-done.10, s32[1,1]{1,0:T(1,128)S(6)} %copy.17.shift_ref, s32[16]{0:T(128)S(1)} %bitcast.15, s32[1,32]{1,0:T(1,128)S(1)} %copy-done.12, bf16[1,256,4096]{2,1,0:T(8,128)(2,1)S(1)} %copy-done.1, bf16[1,256,4096]{2,1,0:T(8,128)(2,1)S(1)} %copy-done.1, ...), custom_call_target="tpu_custom_call" | custom-call | tf_op jit(solution)/shard_map/send_flux/pallas_call | solution.py:291
  43.2 42.8 %all-to-all-done.2 = bf16[128,2,16,512]{3,2,1,0:T(8,128)(2,1)} async-done(((bf16[128,2,16,512]{3,2,1,0:T(8,128)(2,1)}), bf16[128,2,16,512]{3,2,1,0:T(8,128)(2,1)}, u32[]{:S(2)}, u32[]{:S(2)}) %all-to-all-start.2) | async-done | bytes 4194336 | tf_op jit(solution)/shard_map/all_to_all | solution.py:309
  85.9 6.0 %all-to-all-start.1 = ((bf16[128,2,16,512]{3,2,1,0:T(8,128)(2,1)}), bf16[128,2,16,512]{3,2,1,0:T(8,128)(2,1)}, u32[]{:S(2)}, u32[]{:S(2)}) async-start(bf16[128,2,16,512]{3,2,1,0:T(8,128)(2,1)} %bitcast.16), calls=%async_computation.1 | async-start | bytes 8388608 | tf_op jit(solution)/shard_map/all_to_all | solution.py:309
  92.1 1.8 collective-permute-start.6
  94.9 2.6 %collective-permute-start.3 = (f32[1,32]{1,0:T(1,128)S(1)}, f32[1,32]{1,0:T(1,128)S(1)}, u32[]{:S(2)}, u32[]{:S(2)}) collective-permute-start(f32[1,32]{1,0:T(1,128)S(1)} %concatenate.9), channel_id=1, source_target_pairs={{0,64},{16,80},{32,96},{48,112},{64,0},{80,16},{96,32},{112,48},{1... | collective-permute-start | bytes 392 | tf_op jit(solution)/shard_map/ppermute | solution.py:363
  97.5 37.0 %collective-permute-done.6 = f32[1,32]{1,0:T(1,128)S(1)} collective-permute-done((f32[1,32]{1,0:T(1,128)S(1)}, f32[1,32]{1,0:T(1,128)S(1)}, u32[]{:S(2)}, u32[]{:S(2)}) %collective-permute-start.6) | collective-permute-done | bytes 160 | tf_op jit(solution)/shard_map/ppermute | solution.py:363
  134.5 2.7 %collective-permute-start.1 = (f32[1,32]{1,0:T(1,128)S(1)}, f32[1,32]{1,0:T(1,128)S(1)}, u32[]{:S(2)}, u32[]{:S(2)}) collective-permute-start(f32[1,32]{1,0:T(1,128)S(1)} %concatenate.9), channel_id=1, source_target_pairs={{0,32},{16,48},{32,64},{48,80},{64,96},{80,112},{96,0},{112,16},{1... | collective-permute-start | bytes 392 | tf_op jit(solution)/shard_map/ppermute | solution.py:363
  139.9 1.8 collective-permute-done
  142.0 7.4 %scatter.3 = (f32[4,456,512]{2,1,0:T(8,128)S(1)}, bf16[4,200,512]{2,1,0:T(8,128)(2,1)S(1)}, bf16[4,200,512]{2,1,0:T(8,128)(2,1)S(1)}) custom-call(s32[2]{0:T(128)S(1)} %copy-done.8, s32[8]{0:T(128)S(1)} %copy-done.13, s32[8,1,512]{2,1,0:T(1,128)S(1)} %broadcast_add_fusion.rows_ref, bf16[8,512,512]{2,1,0:T(8,128)(2,1)} %bitcast.8.received_ref), custom_call_target="tpu_custom_call" | custom-call | tf_op jit(solution)/shard_map/scatter/pallas_call | solution.py:319
  149.4 1.8 copy-done.2
  151.3 4.2 %collective-permute-start.9 = (bf16[4,200,512]{2,1,0:T(8,128)(2,1)S(1)}, bf16[4,200,512]{2,1,0:T(8,128)(2,1)S(1)}, u32[]{:S(2)}, u32[]{:S(2)}) collective-permute-start(bf16[4,200,512]{2,1,0:T(8,128)(2,1)S(1)} %get-tuple-element.16), channel_id=1, source_target_pairs={{0,1},{1,2},{2,3},{3,4},{4,5},{5,6},{6,7},{7,8},{8,9},{9,10},{10,1... | collective-permute-start | bytes 2457608 | tf_op jit(solution)/shard_map/ppermute | solution.py:356
  156.8 7.7 %scatter.2 = (f32[4,456,512]{2,1,0:T(8,128)S(1)}, bf16[4,200,512]{2,1,0:T(8,128)(2,1)S(1)}, bf16[4,200,512]{2,1,0:T(8,128)(2,1)S(1)}) custom-call(s32[2]{0:T(128)S(1)} %copy-done.8, s32[8]{0:T(128)S(1)} %copy-done.13, s32[8,1,512]{2,1,0:T(1,128)S(1)} %broadcast_add_fusion.rows_ref, bf16[8,512,512]{2,1,0:T(8,128)(2,1)} %bitcast.4.received_ref), custom_call_target="tpu_custom_call" | custom-call | tf_op jit(solution)/shard_map/scatter/pallas_call | solution.py:319
  164.5 4.6 %collective-permute-start.7 = (bf16[4,200,512]{2,1,0:T(8,128)(2,1)S(1)}, bf16[4,200,512]{2,1,0:T(8,128)(2,1)S(1)}, u32[]{:S(2)}, u32[]{:S(2)}) collective-permute-start(bf16[4,200,512]{2,1,0:T(8,128)(2,1)S(1)} %get-tuple-element.12), channel_id=1, source_target_pairs={{0,1},{1,2},{2,3},{3,4},{4,5},{5,6},{6,7},{7,8},{8,9},{9,10},{10,1... | collective-permute-start | bytes 2457608 | tf_op jit(solution)/shard_map/ppermute | solution.py:356
  170.4 3.6 %collective-permute-done.9.before_ref = bf16[4,200,512]{2,1,0:T(8,128)(2,1)S(1)} collective-permute-done((bf16[4,200,512]{2,1,0:T(8,128)(2,1)S(1)}, bf16[4,200,512]{2,1,0:T(8,128)(2,1)S(1)}, u32[]{:S(2)}, u32[]{:S(2)}) %collective-permute-start.9) | collective-permute-done | bytes 819232 | tf_op jit(solution)/shard_map/ppermute | solution.py:356
  174.0 4.5 %collective-permute-done.10.after_ref = bf16[4,200,512]{2,1,0:T(8,128)(2,1)S(1)} collective-permute-done((bf16[4,200,512]{2,1,0:T(8,128)(2,1)S(1)}, bf16[4,200,512]{2,1,0:T(8,128)(2,1)S(1)}, u32[]{:S(2)}, u32[]{:S(2)}) %collective-permute-start.10) | collective-permute-done | bytes 819232 | tf_op jit(solution)/shard_map/ppermute | solution.py:356
  178.5 2.4 %merge.3 = f32[4,456,512]{2,1,0:T(8,128)} custom-call(f32[4,456,512]{2,1,0:T(8,128)S(1)} %copy-done.3, bf16[4,200,512]{2,1,0:T(8,128)(2,1)S(1)} %collective-permute-done.9.before_ref, bf16[4,200,512]{2,1,0:T(8,128)(2,1)S(1)} %collective-permute-done.10.after_ref), custom_call_target="tpu_custom_call" | custom-call | tf_op jit(solution)/shard_map/merge/pallas_call | solution.py:340
  180.9 9.8 %collective-permute-done.7.before_ref = bf16[4,200,512]{2,1,0:T(8,128)(2,1)S(1)} collective-permute-done((bf16[4,200,512]{2,1,0:T(8,128)(2,1)S(1)}, bf16[4,200,512]{2,1,0:T(8,128)(2,1)S(1)}, u32[]{:S(2)}, u32[]{:S(2)}) %collective-permute-start.7) | collective-permute-done | bytes 819232 | tf_op jit(solution)/shard_map/ppermute | solution.py:356
  190.7 4.2 %collective-permute-done.8.after_ref = bf16[4,200,512]{2,1,0:T(8,128)(2,1)S(1)} collective-permute-done((bf16[4,200,512]{2,1,0:T(8,128)(2,1)S(1)}, bf16[4,200,512]{2,1,0:T(8,128)(2,1)S(1)}, u32[]{:S(2)}, u32[]{:S(2)}) %collective-permute-start.8) | collective-permute-done | bytes 819232 | tf_op jit(solution)/shard_map/ppermute | solution.py:356
  194.8 2.3 %merge.2 = f32[4,456,512]{2,1,0:T(8,128)} custom-call(f32[4,456,512]{2,1,0:T(8,128)S(1)} %get-tuple-element.11.total_ref, bf16[4,200,512]{2,1,0:T(8,128)(2,1)S(1)} %collective-permute-done.7.before_ref, bf16[4,200,512]{2,1,0:T(8,128)(2,1)S(1)} %collective-permute-done.8.after_ref), custom_call_target="tpu_custom_call" | custom-call | tf_op jit(solution)/shard_map/merge/pallas_call | solution.py:340
  (49 shorter events, 12.3 us)
Async XLA Ops:
  2.9 20.1 %all-to-all-start = ((f32[16,24,128]{2,1,0:T(8,128)}), f32[16,24,128]{2,1,0:T(8,128)S(1)}, u32[]{:S(2)}, u32[]{:S(2)}) async-start(f32[16,24,128]{2,1,0:T(8,128)} %pack.1), calls=%async_computation | async-start | bytes 393216 | tf_op jit(solution)/shard_map/all_to_all | solution.py:384
  11.7 1.6 copy-start
  23.0 10.8 %copy-start.1 = (bf16[1,256,4096]{2,1,0:T(8,128)(2,1)S(1)}, bf16[1,256,4096]{2,1,0:T(8,128)(2,1)}, u32[]{:S(2)}) copy-start(bf16[1,256,4096]{2,1,0:T(8,128)(2,1)} %right_ref.3) | copy-start | bytes 6291460
  23.0 10.8 %copy-start.7 = (s32[1,16,1]{1,2,0:T(1,128)S(1)}, s32[1,16,1]{1,2,0:T(1,128)}, u32[]{:S(2)}) copy-start(s32[1,16,1]{1,2,0:T(1,128)} %param.17) | copy-start | bytes 196
  23.0 10.8 %copy-start.10 = (f32[1,1,21]{2,1,0:T(1,128)S(1)}, f32[1,1,21]{2,1,0:T(1,128)}, u32[]{:S(2)}) copy-start(f32[1,1,21]{2,1,0:T(1,128)} %psf_ref.3) | copy-start | bytes 256
  23.0 10.8 %copy-start.12 = (s32[1,32]{1,0:T(1,128)S(1)}, s32[1,32]{1,0:T(1,128)}, u32[]{:S(2)}) copy-start(s32[1,32]{1,0:T(1,128)} %bad_ref.3) | copy-start | bytes 388
  23.0 62.9 %all-to-all-start.2 = ((bf16[128,2,16,512]{3,2,1,0:T(8,128)(2,1)}), bf16[128,2,16,512]{3,2,1,0:T(8,128)(2,1)}, u32[]{:S(2)}, u32[]{:S(2)}) async-start(bf16[128,2,16,512]{3,2,1,0:T(8,128)(2,1)} %bitcast.17), calls=%async_computation.2 | async-start | bytes 8388608 | tf_op jit(solution)/shard_map/all_to_all | solution.py:309
  33.9 1.6 copy-start.5
  85.9 56.0 %copy-start.8 = (s32[2]{0:T(128)S(1)}, s32[2]{0:T(128)}, u32[]{:S(2)}) copy-start(s32[2]{0:T(128)} %pad_add_fusion.where_ref) | copy-start | bytes 28
  85.9 56.0 %copy-start.13 = (s32[8]{0:T(128)S(1)}, s32[8]{0:T(128)}, u32[]{:S(2)}) copy-start(s32[8]{0:T(128)} %band_ref.3) | copy-start | bytes 100
  85.9 70.8 %all-to-all-start.1 = ((bf16[128,2,16,512]{3,2,1,0:T(8,128)(2,1)}), bf16[128,2,16,512]{3,2,1,0:T(8,128)(2,1)}, u32[]{:S(2)}, u32[]{:S(2)}) async-start(bf16[128,2,16,512]{3,2,1,0:T(8,128)(2,1)} %bitcast.16), calls=%async_computation.1 | async-start | bytes 8388608 | tf_op jit(solution)/shard_map/all_to_all | solution.py:309
  92.1 42.4 %collective-permute-start.6 = (f32[1,32]{1,0:T(1,128)S(1)}, f32[1,32]{1,0:T(1,128)S(1)}, u32[]{:S(2)}, u32[]{:S(2)}) collective-permute-start(f32[1,32]{1,0:T(1,128)S(1)} %concatenate.9), channel_id=1, source_target_pairs={{0,112},{16,0},{32,16},{48,32},{64,48},{80,64},{96,80},{112,96},{1... | collective-permute-start | bytes 392 | tf_op jit(solution)/shard_map/ppermute | solution.py:363
  93.9 43.6 %collective-permute-start.5 = (f32[1,32]{1,0:T(1,128)S(1)}, f32[1,32]{1,0:T(1,128)S(1)}, u32[]{:S(2)}, u32[]{:S(2)}) collective-permute-start(f32[1,32]{1,0:T(1,128)S(1)} %concatenate.9), channel_id=1, source_target_pairs={{0,96},{16,112},{32,0},{48,16},{64,32},{80,48},{96,64},{112,80},{1... | collective-permute-start | bytes 392 | tf_op jit(solution)/shard_map/ppermute | solution.py:363
  94.7 43.8 %collective-permute-start.4 = (f32[1,32]{1,0:T(1,128)S(1)}, f32[1,32]{1,0:T(1,128)S(1)}, u32[]{:S(2)}, u32[]{:S(2)}) collective-permute-start(f32[1,32]{1,0:T(1,128)S(1)} %concatenate.9), channel_id=1, source_target_pairs={{0,80},{16,96},{32,112},{48,0},{64,16},{80,32},{96,48},{112,64},{1... | collective-permute-start | bytes 392 | tf_op jit(solution)/shard_map/ppermute | solution.py:363
  94.9 44.2 %collective-permute-start.3 = (f32[1,32]{1,0:T(1,128)S(1)}, f32[1,32]{1,0:T(1,128)S(1)}, u32[]{:S(2)}, u32[]{:S(2)}) collective-permute-start(f32[1,32]{1,0:T(1,128)S(1)} %concatenate.9), channel_id=1, source_target_pairs={{0,64},{16,80},{32,96},{48,112},{64,0},{80,16},{96,32},{112,48},{1... | collective-permute-start | bytes 392 | tf_op jit(solution)/shard_map/ppermute | solution.py:363
  97.5 41.5 %collective-permute-start.2 = (f32[1,32]{1,0:T(1,128)S(1)}, f32[1,32]{1,0:T(1,128)S(1)}, u32[]{:S(2)}, u32[]{:S(2)}) collective-permute-start(f32[1,32]{1,0:T(1,128)S(1)} %concatenate.9), channel_id=1, source_target_pairs={{0,48},{16,64},{32,80},{48,96},{64,112},{80,0},{96,16},{112,32},{1... | collective-permute-start | bytes 392 | tf_op jit(solution)/shard_map/ppermute | solution.py:363
  134.5 5.4 %collective-permute-start.1 = (f32[1,32]{1,0:T(1,128)S(1)}, f32[1,32]{1,0:T(1,128)S(1)}, u32[]{:S(2)}, u32[]{:S(2)}) collective-permute-start(f32[1,32]{1,0:T(1,128)S(1)} %concatenate.9), channel_id=1, source_target_pairs={{0,32},{16,48},{32,64},{48,80},{64,96},{80,112},{96,0},{112,16},{1... | collective-permute-start | bytes 392 | tf_op jit(solution)/shard_map/ppermute | solution.py:363
  137.5 4.2 %collective-permute-start = (f32[1,32]{1,0:T(1,128)S(1)}, f32[1,32]{1,0:T(1,128)S(1)}, u32[]{:S(2)}, u32[]{:S(2)}) collective-permute-start(f32[1,32]{1,0:T(1,128)S(1)} %concatenate.9), channel_id=1, source_target_pairs={{0,16},{16,32},{32,48},{48,64},{64,80},{80,96},{96,112},{112,0},{1... | collective-permute-start | bytes 392 | tf_op jit(solution)/shard_map/ppermute | solution.py:363
  149.4 1.9 copy-start.2
  151.3 22.7 %collective-permute-start.9 = (bf16[4,200,512]{2,1,0:T(8,128)(2,1)S(1)}, bf16[4,200,512]{2,1,0:T(8,128)(2,1)S(1)}, u32[]{:S(2)}, u32[]{:S(2)}) collective-permute-start(bf16[4,200,512]{2,1,0:T(8,128)(2,1)S(1)} %get-tuple-element.16), channel_id=1, source_target_pairs={{0,1},{1,2},{2,3},{3,4},{4,5},{5,6},{6,7},{7,8},{8,9},{9,10},{10,1... | collective-permute-start | bytes 2457608 | tf_op jit(solution)/shard_map/ppermute | solution.py:356
  155.5 23.0 %collective-permute-start.10 = (bf16[4,200,512]{2,1,0:T(8,128)(2,1)S(1)}, bf16[4,200,512]{2,1,0:T(8,128)(2,1)S(1)}, u32[]{:S(2)}, u32[]{:S(2)}) collective-permute-start(bf16[4,200,512]{2,1,0:T(8,128)(2,1)S(1)} %get-tuple-element.17), channel_id=1, source_target_pairs={{1,0},{2,1},{3,2},{4,3},{5,4},{6,5},{7,6},{8,7},{9,8},{10,9},{11,1... | collective-permute-start | bytes 2457608 | tf_op jit(solution)/shard_map/ppermute | solution.py:356
  156.8 21.7 %copy-start.3 = (f32[4,456,512]{2,1,0:T(8,128)S(1)}, f32[4,456,512]{2,1,0:T(8,128)}, u32[]{:S(2)}) copy-start(f32[4,456,512]{2,1,0:T(8,128)} %copy-done.2) | copy-start | bytes 11206660
  164.5 26.2 %collective-permute-start.7 = (bf16[4,200,512]{2,1,0:T(8,128)(2,1)S(1)}, bf16[4,200,512]{2,1,0:T(8,128)(2,1)S(1)}, u32[]{:S(2)}, u32[]{:S(2)}) collective-permute-start(bf16[4,200,512]{2,1,0:T(8,128)(2,1)S(1)} %get-tuple-element.12), channel_id=1, source_target_pairs={{0,1},{1,2},{2,3},{3,4},{4,5},{5,6},{6,7},{7,8},{8,9},{9,10},{10,1... | collective-permute-start | bytes 2457608 | tf_op jit(solution)/shard_map/ppermute | solution.py:356
  169.1 25.7 %collective-permute-start.8 = (bf16[4,200,512]{2,1,0:T(8,128)(2,1)S(1)}, bf16[4,200,512]{2,1,0:T(8,128)(2,1)S(1)}, u32[]{:S(2)}, u32[]{:S(2)}) collective-permute-start(bf16[4,200,512]{2,1,0:T(8,128)(2,1)S(1)} %get-tuple-element.13), channel_id=1, source_target_pairs={{1,0},{2,1},{3,2},{4,3},{5,4},{6,5},{7,6},{8,7},{9,8},{10,9},{11,1... | collective-permute-start | bytes 2457608 | tf_op jit(solution)/shard_map/ppermute | solution.py:356
  (4 other events, 3.3 us)

commit v3 on v2

--- a/solution.py
+++ b/solution.py
@@ -26,8 +26,15 @@
 GROUPS = 16
 GRID_ROWS = 16
 PACKED = GRID_ROWS + 8
+BAD_COUNT = 32
+AT_SLOT = 0
+AT_BAD = 16
+AT_SHIFT = 48
+AT_VISIT = 49
+AT_ORDER = 56
 SPAN = ROW_PIX // VISITS
 CHUNKS = 1
+LIM = 60
 BLOCK = 256
 PAD = 128
 WINDOW = BLOCK + 2 * PAD
@@ -35,11 +42,11 @@
 WIDTH = SPAN // CHUNKS
 
 
-def fill_band(psf_ref, shift_ref, band_ref, absolute):
+def fill_band(table_ref, psf_ref, band_ref, absolute):
     shape = (16, WINDOW)
     step = lax.broadcasted_iota(jnp.int32, shape, 0) - 2
     lag = 3 * PAD - lax.broadcasted_iota(jnp.int32, shape, 1) - step
-    offset = (shift_ref[0, 0] - 16 * step).astype(jnp.float32) / 16.0
+    offset = (table_ref[0, AT_SHIFT] - 16 * step).astype(jnp.float32) / 16.0
     angle = offset * jnp.float32(jnp.pi)
     safe = jnp.where(offset == 0.0, 1.0, angle)
     lanczos = jnp.where(
@@ -48,9 +55,9 @@
     lanczos = jnp.where((jnp.abs(offset) < 3.0) & (step < 7), lanczos, 0.0)
     lanczos = lanczos / jnp.sum(lanczos, axis=0, keepdims=True)
     taps = jnp.zeros(shape, jnp.float32)
-    total = psf_ref[0, 0, 0]
+    total = psf_ref[0, 0]
     for e in range(2 * TAPS_HALF + 1):
-        value = psf_ref[0, 0, e]
+        value = psf_ref[0, e]
         taps = jnp.where(lag == e - TAPS_HALF, value, taps)
         total = total + value if e else total
     combined = jnp.sum(lanczos * (taps / total), axis=0, keepdims=True)
@@ -66,11 +73,11 @@
             ]
 
 
-def fill_good(bad_ref, good_ref):
+def fill_good(table_ref, good_ref):
     columns = lax.broadcasted_iota(jnp.int32, good_ref.shape, 1) - PAD
     good = (columns >= 0) & (columns < ROW_PIX)
-    for k in range(bad_ref.shape[-1]):
-        good = good & (columns != bad_ref[0, k])
+    for k in range(BAD_COUNT):
+        good = good & (columns != table_ref[0, AT_BAD + k])
     good_ref[...] = good.astype(jnp.float32)
 
 
@@ -86,33 +93,50 @@
     return parts[0] if len(parts) == 1 else jnp.concatenate(parts, axis=1)
 
 
-def send_pieces(patch_ref, out_ref, values):
+def send_pieces(table_ref, out_ref, values):
     out_ref[...] = jnp.zeros(out_ref.shape, out_ref.dtype)
-    patches = [patch_ref[j] for j in range(PIECES)]
     for j in range(PIECES):
-        rank = jnp.int32(0)
-        for k in range(j):
-            rank = rank + (patches[k] == patches[j]).astype(jnp.int32)
-        slot = patches[j] * MOST + jnp.minimum(rank, MOST - 1)
-        out_ref[0, slot] = values[PIECE_ROWS * j : PIECE_ROWS * (j + 1)]
-
-
-def pack_body(where_ref, mix_ref, patch_ref, pos_ref, grid_ref, out_ref):
-    group = where_ref[1]
+        out_ref[0, table_ref[0, AT_SLOT + j]] = values[PIECE_ROWS * j : PIECE_ROWS * (j + 1)]
+
+
+def pack_body(
+    mix_ref, patch_ref, pos_ref, psf_ref, shift_ref, bad_ref, band_ref, grid_ref, out_ref, table_ref, taps_ref
+):
+    group = lax.axis_index("fp")
     shape = (PATCHES, BINS)
     patch = lax.broadcasted_iota(jnp.int32, shape, 0)
     slot = lax.broadcasted_iota(jnp.int32, shape, 1)
+    lane = lax.broadcasted_iota(jnp.int32, (1, BINS), 1)
     first = jnp.full(shape, UNUSED, jnp.int32)
     patches = [patch_ref[j] for j in range(PIECES)]
+    table = jnp.zeros((1, BINS), jnp.int32)
     for j in range(PIECES):
         rank = jnp.int32(0)
         for k in range(j):
             rank = rank + (patches[k] == patches[j]).astype(jnp.int32)
         first = jnp.where((patch == patches[j]) & (slot == rank), pos_ref[0, j], first)
+        table = jnp.where(
+            lane == AT_SLOT + j, patches[j] * MOST + jnp.minimum(rank, MOST - 1), table
+        )
     first = first.astype(jnp.float32)
     for q in range(PATCHES):
         out_ref[q, :GRID_ROWS] = grid_ref[0, 0] * mix_ref[q, group]
         out_ref[q, GRID_ROWS:] = jnp.broadcast_to(first[q : q + 1], (PACKED - GRID_ROWS, BINS))
+    for k in range(BAD_COUNT):
+        table = jnp.where(lane == AT_BAD + k, bad_ref[0, k], table)
+    table = jnp.where(lane == AT_SHIFT, shift_ref[0, 0], table)
+    table = jnp.where(lane == AT_VISIT, lax.axis_index("visit"), table)
+    bands = [band_ref[v] for v in range(VISITS)]
+    for v in range(VISITS):
+        place = bands[v] * (VISITS // BANDS)
+        for u in range(v):
+            place = place + (bands[u] == bands[v]).astype(jnp.int32)
+        table = jnp.where(lane == AT_ORDER + place, v, table)
+    table_ref[...] = table
+    taps = jnp.zeros((1, BINS), jnp.float32)
+    for e in range(2 * TAPS_HALF + 1):
+        taps = jnp.where(lane == e, psf_ref[0, 0, e], taps)
+    taps_ref[...] = taps
 
 
 def masked_window(chunk, good_ref, left_ref, mid_ref, right_ref):
@@ -125,10 +149,8 @@
 
 def weight_body(
     chunk,
+    table_ref,
     psf_ref,
-    shift_ref,
-    patch_ref,
-    bad_ref,
     left_ref,
     mid_ref,
     right_ref,
@@ -139,21 +161,19 @@
 ):
     @pl.when(pl.program_id(0) == 0)
     def _():
-        fill_good(bad_ref, good_ref)
-        fill_band(psf_ref, shift_ref, band_ref, True)
+        fill_good(table_ref, good_ref)
+        fill_band(table_ref, psf_ref, band_ref, True)
 
     _, _, window = masked_window(chunk, good_ref, left_ref, mid_ref, right_ref)
     weight = convolve(window, band_ref, mid_ref.shape[-1]).astype(jnp.bfloat16)
     weight_ref[0] = weight
-    send_pieces(patch_ref, send_ref, weight)
+    send_pieces(table_ref, send_ref, weight)
 
 
 def flux_body(
     chunk,
+    table_ref,
     psf_ref,
-    shift_ref,
-    patch_ref,
-    bad_ref,
     left_ref,
     mid_ref,
     right_ref,
@@ -166,8 +186,8 @@
 ):
     @pl.when(pl.program_id(0) == 0)
     def _():
-        fill_good(bad_ref, good_ref)
-        fill_band(psf_ref, shift_ref, band_ref, False)
+        fill_good(table_ref, good_ref)
+        fill_band(table_ref, psf_ref, band_ref, False)
         model = packed_ref[0, :GRID_ROWS]
         for k in range(1, GROUPS):
             model = model + packed_ref[k, :GRID_ROWS]
@@ -191,29 +211,28 @@
     ).reshape(CCD_ROWS, width)
     flux = warped[:CCD_ROWS] - backdrop
     send_pieces(
-        patch_ref, send_ref, (flux * weight_ref[0].astype(jnp.float32)).astype(jnp.bfloat16)
-    )
-
-
-def scatter_body(where_ref, band_ref, rows_ref, received_ref, total_ref, low_ref, high_ref):
-    visit = pl.program_id(0)
-
-    @pl.when(visit == 0)
-    def _():
-        total_ref[...] = jnp.zeros(total_ref.shape, total_ref.dtype)
-
+        table_ref, send_ref, (flux * weight_ref[0].astype(jnp.float32)).astype(jnp.bfloat16)
+    )
+
+
+def scatter_body(table_ref, rows_ref, received_ref, total_ref, low_ref, high_ref):
+    turn = pl.program_id(1)
     slots = rows_ref.shape[-1]
     place = lax.broadcasted_iota(jnp.int32, (FRAME, slots), 0) == rows_ref[0]
     frames = jnp.dot(
         place.astype(jnp.bfloat16), received_ref[0], preferred_element_type=jnp.float32
     )
-    band = band_ref[visit]
-    total_ref[band] = total_ref[band] + frames
-
-    @pl.when(visit == pl.num_programs(0) - 1)
+
+    @pl.when(turn == 0)
     def _():
-        low_ref[...] = total_ref[:, :EDGE].astype(jnp.bfloat16)
-        high_ref[...] = total_ref[:, FRAME - EDGE :].astype(jnp.bfloat16)
+        total_ref[0] = frames
+
+    @pl.when(turn == 1)
+    def _():
+        total = total_ref[0] + frames
+        total_ref[0] = total
+        low_ref[0] = total[:EDGE].astype(jnp.bfloat16)
+        high_ref[0] = total[FRAME - EDGE :].astype(jnp.bfloat16)
 
 
 def merge_body(total_ref, before_ref, after_ref, *refs):
@@ -261,37 +280,41 @@
 BAND_SCRATCH = pltpu.VMEM((WINDOW, BLOCK), jnp.bfloat16)
 
 
-def send_weight(chunk, psf, shift, patches, bad, inv_var):
+def send_weight(chunk, table, psf, inv_var):
     return pl.pallas_call(
         functools.partial(weight_body, chunk),
         grid=(VISITS,),
-        in_specs=[SMEM] * 4 + window_specs(chunk),
+        in_specs=[SMEM] * 2 + window_specs(chunk),
         out_specs=[SEND_BLOCK, WEIGHT_BLOCK],
         out_shape=[
             jax.ShapeDtypeStruct(SEND_SHAPE, jnp.bfloat16),
             jax.ShapeDtypeStruct((VISITS, CCD_ROWS, WIDTH), jnp.bfloat16),
         ],
         scratch_shapes=[GOOD_SCRATCH, BAND_SCRATCH],
-        compiler_params=params(48),
+        compiler_params=params(LIM),
         name="send_weight",
-    )(psf, shift, patches, bad, inv_var, inv_var, inv_var)
-
-
-def pack(where, mix, patches, starts, grid):
+    )(table, psf, inv_var, inv_var, inv_var)
+
+
+def pack(*smalls):
     return pl.pallas_call(
         pack_body,
-        in_specs=[SMEM] * 4 + [pl.BlockSpec(memory_space=pltpu.VMEM)],
-        out_specs=pl.BlockSpec(memory_space=pltpu.VMEM),
-        out_shape=jax.ShapeDtypeStruct((PATCHES, PACKED, BINS), jnp.float32),
+        in_specs=[SMEM] * (len(smalls) - 1) + [pl.BlockSpec(memory_space=pltpu.VMEM)],
+        out_specs=[pl.BlockSpec(memory_space=pltpu.VMEM)] * 3,
+        out_shape=[
+            jax.ShapeDtypeStruct((PATCHES, PACKED, BINS), jnp.float32),
+            jax.ShapeDtypeStruct((1, BINS), jnp.int32),
+            jax.ShapeDtypeStruct((1, BINS), jnp.float32),
+        ],
         name="pack",
-    )(where, mix, patches, starts, grid)
-
-
-def send_flux(chunk, psf, shift, patches, bad, image, packed, weight):
+    )(*smalls)
+
+
+def send_flux(chunk, table, psf, image, packed, weight):
     return pl.pallas_call(
         functools.partial(flux_body, chunk),
         grid=(VISITS,),
-        in_specs=[SMEM] * 4 + window_specs(chunk) + [whole(packed.shape), WEIGHT_BLOCK],
+        in_specs=[SMEM] * 2 + window_specs(chunk) + [whole(packed.shape), WEIGHT_BLOCK],
         out_specs=SEND_BLOCK,
         out_shape=jax.ShapeDtypeStruct(SEND_SHAPE, jnp.bfloat16),
         scratch_shapes=[
@@ -299,9 +322,9 @@
             BAND_SCRATCH,
             pltpu.VMEM((2 * GRID_ROWS, BINS), jnp.bfloat16),
         ],
-        compiler_params=params(48),
+        compiler_params=params(LIM),
         name="send_flux",
-    )(psf, shift, patches, bad, image, image, image, packed, weight)
+    )(table, psf, image, image, image, packed, weight)
 
 
 def exchange(pieces):
@@ -309,29 +332,40 @@
     return lax.all_to_all(sent, ("visit", "fp"), split_axis=0, concat_axis=0, tiled=True)
 
 
-def scatter(where, band_of_visit, dest_rows, received):
+def scatter(table, dest_rows, received):
     slots = PATCHES * MOST * PIECE_ROWS
     shapes = [
         jax.ShapeDtypeStruct((BANDS, FRAME, WIDTH), jnp.float32),
         jax.ShapeDtypeStruct((BANDS, EDGE, WIDTH), jnp.bfloat16),
         jax.ShapeDtypeStruct((BANDS, EDGE, WIDTH), jnp.bfloat16),
     ]
+    turns = VISITS // BANDS
+
+    def visit(b, j, at):
+        return at[0, AT_ORDER + turns * b + j]
+
     return pl.pallas_call(
         scatter_body,
         grid_spec=pltpu.PrefetchScalarGridSpec(
             num_scalar_prefetch=1,
-            grid=(VISITS,),
+            grid=(BANDS, turns),
             in_specs=[
-                SMEM,
-                pl.BlockSpec((1, 1, slots), lambda i, at: ((at[0] - i) & (VISITS - 1), 0, 0)),
-                pl.BlockSpec((1, slots, WIDTH), lambda i, at: (i, 0, 0)),
+                pl.BlockSpec(
+                    (1, 1, slots),
+                    lambda b, j, at: ((at[0, AT_VISIT] - visit(b, j, at)) & (VISITS - 1), 0, 0),
+                ),
+                pl.BlockSpec((1, slots, WIDTH), lambda b, j, at: (visit(b, j, at), 0, 0)),
             ],
-            out_specs=[whole(shape.shape) for shape in shapes],
+            out_specs=[
+                pl.BlockSpec((1,) + shape.shape[1:], lambda b, j, at: (b, 0, 0)) for shape in shapes
+            ],
         ),
         out_shape=shapes,
-        compiler_params=params(20),
+        compiler_params=pltpu.CompilerParams(
+            dimension_semantics=("arbitrary", "arbitrary"), vmem_limit_bytes=16 << 20
+        ),
         name="scatter",
-    )(where, band_of_visit, dest_rows, received.reshape(VISITS, slots, WIDTH))
+    )(table, dest_rows, received.reshape(VISITS, slots, WIDTH))
 
 
 def merge(chunk, total, before, after, earlier):
@@ -378,25 +412,30 @@
     piece_pos,
     band_of_visit,
 ):
-    where = jnp.stack([lax.axis_index("visit"), lax.axis_index("fp")]).astype(jnp.int32)
-    patches = piece_patch[0, :, 0]
-    packed = pack(where, bg_mix, patches, piece_pos, bg_grid)
+    packed, table, psf = pack(
+        bg_mix,
+        piece_patch[0, :, 0],
+        piece_pos,
+        psf_taps,
+        warp_shift,
+        bad_cols,
+        band_of_visit,
+        bg_grid,
+    )
     packed = lax.all_to_all(packed, "fp", split_axis=0, concat_axis=0, tiled=True)
-    common = (psf_taps, warp_shift, patches, bad_cols)
     chunks = range(SPAN // WIDTH)
     weights, arrived = [], []
     for chunk in chunks:
-        pieces, weight = send_weight(chunk, *common, inv_var)
+        pieces, weight = send_weight(chunk, table, psf, inv_var)
         weights.append(weight)
         arrived.append(exchange(pieces))
-    for chunk in chunks:
-        arrived.append(
-            exchange(send_flux(chunk, *common, image, packed, weights[chunk]))
-        )
+    fluxes = [send_flux(chunk, table, psf, image, packed, weights[chunk]) for chunk in chunks]
     dest_rows = slot_rows(packed[:, GRID_ROWS, :MOST])
+    fluxes, dest_rows = lax.optimization_barrier((fluxes, dest_rows))
+    arrived += [exchange(pieces) for pieces in fluxes]
     outs = [[], []]
     for turn, received in enumerate(arrived):
-        total, low, high = scatter(where, band_of_visit, dest_rows, received)
+        total, low, high = scatter(table, dest_rows, received)
         kind, chunk = divmod(turn, len(chunks))
         outs[kind] = [merge(chunk, total, *swap_borders(low, high), outs[kind])]
     return (outs[1][0][:, None], outs[0][0][:, None])

time: 198 us -> 180 us (0.909)
  the two profiles are of different devices: /device:TPU:0 before, /device:TPU:102 now
where the time goes in v3:
time: 180 us; the launch traced here: 179 us
  waiting for transfers between devices  84.9 us (47%)
  starting transfers between devices  51 us (28%)
  Pallas kernels  39.1 us (22%)
  local copies, waits for them, and re-layouts  2.29 us (1%)
    all_to_all x2, waiting for transfers between devices, exchange(): lax.all_to_all(sent, ('visit', 'fp'), split_axis=0, concat_axis=0, tiled=...  35.6 us
    ppermute x7, waiting for transfers between devices, slot_rows(): lax.ppermute(first, 'visit', [(i, (i + k) % VISITS) for i in range(VISITS)])  29.7 us
    all_to_all x2, starting transfers between devices, exchange(): lax.all_to_all(sent, ('visit', 'fp'), split_axis=0, concat_axis=0, tiled=...  21.2 us
    ppermute x4, waiting for transfers between devices, swap_borders(): return (lax.ppermute(high, 'fp', up), lax.ppermute(low, 'fp', down))  19.6 us
    pallas_call x2, Pallas kernels, scatter(): pl.pallas_call(scatter_body, grid_spec=pltpu.PrefetchScalarGridSpec(num_s...  15.2 us
    ppermute x4, starting transfers between devices, swap_borders(): return (lax.ppermute(high, 'fp', up), lax.ppermute(low, 'fp', down))  13.8 us
    pallas_call x1, Pallas kernels, send_flux(): pl.pallas_call(functools.partial(flux_body, chunk), grid=(VISITS,), in_sp...  9.31 us
    ppermute x7, starting transfers between devices, slot_rows(): lax.ppermute(first, 'visit', [(i, (i + k) % VISITS) for i in range(VISITS)])  8.79 us
  transfers between devices with their start and end apart: 14, of which 7 were waited for; matrix products, arithmetic and copies ran while one was open for 0% of the time, Pallas kernels for 20%

profile of v3, /device:TPU:102, one launch (start us, length us, event | category | flops | bytes accessed | tf_op | source)
XLA Modules:
  0.0 178.8 jit_solution(7239244576226963783)
XLA Ops:
  1.3 1.8 pack.1
  3.0 7.2 %all-to-all-start = ((f32[16,24,128]{2,1,0:T(8,128)}), f32[16,24,128]{2,1,0:T(8,128)S(1)}, u32[]{:S(2)}, u32[]{:S(2)}) async-start(f32[16,24,128]{2,1,0:T(8,128)} %get-tuple-element.17), calls=%async_computation | async-start | bytes 393216 | tf_op jit(solution)/shard_map/all_to_all | solution.py:425
  10.2 8.1 %send_weight.1 = (bf16[8,32,16,512]{3,2,1,0:T(8,128)(2,1)}, bf16[8,256,512]{2,1,0:T(8,128)(2,1)}) custom-call(s32[1,128]{1,0:T(1,128)} %get-tuple-element.15.table_ref, f32[1,128]{1,0:T(1,128)} %get-tuple-element.16.psf_ref, bf16[1,256,4096]{2,1,0:T(8,128)(2,1)} %right_ref.2, bf16[1,256,4096]{2,1,0:T(8,128)(2,1)} %right_ref.2, bf16[1,256,4096]{2,1,0:T(8,128)(2,1)} %right_ref.2), custom_call_target="tpu_custom_call" | custom-call | tf_op jit(solution)/shard_map/send_weight/pallas_call | solution.py:284
  18.4 10.3 %all-to-all-start.2 = ((bf16[128,2,16,512]{3,2,1,0:T(8,128)(2,1)}), bf16[128,2,16,512]{3,2,1,0:T(8,128)(2,1)}, u32[]{:S(2)}, u32[]{:S(2)}) async-start(bf16[128,2,16,512]{3,2,1,0:T(8,128)(2,1)} %bitcast.12), calls=%async_computation.2 | async-start | bytes 8388608 | tf_op jit(solution)/shard_map/all_to_all | solution.py:332
  30.7 2.6 %collective-permute-start.3 = (f32[1,32]{1,0:T(1,128)S(1)}, f32[1,32]{1,0:T(1,128)S(1)}, u32[]{:S(2)}, u32[]{:S(2)}) collective-permute-start(f32[1,32]{1,0:T(1,128)S(1)} %concatenate.9), channel_id=1, source_target_pairs={{0,64},{16,80},{32,96},{48,112},{64,0},{80,16},{96,32},{112,48},{1... | collective-permute-start | bytes 392 | tf_op jit(solution)/shard_map/ppermute | solution.py:397
  33.4 2.1 %collective-permute-start.2 = (f32[1,32]{1,0:T(1,128)S(1)}, f32[1,32]{1,0:T(1,128)S(1)}, u32[]{:S(2)}, u32[]{:S(2)}) collective-permute-start(f32[1,32]{1,0:T(1,128)S(1)} %concatenate.9), channel_id=1, source_target_pairs={{0,48},{16,64},{32,80},{48,96},{64,112},{80,0},{96,16},{112,32},{1... | collective-permute-start | bytes 392 | tf_op jit(solution)/shard_map/ppermute | solution.py:397
  35.4 9.3 %send_flux.1 = bf16[8,32,16,512]{3,2,1,0:T(8,128)(2,1)} custom-call(s32[1,128]{1,0:T(1,128)} %get-tuple-element.15.table_ref, f32[1,128]{1,0:T(1,128)} %get-tuple-element.16.psf_ref, bf16[1,256,4096]{2,1,0:T(8,128)(2,1)} %right_ref.3, bf16[1,256,4096]{2,1,0:T(8,128)(2,1)} %right_ref.3, bf16[1,256,4096]{2,1,0:T(8,128)(2,1)} %right_ref.3, ...), custom_call_target="tpu_custom_call" | custom-call | tf_op jit(solution)/shard_map/send_flux/pallas_call | solution.py:314
  44.8 28.4 %collective-permute-done.6 = f32[1,32]{1,0:T(1,128)S(1)} collective-permute-done((f32[1,32]{1,0:T(1,128)S(1)}, f32[1,32]{1,0:T(1,128)S(1)}, u32[]{:S(2)}, u32[]{:S(2)}) %collective-permute-start.6) | collective-permute-done | bytes 160 | tf_op jit(solution)/shard_map/ppermute | solution.py:397
  73.2 2.3 %collective-permute-start = (f32[1,32]{1,0:T(1,128)S(1)}, f32[1,32]{1,0:T(1,128)S(1)}, u32[]{:S(2)}, u32[]{:S(2)}) collective-permute-start(f32[1,32]{1,0:T(1,128)S(1)} %concatenate.9), channel_id=1, source_target_pairs={{0,16},{16,32},{32,48},{48,64},{64,80},{80,96},{96,112},{112,0},{1... | collective-permute-start | bytes 392 | tf_op jit(solution)/shard_map/ppermute | solution.py:397
  75.5 1.3 collective-permute-done.1
  78.1 10.9 %all-to-all-start.1 = ((bf16[128,2,16,512]{3,2,1,0:T(8,128)(2,1)}), bf16[128,2,16,512]{3,2,1,0:T(8,128)(2,1)}, u32[]{:S(2)}, u32[]{:S(2)}) async-start(bf16[128,2,16,512]{3,2,1,0:T(8,128)(2,1)} %bitcast.11), calls=%async_computation.1 | async-start | bytes 8388608 | tf_op jit(solution)/shard_map/all_to_all | solution.py:332
  89.0 7.5 %scatter.3 = (f32[4,456,512]{2,1,0:T(8,128)S(1)}, bf16[4,200,512]{2,1,0:T(8,128)(2,1)S(1)}, bf16[4,200,512]{2,1,0:T(8,128)(2,1)S(1)}) custom-call(s32[1,128]{1,0:T(1,128)S(1)} %copy-done.2, s32[8,1,512]{2,1,0:T(1,128)S(1)} %broadcast_add_fusion.rows_ref, bf16[8,512,512]{2,1,0:T(8,128)(2,1)} %bitcast.6.received_ref), custom_call_target="tpu_custom_call" | custom-call | tf_op jit(solution)/shard_map/scatter/pallas_call | solution.py:347
  96.5 1.8 %copy-done = f32[4,456,512]{2,1,0:T(8,128)} copy-done((f32[4,456,512]{2,1,0:T(8,128)}, f32[4,456,512]{2,1,0:T(8,128)S(1)}, u32[]{:S(2)}) %copy-start) | copy-done | bytes 3735576
  98.3 2.7 %collective-permute-start.9 = (bf16[4,200,512]{2,1,0:T(8,128)(2,1)S(1)}, bf16[4,200,512]{2,1,0:T(8,128)(2,1)S(1)}, u32[]{:S(2)}, u32[]{:S(2)}) collective-permute-start(bf16[4,200,512]{2,1,0:T(8,128)(2,1)S(1)} %get-tuple-element.26), channel_id=1, source_target_pairs={{0,1},{1,2},{2,3},{3,4},{4,5},{5,6},{6,7},{7,8},{8,9},{9,10},{10,1... | collective-permute-start | bytes 2457608 | tf_op jit(solution)/shard_map/ppermute | solution.py:390
  101.0 3.2 %collective-permute-start.10 = (bf16[4,200,512]{2,1,0:T(8,128)(2,1)S(1)}, bf16[4,200,512]{2,1,0:T(8,128)(2,1)S(1)}, u32[]{:S(2)}, u32[]{:S(2)}) collective-permute-start(bf16[4,200,512]{2,1,0:T(8,128)(2,1)S(1)} %get-tuple-element.27), channel_id=1, source_target_pairs={{1,0},{2,1},{3,2},{4,3},{5,4},{6,5},{7,6},{8,7},{9,8},{10,9},{11,1... | collective-permute-start | bytes 2457608 | tf_op jit(solution)/shard_map/ppermute | solution.py:390
  104.2 34.6 %all-to-all-done.1 = bf16[128,2,16,512]{3,2,1,0:T(8,128)(2,1)} async-done(((bf16[128,2,16,512]{3,2,1,0:T(8,128)(2,1)}), bf16[128,2,16,512]{3,2,1,0:T(8,128)(2,1)}, u32[]{:S(2)}, u32[]{:S(2)}) %all-to-all-start.1) | async-done | bytes 4194336 | tf_op jit(solution)/shard_map/all_to_all | solution.py:332
  138.7 7.7 %scatter.2 = (f32[4,456,512]{2,1,0:T(8,128)S(1)}, bf16[4,200,512]{2,1,0:T(8,128)(2,1)S(1)}, bf16[4,200,512]{2,1,0:T(8,128)(2,1)S(1)}) custom-call(s32[1,128]{1,0:T(1,128)S(1)} %copy-done.2, s32[8,1,512]{2,1,0:T(1,128)S(1)} %broadcast_add_fusion.rows_ref, bf16[8,512,512]{2,1,0:T(8,128)(2,1)} %bitcast.2.received_ref), custom_call_target="tpu_custom_call" | custom-call | tf_op jit(solution)/shard_map/scatter/pallas_call | solution.py:347
  146.5 6.1 %collective-permute-start.7 = (bf16[4,200,512]{2,1,0:T(8,128)(2,1)S(1)}, bf16[4,200,512]{2,1,0:T(8,128)(2,1)S(1)}, u32[]{:S(2)}, u32[]{:S(2)}) collective-permute-start(bf16[4,200,512]{2,1,0:T(8,128)(2,1)S(1)} %get-tuple-element.22), channel_id=1, source_target_pairs={{0,1},{1,2},{2,3},{3,4},{4,5},{5,6},{6,7},{7,8},{8,9},{9,10},{10,1... | collective-permute-start | bytes 2457608 | tf_op jit(solution)/shard_map/ppermute | solution.py:390
  152.6 1.9 %collective-permute-start.8 = (bf16[4,200,512]{2,1,0:T(8,128)(2,1)S(1)}, bf16[4,200,512]{2,1,0:T(8,128)(2,1)S(1)}, u32[]{:S(2)}, u32[]{:S(2)}) collective-permute-start(bf16[4,200,512]{2,1,0:T(8,128)(2,1)S(1)} %get-tuple-element.23), channel_id=1, source_target_pairs={{1,0},{2,1},{3,2},{4,3},{5,4},{6,5},{7,6},{8,7},{9,8},{10,9},{11,1... | collective-permute-start | bytes 2457608 | tf_op jit(solution)/shard_map/ppermute | solution.py:390
  154.5 1.6 collective-permute-done.10.after_ref
  156.1 2.4 %merge.3 = f32[4,456,512]{2,1,0:T(8,128)} custom-call(f32[4,456,512]{2,1,0:T(8,128)S(1)} %copy-done.1, bf16[4,200,512]{2,1,0:T(8,128)(2,1)S(1)} %collective-permute-done.9.before_ref, bf16[4,200,512]{2,1,0:T(8,128)(2,1)S(1)} %collective-permute-done.10.after_ref), custom_call_target="tpu_custom_call" | custom-call | tf_op jit(solution)/shard_map/merge/pallas_call | solution.py:374
  158.4 13.4 %collective-permute-done.7.before_ref = bf16[4,200,512]{2,1,0:T(8,128)(2,1)S(1)} collective-permute-done((bf16[4,200,512]{2,1,0:T(8,128)(2,1)S(1)}, bf16[4,200,512]{2,1,0:T(8,128)(2,1)S(1)}, u32[]{:S(2)}, u32[]{:S(2)}) %collective-permute-start.7) | collective-permute-done | bytes 819232 | tf_op jit(solution)/shard_map/ppermute | solution.py:390
  171.8 4.6 %collective-permute-done.8.after_ref = bf16[4,200,512]{2,1,0:T(8,128)(2,1)S(1)} collective-permute-done((bf16[4,200,512]{2,1,0:T(8,128)(2,1)S(1)}, bf16[4,200,512]{2,1,0:T(8,128)(2,1)S(1)}, u32[]{:S(2)}, u32[]{:S(2)}) %collective-permute-start.8) | collective-permute-done | bytes 819232 | tf_op jit(solution)/shard_map/ppermute | solution.py:390
  176.4 2.3 %merge.2 = f32[4,456,512]{2,1,0:T(8,128)} custom-call(f32[4,456,512]{2,1,0:T(8,128)S(1)} %get-tuple-element.21.total_ref, bf16[4,200,512]{2,1,0:T(8,128)(2,1)S(1)} %collective-permute-done.7.before_ref, bf16[4,200,512]{2,1,0:T(8,128)(2,1)S(1)} %collective-permute-done.8.after_ref), custom_call_target="tpu_custom_call" | custom-call | tf_op jit(solution)/shard_map/merge/pallas_call | solution.py:374
  (28 shorter events, 3.4 us)
Async XLA Ops:
  3.0 15.3 %all-to-all-start = ((f32[16,24,128]{2,1,0:T(8,128)}), f32[16,24,128]{2,1,0:T(8,128)S(1)}, u32[]{:S(2)}, u32[]{:S(2)}) async-start(f32[16,24,128]{2,1,0:T(8,128)} %get-tuple-element.17), calls=%async_computation | async-start | bytes 393216 | tf_op jit(solution)/shard_map/all_to_all | solution.py:425
  18.4 10.4 %copy-start.3 = (f32[16,24,128]{2,1,0:T(8,128)}, f32[16,24,128]{2,1,0:T(8,128)S(1)}, u32[]{:S(2)}) copy-start(f32[16,24,128]{2,1,0:T(8,128)S(1)} %all-to-all-done.packed_ref) | copy-start | bytes 589828
  18.4 59.7 %all-to-all-start.2 = ((bf16[128,2,16,512]{3,2,1,0:T(8,128)(2,1)}), bf16[128,2,16,512]{3,2,1,0:T(8,128)(2,1)}, u32[]{:S(2)}, u32[]{:S(2)}) async-start(bf16[128,2,16,512]{3,2,1,0:T(8,128)(2,1)} %bitcast.12), calls=%async_computation.2 | async-start | bytes 8388608 | tf_op jit(solution)/shard_map/all_to_all | solution.py:332
  28.9 44.3 %collective-permute-start.6 = (f32[1,32]{1,0:T(1,128)S(1)}, f32[1,32]{1,0:T(1,128)S(1)}, u32[]{:S(2)}, u32[]{:S(2)}) collective-permute-start(f32[1,32]{1,0:T(1,128)S(1)} %concatenate.9), channel_id=1, source_target_pairs={{0,112},{16,0},{32,16},{48,32},{64,48},{80,64},{96,80},{112,96},{1... | collective-permute-start | bytes 392 | tf_op jit(solution)/shard_map/ppermute | solution.py:397
  29.5 43.7 %collective-permute-start.5 = (f32[1,32]{1,0:T(1,128)S(1)}, f32[1,32]{1,0:T(1,128)S(1)}, u32[]{:S(2)}, u32[]{:S(2)}) collective-permute-start(f32[1,32]{1,0:T(1,128)S(1)} %concatenate.9), channel_id=1, source_target_pairs={{0,96},{16,112},{32,0},{48,16},{64,32},{80,48},{96,64},{112,80},{1... | collective-permute-start | bytes 392 | tf_op jit(solution)/shard_map/ppermute | solution.py:397
  30.1 45.4 %collective-permute-start.4 = (f32[1,32]{1,0:T(1,128)S(1)}, f32[1,32]{1,0:T(1,128)S(1)}, u32[]{:S(2)}, u32[]{:S(2)}) collective-permute-start(f32[1,32]{1,0:T(1,128)S(1)} %concatenate.9), channel_id=1, source_target_pairs={{0,80},{16,96},{32,112},{48,0},{64,16},{80,32},{96,48},{112,64},{1... | collective-permute-start | bytes 392 | tf_op jit(solution)/shard_map/ppermute | solution.py:397
  30.7 44.7 %collective-permute-start.3 = (f32[1,32]{1,0:T(1,128)S(1)}, f32[1,32]{1,0:T(1,128)S(1)}, u32[]{:S(2)}, u32[]{:S(2)}) collective-permute-start(f32[1,32]{1,0:T(1,128)S(1)} %concatenate.9), channel_id=1, source_target_pairs={{0,64},{16,80},{32,96},{48,112},{64,0},{80,16},{96,32},{112,48},{1... | collective-permute-start | bytes 392 | tf_op jit(solution)/shard_map/ppermute | solution.py:397
  33.4 42.1 %collective-permute-start.2 = (f32[1,32]{1,0:T(1,128)S(1)}, f32[1,32]{1,0:T(1,128)S(1)}, u32[]{:S(2)}, u32[]{:S(2)}) collective-permute-start(f32[1,32]{1,0:T(1,128)S(1)} %concatenate.9), channel_id=1, source_target_pairs={{0,48},{16,64},{32,80},{48,96},{64,112},{80,0},{96,16},{112,32},{1... | collective-permute-start | bytes 392 | tf_op jit(solution)/shard_map/ppermute | solution.py:397
  73.2 3.5 %collective-permute-start.1 = (f32[1,32]{1,0:T(1,128)S(1)}, f32[1,32]{1,0:T(1,128)S(1)}, u32[]{:S(2)}, u32[]{:S(2)}) collective-permute-start(f32[1,32]{1,0:T(1,128)S(1)} %concatenate.9), channel_id=1, source_target_pairs={{0,32},{16,48},{32,64},{48,80},{64,96},{80,112},{96,0},{112,16},{1... | collective-permute-start | bytes 392 | tf_op jit(solution)/shard_map/ppermute | solution.py:397
  73.2 3.5 %collective-permute-start = (f32[1,32]{1,0:T(1,128)S(1)}, f32[1,32]{1,0:T(1,128)S(1)}, u32[]{:S(2)}, u32[]{:S(2)}) collective-permute-start(f32[1,32]{1,0:T(1,128)S(1)} %concatenate.9), channel_id=1, source_target_pairs={{0,16},{16,32},{32,48},{48,64},{64,80},{80,96},{96,112},{112,0},{1... | collective-permute-start | bytes 392 | tf_op jit(solution)/shard_map/ppermute | solution.py:397
  78.1 10.9 %copy-start.2 = (s32[1,128]{1,0:T(1,128)S(1)}, s32[1,128]{1,0:T(1,128)}, u32[]{:S(2)}) copy-start(s32[1,128]{1,0:T(1,128)} %get-tuple-element.15.table_ref) | copy-start | bytes 1540
  78.1 60.6 %all-to-all-start.1 = ((bf16[128,2,16,512]{3,2,1,0:T(8,128)(2,1)}), bf16[128,2,16,512]{3,2,1,0:T(8,128)(2,1)}, u32[]{:S(2)}, u32[]{:S(2)}) async-start(bf16[128,2,16,512]{3,2,1,0:T(8,128)(2,1)} %bitcast.11), calls=%async_computation.1 | async-start | bytes 8388608 | tf_op jit(solution)/shard_map/all_to_all | solution.py:332
  96.5 1.9 %copy-start = (f32[4,456,512]{2,1,0:T(8,128)}, f32[4,456,512]{2,1,0:T(8,128)S(1)}, u32[]{:S(2)}) copy-start(f32[4,456,512]{2,1,0:T(8,128)S(1)} %get-tuple-element.25.total_ref) | copy-start | bytes 11206660
  98.3 56.2 %collective-permute-start.9 = (bf16[4,200,512]{2,1,0:T(8,128)(2,1)S(1)}, bf16[4,200,512]{2,1,0:T(8,128)(2,1)S(1)}, u32[]{:S(2)}, u32[]{:S(2)}) collective-permute-start(bf16[4,200,512]{2,1,0:T(8,128)(2,1)S(1)} %get-tuple-element.26), channel_id=1, source_target_pairs={{0,1},{1,2},{2,3},{3,4},{4,5},{5,6},{6,7},{7,8},{8,9},{9,10},{10,1... | collective-permute-start | bytes 2457608 | tf_op jit(solution)/shard_map/ppermute | solution.py:390
  101.0 55.1 %collective-permute-start.10 = (bf16[4,200,512]{2,1,0:T(8,128)(2,1)S(1)}, bf16[4,200,512]{2,1,0:T(8,128)(2,1)S(1)}, u32[]{:S(2)}, u32[]{:S(2)}) collective-permute-start(bf16[4,200,512]{2,1,0:T(8,128)(2,1)S(1)} %get-tuple-element.27), channel_id=1, source_target_pairs={{1,0},{2,1},{3,2},{4,3},{5,4},{6,5},{7,6},{8,7},{9,8},{10,9},{11,1... | collective-permute-start | bytes 2457608 | tf_op jit(solution)/shard_map/ppermute | solution.py:390
  138.7 17.3 %copy-start.1 = (f32[4,456,512]{2,1,0:T(8,128)S(1)}, f32[4,456,512]{2,1,0:T(8,128)}, u32[]{:S(2)}) copy-start(f32[4,456,512]{2,1,0:T(8,128)} %copy-done) | copy-start | bytes 11206660
  146.5 25.4 %collective-permute-start.7 = (bf16[4,200,512]{2,1,0:T(8,128)(2,1)S(1)}, bf16[4,200,512]{2,1,0:T(8,128)(2,1)S(1)}, u32[]{:S(2)}, u32[]{:S(2)}) collective-permute-start(bf16[4,200,512]{2,1,0:T(8,128)(2,1)S(1)} %get-tuple-element.22), channel_id=1, source_target_pairs={{0,1},{1,2},{2,3},{3,4},{4,5},{5,6},{6,7},{7,8},{8,9},{9,10},{10,1... | collective-permute-start | bytes 2457608 | tf_op jit(solution)/shard_map/ppermute | solution.py:390
  152.6 23.8 %collective-permute-start.8 = (bf16[4,200,512]{2,1,0:T(8,128)(2,1)S(1)}, bf16[4,200,512]{2,1,0:T(8,128)(2,1)S(1)}, u32[]{:S(2)}, u32[]{:S(2)}) collective-permute-start(bf16[4,200,512]{2,1,0:T(8,128)(2,1)S(1)} %get-tuple-element.23), channel_id=1, source_target_pairs={{1,0},{2,1},{3,2},{4,3},{5,4},{6,5},{7,6},{8,7},{9,8},{10,9},{11,1... | collective-permute-start | bytes 2457608 | tf_op jit(solution)/shard_map/ppermute | solution.py:390

commit v4 on v3

--- a/solution.py
+++ b/solution.py
@@ -23,6 +23,7 @@
 BIN_PIX = ROW_PIX // BINS
 PATCHES = 16
 VISITS = 8
+TURNS = VISITS // BANDS
 GROUPS = 16
 GRID_ROWS = 16
 PACKED = GRID_ROWS + 8
@@ -33,13 +34,14 @@
 AT_VISIT = 49
 AT_ORDER = 56
 SPAN = ROW_PIX // VISITS
-CHUNKS = 1
-LIM = 60
+PER = 4
+HALVES = 2
 BLOCK = 256
 PAD = 128
 WINDOW = BLOCK + 2 * PAD
 UNUSED = 1 << 20
-WIDTH = SPAN // CHUNKS
+STEPS = VISITS // PER
+WIDTH = SPAN * PER
 
 
 def fill_band(table_ref, psf_ref, band_ref, absolute):
@@ -81,22 +83,20 @@
     good_ref[...] = good.astype(jnp.float32)
 
 
-def convolve(window, band_ref, width):
+def convolve(window, band_ref, span):
     parts = [
         jnp.dot(
-            window[:, BLOCK * n : BLOCK * n + WINDOW],
-            band_ref[...],
-            preferred_element_type=jnp.float32,
+            window[:, start : start + WINDOW], band_ref[...], preferred_element_type=jnp.float32
         )
-        for n in range(width // BLOCK)
+        for start in range(span * SPAN, (span + 1) * SPAN, BLOCK)
     ]
-    return parts[0] if len(parts) == 1 else jnp.concatenate(parts, axis=1)
-
-
-def send_pieces(table_ref, out_ref, values):
-    out_ref[...] = jnp.zeros(out_ref.shape, out_ref.dtype)
+    return jnp.concatenate(parts, axis=1)
+
+
+def send_pieces(table_ref, out_ref, span, values):
+    out_ref[span] = jnp.zeros(out_ref.shape[1:], out_ref.dtype)
     for j in range(PIECES):
-        out_ref[0, table_ref[0, AT_SLOT + j]] = values[PIECE_ROWS * j : PIECE_ROWS * (j + 1)]
+        out_ref[span, table_ref[0, AT_SLOT + j]] = values[PIECE_ROWS * j : PIECE_ROWS * (j + 1)]
 
 
 def pack_body(
@@ -128,7 +128,7 @@
     table = jnp.where(lane == AT_VISIT, lax.axis_index("visit"), table)
     bands = [band_ref[v] for v in range(VISITS)]
     for v in range(VISITS):
-        place = bands[v] * (VISITS // BANDS)
+        place = bands[v] * TURNS
         for u in range(v):
             place = place + (bands[u] == bands[v]).astype(jnp.int32)
         table = jnp.where(lane == AT_ORDER + place, v, table)
@@ -139,16 +139,14 @@
     taps_ref[...] = taps
 
 
-def masked_window(chunk, good_ref, left_ref, mid_ref, right_ref):
-    width = mid_ref.shape[-1]
-    start = pl.multiple_of(pl.program_id(0) * SPAN + chunk * width, 128)
-    good = good_ref[:, pl.ds(start, width + 2 * PAD)]
+def masked_window(good_ref, left_ref, mid_ref, right_ref):
+    start = pl.multiple_of(pl.program_id(0) * WIDTH, 128)
+    good = good_ref[:, pl.ds(start, WIDTH + 2 * PAD)]
     window = jnp.concatenate([left_ref[0], mid_ref[0], right_ref[0]], axis=1)
     return start, good, window * good.astype(jnp.bfloat16)
 
 
 def weight_body(
-    chunk,
     table_ref,
     psf_ref,
     left_ref,
@@ -164,14 +162,14 @@
         fill_good(table_ref, good_ref)
         fill_band(table_ref, psf_ref, band_ref, True)
 
-    _, _, window = masked_window(chunk, good_ref, left_ref, mid_ref, right_ref)
-    weight = convolve(window, band_ref, mid_ref.shape[-1]).astype(jnp.bfloat16)
-    weight_ref[0] = weight
-    send_pieces(table_ref, send_ref, weight)
+    _, _, window = masked_window(good_ref, left_ref, mid_ref, right_ref)
+    for span in range(PER):
+        weight = convolve(window, band_ref, span).astype(jnp.bfloat16)
+        weight_ref[span] = weight
+        send_pieces(table_ref, send_ref, span, weight)
 
 
 def flux_body(
-    chunk,
     table_ref,
     psf_ref,
     left_ref,
@@ -195,44 +193,39 @@
         model_ref[:GRID_ROWS] = upper
         model_ref[GRID_ROWS:] = (model - upper.astype(jnp.float32)).astype(jnp.bfloat16)
 
-    width = mid_ref.shape[-1]
-    start, good, window = masked_window(chunk, good_ref, left_ref, mid_ref, right_ref)
-    shape = (BINS, width + 2 * PAD)
+    start, good, window = masked_window(good_ref, left_ref, mid_ref, right_ref)
+    shape = (BINS, WIDTH + 2 * PAD)
     first = lax.broadcasted_iota(jnp.int32, shape, 0) * BIN_PIX
     column = lax.broadcasted_iota(jnp.int32, shape, 1) + (start - PAD)
     spread = ((column >= first) & (column < first + BIN_PIX)).astype(jnp.bfloat16)
     expanded = jnp.dot(model_ref[...], spread, preferred_element_type=jnp.float32) * good
-    warped = convolve(
-        jnp.concatenate([window, expanded.astype(jnp.bfloat16)], axis=0), band_ref, width
-    )
-    backdrop = warped[CCD_ROWS : CCD_ROWS + GRID_ROWS] + warped[CCD_ROWS + GRID_ROWS :]
-    backdrop = jnp.broadcast_to(
-        backdrop[:, None, :], (GRID_ROWS, CCD_ROWS // GRID_ROWS, width)
-    ).reshape(CCD_ROWS, width)
-    flux = warped[:CCD_ROWS] - backdrop
-    send_pieces(
-        table_ref, send_ref, (flux * weight_ref[0].astype(jnp.float32)).astype(jnp.bfloat16)
-    )
-
-
-def scatter_body(table_ref, rows_ref, received_ref, total_ref, low_ref, high_ref):
-    turn = pl.program_id(1)
+    window = jnp.concatenate([window, expanded.astype(jnp.bfloat16)], axis=0)
+    for span in range(PER):
+        warped = convolve(window, band_ref, span)
+        backdrop = warped[CCD_ROWS : CCD_ROWS + GRID_ROWS] + warped[CCD_ROWS + GRID_ROWS :]
+        backdrop = jnp.broadcast_to(
+            backdrop[:, None, :], (GRID_ROWS, CCD_ROWS // GRID_ROWS, SPAN)
+        ).reshape(CCD_ROWS, SPAN)
+        flux = warped[:CCD_ROWS] - backdrop
+        product = flux * weight_ref[span].astype(jnp.float32)
+        send_pieces(table_ref, send_ref, span, product.astype(jnp.bfloat16))
+
+
+def scatter_body(half, table_ref, rows_ref, *refs):
+    received_refs, (total_ref, low_ref, high_ref) = refs[:TURNS], refs[TURNS:]
     slots = rows_ref.shape[-1]
-    place = lax.broadcasted_iota(jnp.int32, (FRAME, slots), 0) == rows_ref[0]
-    frames = jnp.dot(
-        place.astype(jnp.bfloat16), received_ref[0], preferred_element_type=jnp.float32
-    )
-
-    @pl.when(turn == 0)
-    def _():
-        total_ref[0] = frames
-
-    @pl.when(turn == 1)
-    def _():
-        total = total_ref[0] + frames
-        total_ref[0] = total
-        low_ref[0] = total[:EDGE].astype(jnp.bfloat16)
-        high_ref[0] = total[FRAME - EDGE :].astype(jnp.bfloat16)
+    total = None
+    for turn, received_ref in enumerate(received_refs):
+        visit = table_ref[0, AT_ORDER + TURNS * (half + pl.program_id(0)) + turn]
+        rows = rows_ref[(table_ref[0, AT_VISIT] - visit) & (VISITS - 1)]
+        place = lax.broadcasted_iota(jnp.int32, (FRAME, slots), 0) == rows
+        frames = jnp.dot(
+            place.astype(jnp.bfloat16), received_ref[0], preferred_element_type=jnp.float32
+        )
+        total = total + frames if turn else frames
+    total_ref[0] = total
+    low_ref[0] = total[:EDGE].astype(jnp.bfloat16)
+    high_ref[0] = total[FRAME - EDGE :].astype(jnp.bfloat16)
 
 
 def merge_body(total_ref, before_ref, after_ref, *refs):
@@ -257,41 +250,34 @@
     )
 
 
-def window_specs(chunk):
-    per = SPAN // WIDTH
+def window_specs():
     tiles = WIDTH // 128
     last = ROW_PIX // 128 - 1
-    left = pl.BlockSpec(
-        (1, CCD_ROWS, 128),
-        lambda i, *_: (0, 0, jnp.maximum((per * i + chunk) * tiles - 1, 0)),
-    )
-    mid = pl.BlockSpec((1, CCD_ROWS, WIDTH), lambda i, *_: (0, 0, per * i + chunk))
-    right = pl.BlockSpec(
-        (1, CCD_ROWS, 128),
-        lambda i, *_: (0, 0, jnp.minimum((per * i + chunk + 1) * tiles, last)),
-    )
+    left = pl.BlockSpec((1, CCD_ROWS, 128), lambda i: (0, 0, jnp.maximum(i * tiles - 1, 0)))
+    mid = pl.BlockSpec((1, CCD_ROWS, WIDTH), lambda i: (0, 0, i))
+    right = pl.BlockSpec((1, CCD_ROWS, 128), lambda i: (0, 0, jnp.minimum((i + 1) * tiles, last)))
     return [left, mid, right]
 
 
-SEND_SHAPE = (VISITS, PATCHES * MOST, PIECE_ROWS, WIDTH)
-SEND_BLOCK = pl.BlockSpec((1,) + SEND_SHAPE[1:], lambda i, *_: (i, 0, 0, 0))
-WEIGHT_BLOCK = pl.BlockSpec((1, CCD_ROWS, WIDTH), lambda i, *_: (i, 0, 0))
+SEND_SHAPE = (VISITS, PATCHES * MOST, PIECE_ROWS, SPAN)
+SEND_BLOCK = pl.BlockSpec((PER,) + SEND_SHAPE[1:], lambda i: (i, 0, 0, 0))
+WEIGHT_BLOCK = pl.BlockSpec((PER, CCD_ROWS, SPAN), lambda i: (i, 0, 0))
 GOOD_SCRATCH = pltpu.VMEM((1, ROW_PIX + 2 * PAD), jnp.float32)
 BAND_SCRATCH = pltpu.VMEM((WINDOW, BLOCK), jnp.bfloat16)
 
 
-def send_weight(chunk, table, psf, inv_var):
+def send_weight(table, psf, inv_var):
     return pl.pallas_call(
-        functools.partial(weight_body, chunk),
-        grid=(VISITS,),
-        in_specs=[SMEM] * 2 + window_specs(chunk),
+        weight_body,
+        grid=(STEPS,),
+        in_specs=[SMEM] * 2 + window_specs(),
         out_specs=[SEND_BLOCK, WEIGHT_BLOCK],
         out_shape=[
             jax.ShapeDtypeStruct(SEND_SHAPE, jnp.bfloat16),
-            jax.ShapeDtypeStruct((VISITS, CCD_ROWS, WIDTH), jnp.bfloat16),
+            jax.ShapeDtypeStruct((VISITS, CCD_ROWS, SPAN), jnp.bfloat16),
         ],
         scratch_shapes=[GOOD_SCRATCH, BAND_SCRATCH],
-        compiler_params=params(LIM),
+        compiler_params=params(60),
         name="send_weight",
     )(table, psf, inv_var, inv_var, inv_var)
 
@@ -310,11 +296,11 @@
     )(*smalls)
 
 
-def send_flux(chunk, table, psf, image, packed, weight):
+def send_flux(table, psf, image, packed, weight):
     return pl.pallas_call(
-        functools.partial(flux_body, chunk),
-        grid=(VISITS,),
-        in_specs=[SMEM] * 2 + window_specs(chunk) + [whole(packed.shape), WEIGHT_BLOCK],
+        flux_body,
+        grid=(STEPS,),
+        in_specs=[SMEM] * 2 + window_specs() + [whole(packed.shape), WEIGHT_BLOCK],
         out_specs=SEND_BLOCK,
         out_shape=jax.ShapeDtypeStruct(SEND_SHAPE, jnp.bfloat16),
         scratch_shapes=[
@@ -322,60 +308,58 @@
             BAND_SCRATCH,
             pltpu.VMEM((2 * GRID_ROWS, BINS), jnp.bfloat16),
         ],
-        compiler_params=params(LIM),
+        compiler_params=params(60),
         name="send_flux",
     )(table, psf, image, image, image, packed, weight)
 
 
 def exchange(pieces):
-    sent = pieces.reshape(VISITS * PATCHES, MOST, PIECE_ROWS, WIDTH)
+    sent = pieces.reshape(VISITS * PATCHES, MOST, PIECE_ROWS, SPAN)
     return lax.all_to_all(sent, ("visit", "fp"), split_axis=0, concat_axis=0, tiled=True)
 
 
-def scatter(table, dest_rows, received):
+def scatter(half, table, dest_rows, received):
     slots = PATCHES * MOST * PIECE_ROWS
+    bands = BANDS // HALVES
     shapes = [
-        jax.ShapeDtypeStruct((BANDS, FRAME, WIDTH), jnp.float32),
-        jax.ShapeDtypeStruct((BANDS, EDGE, WIDTH), jnp.bfloat16),
-        jax.ShapeDtypeStruct((BANDS, EDGE, WIDTH), jnp.bfloat16),
+        jax.ShapeDtypeStruct((bands, FRAME, SPAN), jnp.float32),
+        jax.ShapeDtypeStruct((bands, EDGE, SPAN), jnp.bfloat16),
+        jax.ShapeDtypeStruct((bands, EDGE, SPAN), jnp.bfloat16),
     ]
-    turns = VISITS // BANDS
-
-    def visit(b, j, at):
-        return at[0, AT_ORDER + turns * b + j]
-
+
+    def received_spec(turn):
+        return pl.BlockSpec(
+            (1, slots, SPAN),
+            lambda i, at: (at[0, AT_ORDER + TURNS * (bands * half + i) + turn], 0, 0),
+        )
+
+    received = received.reshape(VISITS, slots, SPAN)
     return pl.pallas_call(
-        scatter_body,
+        functools.partial(scatter_body, bands * half),
         grid_spec=pltpu.PrefetchScalarGridSpec(
             num_scalar_prefetch=1,
-            grid=(BANDS, turns),
-            in_specs=[
-                pl.BlockSpec(
-                    (1, 1, slots),
-                    lambda b, j, at: ((at[0, AT_VISIT] - visit(b, j, at)) & (VISITS - 1), 0, 0),
-                ),
-                pl.BlockSpec((1, slots, WIDTH), lambda b, j, at: (visit(b, j, at), 0, 0)),
-            ],
+            grid=(bands,),
+            in_specs=[pl.BlockSpec((VISITS, 1, slots), lambda i, at: (0, 0, 0))]
+            + [received_spec(turn) for turn in range(TURNS)],
             out_specs=[
-                pl.BlockSpec((1,) + shape.shape[1:], lambda b, j, at: (b, 0, 0)) for shape in shapes
+                pl.BlockSpec((1,) + shape.shape[1:], lambda i, at: (i, 0, 0)) for shape in shapes
             ],
         ),
         out_shape=shapes,
-        compiler_params=pltpu.CompilerParams(
-            dimension_semantics=("arbitrary", "arbitrary"), vmem_limit_bytes=16 << 20
-        ),
+        compiler_params=params(16),
         name="scatter",
-    )(table, dest_rows, received.reshape(VISITS, slots, WIDTH))
-
-
-def merge(chunk, total, before, after, earlier):
-    edge = pl.BlockSpec((1, EDGE, WIDTH), lambda i: (i, 0, 0))
-    frame = pl.BlockSpec((1, FRAME, WIDTH), lambda i: (i, 0, 0))
+    )(table, dest_rows, *[received] * TURNS)
+
+
+def merge(half, total, before, after, earlier):
+    bands = BANDS // HALVES
+    edge = pl.BlockSpec((1, EDGE, SPAN), lambda i: (i, 0, 0))
+    frame = pl.BlockSpec((1, FRAME, SPAN), lambda i: (i, 0, 0))
     return pl.pallas_call(
         merge_body,
-        grid=(BANDS,),
+        grid=(bands,),
         in_specs=[frame, edge, edge] + [pl.BlockSpec(memory_space=pl.ANY)] * len(earlier),
-        out_specs=pl.BlockSpec((1, FRAME, WIDTH), lambda i: (i, 0, chunk)),
+        out_specs=pl.BlockSpec((1, FRAME, SPAN), lambda i: (bands * half + i, 0, 0)),
         out_shape=jax.ShapeDtypeStruct((BANDS, FRAME, SPAN), jnp.float32),
         input_output_aliases={3: 0} if earlier else {},
         compiler_params=params(16),
@@ -423,22 +407,20 @@
         bg_grid,
     )
     packed = lax.all_to_all(packed, "fp", split_axis=0, concat_axis=0, tiled=True)
-    chunks = range(SPAN // WIDTH)
-    weights, arrived = [], []
-    for chunk in chunks:
-        pieces, weight = send_weight(chunk, table, psf, inv_var)
-        weights.append(weight)
-        arrived.append(exchange(pieces))
-    fluxes = [send_flux(chunk, table, psf, image, packed, weights[chunk]) for chunk in chunks]
+    weight_pieces, weight = send_weight(table, psf, inv_var)
+    weight_arrived = exchange(weight_pieces)
+    flux_pieces = send_flux(table, psf, image, packed, weight)
     dest_rows = slot_rows(packed[:, GRID_ROWS, :MOST])
-    fluxes, dest_rows = lax.optimization_barrier((fluxes, dest_rows))
-    arrived += [exchange(pieces) for pieces in fluxes]
-    outs = [[], []]
-    for turn, received in enumerate(arrived):
-        total, low, high = scatter(table, dest_rows, received)
-        kind, chunk = divmod(turn, len(chunks))
-        outs[kind] = [merge(chunk, total, *swap_borders(low, high), outs[kind])]
-    return (outs[1][0][:, None], outs[0][0][:, None])
+    flux_pieces, dest_rows = lax.optimization_barrier((flux_pieces, dest_rows))
+    flux_arrived = exchange(flux_pieces)
+    outs = []
+    for received in (weight_arrived, flux_arrived):
+        out = []
+        for half in range(HALVES):
+            total, low, high = scatter(half, table, dest_rows, received)
+            out = [merge(half, total, *swap_borders(low, high), out)]
+        outs.append(out[0])
+    return (outs[1][:, None], outs[0][:, None])
 
 
 def solution(mesh):

time: 180 us -> 175 us (0.972)
  the two profiles are of different devices: /device:TPU:102 before, /device:TPU:14 now
where the time goes in v4:
time: 175 us; the launch traced here: 174 us
  waiting for transfers between devices  73.4 us (42%)
  starting transfers between devices  66 us (38%)
  Pallas kernels  32.8 us (19%)
    all_to_all x2, waiting for transfers between devices, exchange(): lax.all_to_all(sent, ('visit', 'fp'), split_axis=0, concat_axis=0, tiled=...  33 us
    ppermute x7, waiting for transfers between devices, slot_rows(): lax.ppermute(first, 'visit', [(i, (i + k) % VISITS) for i in range(VISITS)])  32.3 us
    ppermute x8, starting transfers between devices, swap_borders(): return (lax.ppermute(high, 'fp', up), lax.ppermute(low, 'fp', down))  31.8 us
    all_to_all x2, starting transfers between devices, exchange(): lax.all_to_all(sent, ('visit', 'fp'), split_axis=0, concat_axis=0, tiled=...  16.9 us
    pallas_call x4, Pallas kernels, scatter(): pl.pallas_call(functools.partial(scatter_body, bands * half), grid_spec=p...  13.9 us
    ppermute x7, starting transfers between devices, slot_rows(): lax.ppermute(first, 'visit', [(i, (i + k) % VISITS) for i in range(VISITS)])  8.83 us
    all_to_all x1, starting transfers between devices, shards(): lax.all_to_all(packed, 'fp', split_axis=0, concat_axis=0, tiled=True)  8.41 us
    ppermute x8, waiting for transfers between devices, swap_borders(): return (lax.ppermute(high, 'fp', up), lax.ppermute(low, 'fp', down))  6.77 us
  transfers between devices with their start and end apart: 18, of which 6 were waited for; matrix products, arithmetic and copies ran while one was open for 0% of the time, Pallas kernels for 17%

profile of v4, /device:TPU:14, one launch (start us, length us, event | category | flops | bytes accessed | tf_op | source)
XLA Modules:
  0.0 174.1 jit_solution(18416110051034816617)
XLA Ops:
  3.0 8.4 %all-to-all-start = ((f32[16,24,128]{2,1,0:T(8,128)}), f32[16,24,128]{2,1,0:T(8,128)S(1)}, u32[]{:S(2)}, u32[]{:S(2)}) async-start(f32[16,24,128]{2,1,0:T(8,128)} %get-tuple-element.23), calls=%async_computation | async-start | bytes 393216 | tf_op jit(solution)/shard_map/all_to_all | solution.py:409
  11.5 5.2 %send_weight.1 = (bf16[8,32,16,512]{3,2,1,0:T(8,128)(2,1)}, bf16[8,256,512]{2,1,0:T(8,128)(2,1)}) custom-call(s32[1,128]{1,0:T(1,128)} %get-tuple-element.21.table_ref, f32[1,128]{1,0:T(1,128)} %get-tuple-element.22.psf_ref, bf16[1,256,4096]{2,1,0:T(8,128)(2,1)} %right_ref.2, bf16[1,256,4096]{2,1,0:T(8,128)(2,1)} %right_ref.2, bf16[1,256,4096]{2,1,0:T(8,128)(2,1)} %right_ref.2), custom_call_target="tpu_custom_call" | custom-call | tf_op jit(solution)/shard_map/send_weight/pallas_call | solution.py:270
  18.0 8.3 %all-to-all-start.2 = ((bf16[128,2,16,512]{3,2,1,0:T(8,128)(2,1)}), bf16[128,2,16,512]{3,2,1,0:T(8,128)(2,1)}, u32[]{:S(2)}, u32[]{:S(2)}) async-start(bf16[128,2,16,512]{3,2,1,0:T(8,128)(2,1)} %bitcast.14), calls=%async_computation.2 | async-start | bytes 8388608 | tf_op jit(solution)/shard_map/all_to_all | solution.py:318
  28.5 2.6 %collective-permute-start.3 = (f32[1,32]{1,0:T(1,128)S(1)}, f32[1,32]{1,0:T(1,128)S(1)}, u32[]{:S(2)}, u32[]{:S(2)}) collective-permute-start(f32[1,32]{1,0:T(1,128)S(1)} %concatenate.9), channel_id=1, source_target_pairs={{0,64},{16,80},{32,96},{48,112},{64,0},{80,16},{96,32},{112,48},{1... | collective-permute-start | bytes 392 | tf_op jit(solution)/shard_map/ppermute | solution.py:381
  31.1 2.1 %collective-permute-start.2 = (f32[1,32]{1,0:T(1,128)S(1)}, f32[1,32]{1,0:T(1,128)S(1)}, u32[]{:S(2)}, u32[]{:S(2)}) collective-permute-start(f32[1,32]{1,0:T(1,128)S(1)} %concatenate.9), channel_id=1, source_target_pairs={{0,48},{16,64},{32,80},{48,96},{64,112},{80,0},{96,16},{112,32},{1... | collective-permute-start | bytes 392 | tf_op jit(solution)/shard_map/ppermute | solution.py:381
  33.1 6.7 %send_flux.1 = bf16[8,32,16,512]{3,2,1,0:T(8,128)(2,1)} custom-call(s32[1,128]{1,0:T(1,128)} %get-tuple-element.21.table_ref, f32[1,128]{1,0:T(1,128)} %get-tuple-element.22.psf_ref, bf16[1,256,4096]{2,1,0:T(8,128)(2,1)} %right_ref.3, bf16[1,256,4096]{2,1,0:T(8,128)(2,1)} %right_ref.3, bf16[1,256,4096]{2,1,0:T(8,128)(2,1)} %right_ref.3, ...), custom_call_target="tpu_custom_call" | custom-call | tf_op jit(solution)/shard_map/send_flux/pallas_call | solution.py:300
  39.8 31.1 %collective-permute-done.6 = f32[1,32]{1,0:T(1,128)S(1)} collective-permute-done((f32[1,32]{1,0:T(1,128)S(1)}, f32[1,32]{1,0:T(1,128)S(1)}, u32[]{:S(2)}, u32[]{:S(2)}) %collective-permute-start.6) | collective-permute-done | bytes 160 | tf_op jit(solution)/shard_map/ppermute | solution.py:381
  70.9 2.3 %collective-permute-start = (f32[1,32]{1,0:T(1,128)S(1)}, f32[1,32]{1,0:T(1,128)S(1)}, u32[]{:S(2)}, u32[]{:S(2)}) collective-permute-start(f32[1,32]{1,0:T(1,128)S(1)} %concatenate.9), channel_id=1, source_target_pairs={{0,16},{16,32},{32,48},{48,64},{64,80},{80,96},{96,112},{112,0},{1... | collective-permute-start | bytes 392 | tf_op jit(solution)/shard_map/ppermute | solution.py:381
  74.7 3.3 %all-to-all-done.2 = bf16[128,2,16,512]{3,2,1,0:T(8,128)(2,1)} async-done(((bf16[128,2,16,512]{3,2,1,0:T(8,128)(2,1)}), bf16[128,2,16,512]{3,2,1,0:T(8,128)(2,1)}, u32[]{:S(2)}, u32[]{:S(2)}) %all-to-all-start.2) | async-done | bytes 4194336 | tf_op jit(solution)/shard_map/all_to_all | solution.py:318
  78.0 8.6 %all-to-all-start.1 = ((bf16[128,2,16,512]{3,2,1,0:T(8,128)(2,1)}), bf16[128,2,16,512]{3,2,1,0:T(8,128)(2,1)}, u32[]{:S(2)}, u32[]{:S(2)}) async-start(bf16[128,2,16,512]{3,2,1,0:T(8,128)(2,1)} %bitcast.11), calls=%async_computation.1 | async-start | bytes 8388608 | tf_op jit(solution)/shard_map/all_to_all | solution.py:318
  86.7 3.8 %scatter.7 = (f32[2,456,512]{2,1,0:T(8,128)S(1)}, bf16[2,200,512]{2,1,0:T(8,128)(2,1)}, bf16[2,200,512]{2,1,0:T(8,128)(2,1)}) custom-call(s32[1,128]{1,0:T(1,128)S(1)} %copy-done.2, s32[8,1,512]{2,1,0:T(1,128)S(1)} %broadcast_add_fusion.rows_ref, bf16[8,512,512]{2,1,0:T(8,128)(2,1)} %bitcast.6.refs_0_.refs_1_, bf16[8,512,512]{2,1,0:T(8,128)(2,1)} %bitcast.6.refs_0_.refs_1_), custom_call_target="tpu_custom_call" | custom-call | tf_op jit(solution)/shard_map/scatter/pallas_call | solution.py:337
  90.5 3.6 %collective-permute-start.13 = (bf16[2,200,512]{2,1,0:T(8,128)(2,1)}, bf16[2,200,512]{2,1,0:T(8,128)(2,1)S(1)}, u32[]{:S(2)}, u32[]{:S(2)}) collective-permute-start(bf16[2,200,512]{2,1,0:T(8,128)(2,1)} %get-tuple-element.38), channel_id=1, source_target_pairs={{0,1},{1,2},{2,3},{3,4},{4,5},{5,6},{6,7},{7,8},{8,9},{9,10},{10,1... | collective-permute-start | bytes 1228808 | tf_op jit(solution)/shard_map/ppermute | solution.py:374
  94.1 4.3 %collective-permute-start.14 = (bf16[2,200,512]{2,1,0:T(8,128)(2,1)}, bf16[2,200,512]{2,1,0:T(8,128)(2,1)S(1)}, u32[]{:S(2)}, u32[]{:S(2)}) collective-permute-start(bf16[2,200,512]{2,1,0:T(8,128)(2,1)} %get-tuple-element.39), channel_id=1, source_target_pairs={{1,0},{2,1},{3,2},{4,3},{5,4},{6,5},{7,6},{8,7},{9,8},{10,9},{11,1... | collective-permute-start | bytes 1228808 | tf_op jit(solution)/shard_map/ppermute | solution.py:374
  98.4 3.8 %scatter.6 = (f32[2,456,512]{2,1,0:T(8,128)S(1)}, bf16[2,200,512]{2,1,0:T(8,128)(2,1)}, bf16[2,200,512]{2,1,0:T(8,128)(2,1)}) custom-call(s32[1,128]{1,0:T(1,128)S(1)} %copy-done.2, s32[8,1,512]{2,1,0:T(1,128)S(1)} %broadcast_add_fusion.rows_ref, bf16[8,512,512]{2,1,0:T(8,128)(2,1)} %bitcast.6.refs_0_.refs_1_, bf16[8,512,512]{2,1,0:T(8,128)(2,1)} %bitcast.6.refs_0_.refs_1_), custom_call_target="tpu_custom_call" | custom-call | tf_op jit(solution)/shard_map/scatter/pallas_call | solution.py:337
  102.3 1.9 %collective-permute-start.11 = (bf16[2,200,512]{2,1,0:T(8,128)(2,1)}, bf16[2,200,512]{2,1,0:T(8,128)(2,1)S(1)}, u32[]{:S(2)}, u32[]{:S(2)}) collective-permute-start(bf16[2,200,512]{2,1,0:T(8,128)(2,1)} %get-tuple-element.35), channel_id=1, source_target_pairs={{0,1},{1,2},{2,3},{3,4},{4,5},{5,6},{6,7},{7,8},{8,9},{9,10},{10,1... | collective-permute-start | bytes 1228808 | tf_op jit(solution)/shard_map/ppermute | solution.py:374
  104.2 6.0 %collective-permute-start.12 = (bf16[2,200,512]{2,1,0:T(8,128)(2,1)}, bf16[2,200,512]{2,1,0:T(8,128)(2,1)S(1)}, u32[]{:S(2)}, u32[]{:S(2)}) collective-permute-start(bf16[2,200,512]{2,1,0:T(8,128)(2,1)} %get-tuple-element.36), channel_id=1, source_target_pairs={{1,0},{2,1},{3,2},{4,3},{5,4},{6,5},{7,6},{8,7},{9,8},{10,9},{11,1... | collective-permute-start | bytes 1228808 | tf_op jit(solution)/shard_map/ppermute | solution.py:374
  110.2 29.6 %all-to-all-done.1 = bf16[128,2,16,512]{3,2,1,0:T(8,128)(2,1)} async-done(((bf16[128,2,16,512]{3,2,1,0:T(8,128)(2,1)}), bf16[128,2,16,512]{3,2,1,0:T(8,128)(2,1)}, u32[]{:S(2)}, u32[]{:S(2)}) %all-to-all-start.1) | async-done | bytes 4194336 | tf_op jit(solution)/shard_map/all_to_all | solution.py:318
  139.8 3.1 %scatter.5 = (f32[2,456,512]{2,1,0:T(8,128)S(1)}, bf16[2,200,512]{2,1,0:T(8,128)(2,1)S(1)}, bf16[2,200,512]{2,1,0:T(8,128)(2,1)S(1)}) custom-call(s32[1,128]{1,0:T(1,128)S(1)} %copy-done.2, s32[8,1,512]{2,1,0:T(1,128)S(1)} %broadcast_add_fusion.rows_ref, bf16[8,512,512]{2,1,0:T(8,128)(2,1)} %bitcast.2.refs_0_.refs_1_, ...), custom_call_target="tpu_custom_call" | custom-call | tf_op jit(solution)/shard_map/scatter/pallas_call | solution.py:337
  143.0 3.1 %scatter.4 = (f32[2,456,512]{2,1,0:T(8,128)S(1)}, bf16[2,200,512]{2,1,0:T(8,128)(2,1)S(1)}, bf16[2,200,512]{2,1,0:T(8,128)(2,1)S(1)}) custom-call(s32[1,128]{1,0:T(1,128)S(1)} %copy-done.2, s32[8,1,512]{2,1,0:T(1,128)S(1)} %broadcast_add_fusion.rows_ref, bf16[8,512,512]{2,1,0:T(8,128)(2,1)} %bitcast.2.refs_0_.refs_1_, ...), custom_call_target="tpu_custom_call" | custom-call | tf_op jit(solution)/shard_map/scatter/pallas_call | solution.py:337
  146.1 1.9 %collective-permute-start.9 = (bf16[2,200,512]{2,1,0:T(8,128)(2,1)S(1)}, bf16[2,200,512]{2,1,0:T(8,128)(2,1)S(1)}, u32[]{:S(2)}, u32[]{:S(2)}) collective-permute-start(bf16[2,200,512]{2,1,0:T(8,128)(2,1)S(1)} %get-tuple-element.31), channel_id=1, source_target_pairs={{0,1},{1,2},{2,3},{3,4},{4,5},{5,6},{6,7},{7,8},{8,9},{9,10},{10,1... | collective-permute-start | bytes 1228808 | tf_op jit(solution)/shard_map/ppermute | solution.py:374
  148.0 6.0 %collective-permute-start.10 = (bf16[2,200,512]{2,1,0:T(8,128)(2,1)S(1)}, bf16[2,200,512]{2,1,0:T(8,128)(2,1)S(1)}, u32[]{:S(2)}, u32[]{:S(2)}) collective-permute-start(bf16[2,200,512]{2,1,0:T(8,128)(2,1)S(1)} %get-tuple-element.32), channel_id=1, source_target_pairs={{1,0},{2,1},{3,2},{4,3},{5,4},{6,5},{7,6},{8,7},{9,8},{10,9},{11,1... | collective-permute-start | bytes 1228808 | tf_op jit(solution)/shard_map/ppermute | solution.py:374
  154.1 1.9 %collective-permute-start.7 = (bf16[2,200,512]{2,1,0:T(8,128)(2,1)S(1)}, bf16[2,200,512]{2,1,0:T(8,128)(2,1)S(1)}, u32[]{:S(2)}, u32[]{:S(2)}) collective-permute-start(bf16[2,200,512]{2,1,0:T(8,128)(2,1)S(1)} %get-tuple-element.28), channel_id=1, source_target_pairs={{0,1},{1,2},{2,3},{3,4},{4,5},{5,6},{6,7},{7,8},{8,9},{9,10},{10,1... | collective-permute-start | bytes 1228808 | tf_op jit(solution)/shard_map/ppermute | solution.py:374
  156.0 6.0 %collective-permute-start.8 = (bf16[2,200,512]{2,1,0:T(8,128)(2,1)S(1)}, bf16[2,200,512]{2,1,0:T(8,128)(2,1)S(1)}, u32[]{:S(2)}, u32[]{:S(2)}) collective-permute-start(bf16[2,200,512]{2,1,0:T(8,128)(2,1)S(1)} %get-tuple-element.29), channel_id=1, source_target_pairs={{1,0},{2,1},{3,2},{4,3},{5,4},{6,5},{7,6},{8,7},{9,8},{10,9},{11,1... | collective-permute-start | bytes 1228808 | tf_op jit(solution)/shard_map/ppermute | solution.py:374
  166.1 6.7 %collective-permute-done.7.before_ref = bf16[2,200,512]{2,1,0:T(8,128)(2,1)S(1)} collective-permute-done((bf16[2,200,512]{2,1,0:T(8,128)(2,1)S(1)}, bf16[2,200,512]{2,1,0:T(8,128)(2,1)S(1)}, u32[]{:S(2)}, u32[]{:S(2)}) %collective-permute-start.7) | collective-permute-done | bytes 409632 | tf_op jit(solution)/shard_map/ppermute | solution.py:374
  (40 shorter events, 12.0 us)
Async XLA Ops:
  3.0 15.0 %all-to-all-start = ((f32[16,24,128]{2,1,0:T(8,128)}), f32[16,24,128]{2,1,0:T(8,128)S(1)}, u32[]{:S(2)}, u32[]{:S(2)}) async-start(f32[16,24,128]{2,1,0:T(8,128)} %get-tuple-element.23), calls=%async_computation | async-start | bytes 393216 | tf_op jit(solution)/shard_map/all_to_all | solution.py:409
  18.0 8.4 %copy-start.3 = (f32[16,24,128]{2,1,0:T(8,128)}, f32[16,24,128]{2,1,0:T(8,128)S(1)}, u32[]{:S(2)}) copy-start(f32[16,24,128]{2,1,0:T(8,128)S(1)} %all-to-all-done.packed_ref) | copy-start | bytes 589828
  18.0 60.0 %all-to-all-start.2 = ((bf16[128,2,16,512]{3,2,1,0:T(8,128)(2,1)}), bf16[128,2,16,512]{3,2,1,0:T(8,128)(2,1)}, u32[]{:S(2)}, u32[]{:S(2)}) async-start(bf16[128,2,16,512]{3,2,1,0:T(8,128)(2,1)} %bitcast.14), calls=%async_computation.2 | async-start | bytes 8388608 | tf_op jit(solution)/shard_map/all_to_all | solution.py:318
  26.6 44.3 %collective-permute-start.6 = (f32[1,32]{1,0:T(1,128)S(1)}, f32[1,32]{1,0:T(1,128)S(1)}, u32[]{:S(2)}, u32[]{:S(2)}) collective-permute-start(f32[1,32]{1,0:T(1,128)S(1)} %concatenate.9), channel_id=1, source_target_pairs={{0,112},{16,0},{32,16},{48,32},{64,48},{80,64},{96,80},{112,96},{1... | collective-permute-start | bytes 392 | tf_op jit(solution)/shard_map/ppermute | solution.py:381
  27.2 43.7 %collective-permute-start.5 = (f32[1,32]{1,0:T(1,128)S(1)}, f32[1,32]{1,0:T(1,128)S(1)}, u32[]{:S(2)}, u32[]{:S(2)}) collective-permute-start(f32[1,32]{1,0:T(1,128)S(1)} %concatenate.9), channel_id=1, source_target_pairs={{0,96},{16,112},{32,0},{48,16},{64,32},{80,48},{96,64},{112,80},{1... | collective-permute-start | bytes 392 | tf_op jit(solution)/shard_map/ppermute | solution.py:381
  27.8 45.4 %collective-permute-start.4 = (f32[1,32]{1,0:T(1,128)S(1)}, f32[1,32]{1,0:T(1,128)S(1)}, u32[]{:S(2)}, u32[]{:S(2)}) collective-permute-start(f32[1,32]{1,0:T(1,128)S(1)} %concatenate.9), channel_id=1, source_target_pairs={{0,80},{16,96},{32,112},{48,0},{64,16},{80,32},{96,48},{112,64},{1... | collective-permute-start | bytes 392 | tf_op jit(solution)/shard_map/ppermute | solution.py:381
  28.5 44.7 %collective-permute-start.3 = (f32[1,32]{1,0:T(1,128)S(1)}, f32[1,32]{1,0:T(1,128)S(1)}, u32[]{:S(2)}, u32[]{:S(2)}) collective-permute-start(f32[1,32]{1,0:T(1,128)S(1)} %concatenate.9), channel_id=1, source_target_pairs={{0,64},{16,80},{32,96},{48,112},{64,0},{80,16},{96,32},{112,48},{1... | collective-permute-start | bytes 392 | tf_op jit(solution)/shard_map/ppermute | solution.py:381
  31.1 42.1 %collective-permute-start.2 = (f32[1,32]{1,0:T(1,128)S(1)}, f32[1,32]{1,0:T(1,128)S(1)}, u32[]{:S(2)}, u32[]{:S(2)}) collective-permute-start(f32[1,32]{1,0:T(1,128)S(1)} %concatenate.9), channel_id=1, source_target_pairs={{0,48},{16,64},{32,80},{48,96},{64,112},{80,0},{96,16},{112,32},{1... | collective-permute-start | bytes 392 | tf_op jit(solution)/shard_map/ppermute | solution.py:381
  70.9 3.5 %collective-permute-start.1 = (f32[1,32]{1,0:T(1,128)S(1)}, f32[1,32]{1,0:T(1,128)S(1)}, u32[]{:S(2)}, u32[]{:S(2)}) collective-permute-start(f32[1,32]{1,0:T(1,128)S(1)} %concatenate.9), channel_id=1, source_target_pairs={{0,32},{16,48},{32,64},{48,80},{64,96},{80,112},{96,0},{112,16},{1... | collective-permute-start | bytes 392 | tf_op jit(solution)/shard_map/ppermute | solution.py:381
  70.9 3.5 %collective-permute-start = (f32[1,32]{1,0:T(1,128)S(1)}, f32[1,32]{1,0:T(1,128)S(1)}, u32[]{:S(2)}, u32[]{:S(2)}) collective-permute-start(f32[1,32]{1,0:T(1,128)S(1)} %concatenate.9), channel_id=1, source_target_pairs={{0,16},{16,32},{32,48},{48,64},{64,80},{80,96},{96,112},{112,0},{1... | collective-permute-start | bytes 392 | tf_op jit(solution)/shard_map/ppermute | solution.py:381
  78.0 8.6 %copy-start.2 = (s32[1,128]{1,0:T(1,128)S(1)}, s32[1,128]{1,0:T(1,128)}, u32[]{:S(2)}) copy-start(s32[1,128]{1,0:T(1,128)} %get-tuple-element.21.table_ref) | copy-start | bytes 1540
  78.0 61.8 %all-to-all-start.1 = ((bf16[128,2,16,512]{3,2,1,0:T(8,128)(2,1)}), bf16[128,2,16,512]{3,2,1,0:T(8,128)(2,1)}, u32[]{:S(2)}, u32[]{:S(2)}) async-start(bf16[128,2,16,512]{3,2,1,0:T(8,128)(2,1)} %bitcast.11), calls=%async_computation.1 | async-start | bytes 8388608 | tf_op jit(solution)/shard_map/all_to_all | solution.py:318
  90.5 11.8 %copy-start = (f32[2,456,512]{2,1,0:T(8,128)}, f32[2,456,512]{2,1,0:T(8,128)S(1)}, u32[]{:S(2)}) copy-start(f32[2,456,512]{2,1,0:T(8,128)S(1)} %get-tuple-element.37.total_ref) | copy-start | bytes 5603332
  90.5 57.5 %collective-permute-start.13 = (bf16[2,200,512]{2,1,0:T(8,128)(2,1)}, bf16[2,200,512]{2,1,0:T(8,128)(2,1)S(1)}, u32[]{:S(2)}, u32[]{:S(2)}) collective-permute-start(bf16[2,200,512]{2,1,0:T(8,128)(2,1)} %get-tuple-element.38), channel_id=1, source_target_pairs={{0,1},{1,2},{2,3},{3,4},{4,5},{5,6},{6,7},{7,8},{8,9},{9,10},{10,1... | collective-permute-start | bytes 1228808 | tf_op jit(solution)/shard_map/ppermute | solution.py:374
  94.1 60.0 %collective-permute-start.14 = (bf16[2,200,512]{2,1,0:T(8,128)(2,1)}, bf16[2,200,512]{2,1,0:T(8,128)(2,1)S(1)}, u32[]{:S(2)}, u32[]{:S(2)}) collective-permute-start(bf16[2,200,512]{2,1,0:T(8,128)(2,1)} %get-tuple-element.39), channel_id=1, source_target_pairs={{1,0},{2,1},{3,2},{4,3},{5,4},{6,5},{7,6},{8,7},{9,8},{10,9},{11,1... | collective-permute-start | bytes 1228808 | tf_op jit(solution)/shard_map/ppermute | solution.py:374
  102.3 53.8 %collective-permute-start.11 = (bf16[2,200,512]{2,1,0:T(8,128)(2,1)}, bf16[2,200,512]{2,1,0:T(8,128)(2,1)S(1)}, u32[]{:S(2)}, u32[]{:S(2)}) collective-permute-start(bf16[2,200,512]{2,1,0:T(8,128)(2,1)} %get-tuple-element.35), channel_id=1, source_target_pairs={{0,1},{1,2},{2,3},{3,4},{4,5},{5,6},{6,7},{7,8},{8,9},{9,10},{10,1... | collective-permute-start | bytes 1228808 | tf_op jit(solution)/shard_map/ppermute | solution.py:374
  104.2 59.2 %collective-permute-start.12 = (bf16[2,200,512]{2,1,0:T(8,128)(2,1)}, bf16[2,200,512]{2,1,0:T(8,128)(2,1)S(1)}, u32[]{:S(2)}, u32[]{:S(2)}) collective-permute-start(bf16[2,200,512]{2,1,0:T(8,128)(2,1)} %get-tuple-element.36), channel_id=1, source_target_pairs={{1,0},{2,1},{3,2},{4,3},{5,4},{6,5},{7,6},{8,7},{9,8},{10,9},{11,1... | collective-permute-start | bytes 1228808 | tf_op jit(solution)/shard_map/ppermute | solution.py:374
  143.0 19.1 %copy-start.1 = (f32[2,456,512]{2,1,0:T(8,128)S(1)}, f32[2,456,512]{2,1,0:T(8,128)}, u32[]{:S(2)}) copy-start(f32[2,456,512]{2,1,0:T(8,128)} %copy-done) | copy-start | bytes 5603332
  146.1 18.6 %collective-permute-start.9 = (bf16[2,200,512]{2,1,0:T(8,128)(2,1)S(1)}, bf16[2,200,512]{2,1,0:T(8,128)(2,1)S(1)}, u32[]{:S(2)}, u32[]{:S(2)}) collective-permute-start(bf16[2,200,512]{2,1,0:T(8,128)(2,1)S(1)} %get-tuple-element.31), channel_id=1, source_target_pairs={{0,1},{1,2},{2,3},{3,4},{4,5},{5,6},{6,7},{7,8},{8,9},{9,10},{10,1... | collective-permute-start | bytes 1228808 | tf_op jit(solution)/shard_map/ppermute | solution.py:374
  148.0 16.7 %collective-permute-start.10 = (bf16[2,200,512]{2,1,0:T(8,128)(2,1)S(1)}, bf16[2,200,512]{2,1,0:T(8,128)(2,1)S(1)}, u32[]{:S(2)}, u32[]{:S(2)}) collective-permute-start(bf16[2,200,512]{2,1,0:T(8,128)(2,1)S(1)} %get-tuple-element.32), channel_id=1, source_target_pairs={{1,0},{2,1},{3,2},{4,3},{5,4},{6,5},{7,6},{8,7},{9,8},{10,9},{11,1... | collective-permute-start | bytes 1228808 | tf_op jit(solution)/shard_map/ppermute | solution.py:374
  154.1 18.7 %collective-permute-start.7 = (bf16[2,200,512]{2,1,0:T(8,128)(2,1)S(1)}, bf16[2,200,512]{2,1,0:T(8,128)(2,1)S(1)}, u32[]{:S(2)}, u32[]{:S(2)}) collective-permute-start(bf16[2,200,512]{2,1,0:T(8,128)(2,1)S(1)} %get-tuple-element.28), channel_id=1, source_target_pairs={{0,1},{1,2},{2,3},{3,4},{4,5},{5,6},{6,7},{7,8},{8,9},{9,10},{10,1... | collective-permute-start | bytes 1228808 | tf_op jit(solution)/shard_map/ppermute | solution.py:374
  156.0 16.8 %collective-permute-start.8 = (bf16[2,200,512]{2,1,0:T(8,128)(2,1)S(1)}, bf16[2,200,512]{2,1,0:T(8,128)(2,1)S(1)}, u32[]{:S(2)}, u32[]{:S(2)}) collective-permute-start(bf16[2,200,512]{2,1,0:T(8,128)(2,1)S(1)} %get-tuple-element.29), channel_id=1, source_target_pairs={{1,0},{2,1},{3,2},{4,3},{5,4},{6,5},{7,6},{8,7},{9,8},{10,9},{11,1... | collective-permute-start | bytes 1228808 | tf_op jit(solution)/shard_map/ppermute | solution.py:374

commit v5 on v4

--- a/solution.py
+++ b/solution.py
@@ -1,5 +1,3 @@
-import functools
-
 import jax
 import jax.numpy as jnp
 from jax import lax
@@ -10,13 +8,9 @@
 ROW_PIX = 4096
 BANDS = 4
 CCD_ROWS = 256
-MOST = 2
-BORDER = 100
-EDGE = 2 * BORDER
 TAPS_HALF = 10
 FRAME = 456
 HALF = 16
-TAPS = 2 * HALF + 1
 PIECES = 16
 PIECE_ROWS = 16
 BINS = 128
@@ -28,18 +22,21 @@
 GRID_ROWS = 16
 PACKED = GRID_ROWS + 8
 BAD_COUNT = 32
-AT_SLOT = 0
 AT_BAD = 16
 AT_SHIFT = 48
 AT_VISIT = 49
 AT_ORDER = 56
 SPAN = ROW_PIX // VISITS
 PER = 4
-HALVES = 2
+PARTS = 4
+LANES = 128
+SHARE = LANES // PARTS
+PART_ROWS = CCD_ROWS // PARTS
+STRIP = 16 * 256 + 208
+STRIDE = 256
 BLOCK = 256
 PAD = 128
 WINDOW = BLOCK + 2 * PAD
-UNUSED = 1 << 20
 STEPS = VISITS // PER
 WIDTH = SPAN * PER
 
@@ -93,35 +90,47 @@
     return jnp.concatenate(parts, axis=1)
 
 
-def send_pieces(table_ref, out_ref, span, values):
-    out_ref[span] = jnp.zeros(out_ref.shape[1:], out_ref.dtype)
-    for j in range(PIECES):
-        out_ref[span, table_ref[0, AT_SLOT + j]] = values[PIECE_ROWS * j : PIECE_ROWS * (j + 1)]
+def lane_part(shape):
+    return lax.broadcasted_iota(jnp.int32, shape, 1) // SHARE
+
+
+def swap_parts(blocks):
+    part = lane_part(blocks[0].shape)
+    even = part % 2 == 0
+    low = part < 2
+
+    def cross(a, b, mask, shift):
+        first = jnp.where(mask, a, pltpu.roll(b, shift, axis=1))
+        return first, jnp.where(mask, pltpu.roll(a, LANES - shift, axis=1), b)
+
+    y0, y1 = cross(blocks[0], blocks[1], even, SHARE)
+    y2, y3 = cross(blocks[2], blocks[3], even, SHARE)
+    z0, z2 = cross(y0, y2, low, 2 * SHARE)
+    z1, z3 = cross(y1, y3, low, 2 * SHARE)
+    return z0, z1, z2, z3
+
+
+def send_pieces(out_ref, span, values):
+    for tile in range(SPAN // LANES):
+        column = values[:, LANES * tile : LANES * (tile + 1)]
+        blocks = [column[PART_ROWS * g : PART_ROWS * (g + 1)] for g in range(PARTS)]
+        for k, block in enumerate(swap_parts(blocks)):
+            out_ref[span * (SPAN // SHARE) + PARTS * tile + k] = block.astype(jnp.bfloat16)
 
 
 def pack_body(
     mix_ref, patch_ref, pos_ref, psf_ref, shift_ref, bad_ref, band_ref, grid_ref, out_ref, table_ref, taps_ref
 ):
     group = lax.axis_index("fp")
-    shape = (PATCHES, BINS)
-    patch = lax.broadcasted_iota(jnp.int32, shape, 0)
-    slot = lax.broadcasted_iota(jnp.int32, shape, 1)
     lane = lax.broadcasted_iota(jnp.int32, (1, BINS), 1)
-    first = jnp.full(shape, UNUSED, jnp.int32)
-    patches = [patch_ref[j] for j in range(PIECES)]
     table = jnp.zeros((1, BINS), jnp.int32)
+    first = table
     for j in range(PIECES):
-        rank = jnp.int32(0)
-        for k in range(j):
-            rank = rank + (patches[k] == patches[j]).astype(jnp.int32)
-        first = jnp.where((patch == patches[j]) & (slot == rank), pos_ref[0, j], first)
-        table = jnp.where(
-            lane == AT_SLOT + j, patches[j] * MOST + jnp.minimum(rank, MOST - 1), table
-        )
+        first = jnp.where(lane == j, patch_ref[j] * STRIDE + pos_ref[0, j], first)
     first = first.astype(jnp.float32)
     for q in range(PATCHES):
         out_ref[q, :GRID_ROWS] = grid_ref[0, 0] * mix_ref[q, group]
-        out_ref[q, GRID_ROWS:] = jnp.broadcast_to(first[q : q + 1], (PACKED - GRID_ROWS, BINS))
+        out_ref[q, GRID_ROWS:] = jnp.broadcast_to(first, (PACKED - GRID_ROWS, BINS))
     for k in range(BAD_COUNT):
         table = jnp.where(lane == AT_BAD + k, bad_ref[0, k], table)
     table = jnp.where(lane == AT_SHIFT, shift_ref[0, 0], table)
@@ -164,9 +173,9 @@
 
     _, _, window = masked_window(good_ref, left_ref, mid_ref, right_ref)
     for span in range(PER):
-        weight = convolve(window, band_ref, span).astype(jnp.bfloat16)
-        weight_ref[span] = weight
-        send_pieces(table_ref, send_ref, span, weight)
+        weight = convolve(window, band_ref, span)
+        weight_ref[span] = weight.astype(jnp.bfloat16)
+        send_pieces(send_ref, span, weight)
 
 
 def flux_body(
@@ -207,33 +216,53 @@
             backdrop[:, None, :], (GRID_ROWS, CCD_ROWS // GRID_ROWS, SPAN)
         ).reshape(CCD_ROWS, SPAN)
         flux = warped[:CCD_ROWS] - backdrop
-        product = flux * weight_ref[span].astype(jnp.float32)
-        send_pieces(table_ref, send_ref, span, product.astype(jnp.bfloat16))
-
-
-def scatter_body(half, table_ref, rows_ref, *refs):
-    received_refs, (total_ref, low_ref, high_ref) = refs[:TURNS], refs[TURNS:]
-    slots = rows_ref.shape[-1]
-    total = None
-    for turn, received_ref in enumerate(received_refs):
-        visit = table_ref[0, AT_ORDER + TURNS * (half + pl.program_id(0)) + turn]
-        rows = rows_ref[(table_ref[0, AT_VISIT] - visit) & (VISITS - 1)]
-        place = lax.broadcasted_iota(jnp.int32, (FRAME, slots), 0) == rows
-        frames = jnp.dot(
-            place.astype(jnp.bfloat16), received_ref[0], preferred_element_type=jnp.float32
-        )
-        total = total + frames if turn else frames
-    total_ref[0] = total
-    low_ref[0] = total[:EDGE].astype(jnp.bfloat16)
-    high_ref[0] = total[FRAME - EDGE :].astype(jnp.bfloat16)
-
-
-def merge_body(total_ref, before_ref, after_ref, *refs):
-    out_ref = refs[-1]
-    total = total_ref[0]
-    out_ref[0, :EDGE] = total[:EDGE] + before_ref[0].astype(jnp.float32)
-    out_ref[0, EDGE : FRAME - EDGE] = total[EDGE : FRAME - EDGE]
-    out_ref[0, FRAME - EDGE :] = total[FRAME - EDGE :] + after_ref[0].astype(jnp.float32)
+        send_pieces(send_ref, span, flux * weight_ref[span].astype(jnp.float32))
+
+
+def strip_body(table_ref, rows_ref, received_ref, out_ref, *strips):
+    for strip_ref in strips:
+        strip_ref[...] = jnp.zeros(strip_ref.shape, strip_ref.dtype)
+    part = lane_part((PIECE_ROWS, LANES))
+    masks = [part == m for m in range(PARTS)]
+    blocks = PART_ROWS // PIECE_ROWS
+
+    def step(index, carry):
+        turn = index // (GROUPS * blocks)
+        group = index // blocks % GROUPS
+        block = index % blocks
+        work = []
+        for band, strip_ref in enumerate(strips):
+            visit = table_ref[0, AT_ORDER + TURNS * band + turn]
+            value = received_ref[(visit * GROUPS + group) * blocks + block].astype(jnp.float32)
+            base = (((table_ref[0, AT_VISIT] - visit) & (VISITS - 1)) * GROUPS + group) * PIECES
+            for m in range(PARTS):
+                row = rows_ref[base + blocks * m + block]
+                work.append((strip_ref.at[pl.ds(row, PIECE_ROWS), :], value, masks[m]))
+        sums = [ref[...] + value for ref, value, _ in work]
+        for (ref, _, mask), total in zip(work, sums):
+            pltpu.store(ref, total, mask=mask)
+        return carry
+
+    lax.fori_loop(0, TURNS * GROUPS * blocks, step, 0)
+    part = lane_part((FRAME, LANES))
+    even = part % 2 == 0
+    low = part < 2
+
+    def fold(a, b, mask, shift):
+        return jnp.where(mask, a, b) + pltpu.roll(jnp.where(mask, b, a), shift, axis=1)
+
+    for patch in range(PATCHES):
+        frames = [strip_ref[STRIDE * patch : STRIDE * patch + FRAME] for strip_ref in strips]
+        first = fold(frames[0], frames[1], even, SHARE)
+        second = fold(frames[2], frames[3], even, SHARE)
+        out_ref[patch] = fold(first, second, low, 2 * SHARE).astype(jnp.bfloat16)
+
+
+def spread_body(received_ref, out_ref):
+    for tile in range(SPAN // LANES):
+        blocks = [received_ref[PARTS * tile + m].astype(jnp.float32) for m in range(PARTS)]
+        for band, block in enumerate(swap_parts(blocks)):
+            out_ref[band, :, LANES * tile : LANES * (tile + 1)] = block
 
 
 SMEM = pl.BlockSpec(memory_space=pltpu.SMEM)
@@ -259,8 +288,8 @@
     return [left, mid, right]
 
 
-SEND_SHAPE = (VISITS, PATCHES * MOST, PIECE_ROWS, SPAN)
-SEND_BLOCK = pl.BlockSpec((PER,) + SEND_SHAPE[1:], lambda i: (i, 0, 0, 0))
+SEND_SHAPE = (VISITS * GROUPS, PART_ROWS, LANES)
+SEND_BLOCK = pl.BlockSpec((PER * GROUPS,) + SEND_SHAPE[1:], lambda i: (i, 0, 0))
 WEIGHT_BLOCK = pl.BlockSpec((PER, CCD_ROWS, SPAN), lambda i: (i, 0, 0))
 GOOD_SCRATCH = pltpu.VMEM((1, ROW_PIX + 2 * PAD), jnp.float32)
 BAND_SCRATCH = pltpu.VMEM((WINDOW, BLOCK), jnp.bfloat16)
@@ -313,75 +342,41 @@
     )(table, psf, image, image, image, packed, weight)
 
 
-def exchange(pieces):
-    sent = pieces.reshape(VISITS * PATCHES, MOST, PIECE_ROWS, SPAN)
-    return lax.all_to_all(sent, ("visit", "fp"), split_axis=0, concat_axis=0, tiled=True)
-
-
-def scatter(half, table, dest_rows, received):
-    slots = PATCHES * MOST * PIECE_ROWS
-    bands = BANDS // HALVES
-    shapes = [
-        jax.ShapeDtypeStruct((bands, FRAME, SPAN), jnp.float32),
-        jax.ShapeDtypeStruct((bands, EDGE, SPAN), jnp.bfloat16),
-        jax.ShapeDtypeStruct((bands, EDGE, SPAN), jnp.bfloat16),
-    ]
-
-    def received_spec(turn):
-        return pl.BlockSpec(
-            (1, slots, SPAN),
-            lambda i, at: (at[0, AT_ORDER + TURNS * (bands * half + i) + turn], 0, 0),
-        )
-
-    received = received.reshape(VISITS, slots, SPAN)
+def exchange(pieces, axes):
+    return lax.all_to_all(pieces, axes, split_axis=0, concat_axis=0, tiled=True)
+
+
+def strip(table, rows, received):
     return pl.pallas_call(
-        functools.partial(scatter_body, bands * half),
-        grid_spec=pltpu.PrefetchScalarGridSpec(
-            num_scalar_prefetch=1,
-            grid=(bands,),
-            in_specs=[pl.BlockSpec((VISITS, 1, slots), lambda i, at: (0, 0, 0))]
-            + [received_spec(turn) for turn in range(TURNS)],
-            out_specs=[
-                pl.BlockSpec((1,) + shape.shape[1:], lambda i, at: (i, 0, 0)) for shape in shapes
-            ],
-        ),
-        out_shape=shapes,
-        compiler_params=params(16),
-        name="scatter",
-    )(table, dest_rows, *[received] * TURNS)
-
-
-def merge(half, total, before, after, earlier):
-    bands = BANDS // HALVES
-    edge = pl.BlockSpec((1, EDGE, SPAN), lambda i: (i, 0, 0))
-    frame = pl.BlockSpec((1, FRAME, SPAN), lambda i: (i, 0, 0))
+        strip_body,
+        in_specs=[SMEM, SMEM, pl.BlockSpec(memory_space=pltpu.VMEM)],
+        out_specs=pl.BlockSpec(memory_space=pltpu.VMEM),
+        out_shape=jax.ShapeDtypeStruct((PATCHES, FRAME, LANES), jnp.bfloat16),
+        scratch_shapes=[pltpu.VMEM((STRIP, LANES), jnp.float32)] * BANDS,
+        compiler_params=pltpu.CompilerParams(vmem_limit_bytes=24 << 20),
+        name="strip",
+    )(table, rows, received.reshape(-1, PIECE_ROWS, LANES))
+
+
+def spread(received):
+    rows = FRAME // 3
     return pl.pallas_call(
-        merge_body,
-        grid=(bands,),
-        in_specs=[frame, edge, edge] + [pl.BlockSpec(memory_space=pl.ANY)] * len(earlier),
-        out_specs=pl.BlockSpec((1, FRAME, SPAN), lambda i: (bands * half + i, 0, 0)),
+        spread_body,
+        grid=(3,),
+        in_specs=[pl.BlockSpec((PATCHES, rows, LANES), lambda i: (0, i, 0))],
+        out_specs=pl.BlockSpec((BANDS, rows, SPAN), lambda i: (0, i, 0)),
         out_shape=jax.ShapeDtypeStruct((BANDS, FRAME, SPAN), jnp.float32),
-        input_output_aliases={3: 0} if earlier else {},
-        compiler_params=params(16),
-        name="merge",
-    )(total, before, after, *earlier)
-
-
-def swap_borders(low, high):
-    peers = lax.axis_size("fp")
-    up = [(i, i + 1) for i in range(peers - 1)]
-    down = [(j, i) for i, j in up]
-    return lax.ppermute(high, "fp", up), lax.ppermute(low, "fp", down)
-
-
-def slot_rows(first):
-    first = first.reshape(1, GROUPS * MOST)
+        compiler_params=params(24),
+        name="spread",
+    )(received)
+
+
+def strip_rows(first):
+    first = first.reshape(1, GROUPS * PIECES)
     blocks = [first]
     for k in range(1, VISITS):
         blocks.append(lax.ppermute(first, "visit", [(i, (i + k) % VISITS) for i in range(VISITS)]))
-    first = jnp.concatenate(blocks).astype(jnp.int32)
-    rows = first[:, :, None] + jnp.arange(PIECE_ROWS, dtype=jnp.int32)
-    return rows.reshape(VISITS, 1, GROUPS * MOST * PIECE_ROWS)
+    return jnp.concatenate(blocks, axis=1).astype(jnp.int32).reshape(-1)
 
 
 def shards(
@@ -408,19 +403,15 @@
     )
     packed = lax.all_to_all(packed, "fp", split_axis=0, concat_axis=0, tiled=True)
     weight_pieces, weight = send_weight(table, psf, inv_var)
-    weight_arrived = exchange(weight_pieces)
+    both = ("visit", "fp")
+    weight_arrived = exchange(weight_pieces, both)
     flux_pieces = send_flux(table, psf, image, packed, weight)
-    dest_rows = slot_rows(packed[:, GRID_ROWS, :MOST])
-    flux_pieces, dest_rows = lax.optimization_barrier((flux_pieces, dest_rows))
-    flux_arrived = exchange(flux_pieces)
-    outs = []
-    for received in (weight_arrived, flux_arrived):
-        out = []
-        for half in range(HALVES):
-            total, low, high = scatter(half, table, dest_rows, received)
-            out = [merge(half, total, *swap_borders(low, high), out)]
-        outs.append(out[0])
-    return (outs[1][:, None], outs[0][:, None])
+    rows = strip_rows(packed[:, GRID_ROWS, :PIECES])
+    flux_pieces, rows = lax.optimization_barrier((flux_pieces, rows))
+    flux_arrived = exchange(flux_pieces, both)
+    weight_frames = exchange(strip(table, rows, weight_arrived), "fp")
+    flux_frames = exchange(strip(table, rows, flux_arrived), "fp")
+    return (spread(flux_frames)[:, None], spread(weight_frames)[:, None])
 
 
 def solution(mesh):

time: 175 us -> 163 us (0.931)
  the two profiles are of different devices: /device:TPU:14 before, /device:TPU:0 now
where the time goes in v5:
time: 163 us; the launch traced here: 162 us
  waiting for transfers between devices  76.4 us (47%)
  Pallas kernels  43.7 us (27%)
  starting transfers between devices  37.9 us (23%)
  local copies, waits for them, and re-layouts  2.71 us (2%)
    all_to_all x4, waiting for transfers between devices, exchange(): return lax.all_to_all(pieces, axes, split_axis=0, concat_axis=0, tiled=True)  52 us
    all_to_all x4, starting transfers between devices, exchange(): return lax.all_to_all(pieces, axes, split_axis=0, concat_axis=0, tiled=True)  23.9 us
    ppermute x7, waiting for transfers between devices, strip_rows(): lax.ppermute(first, 'visit', [(i, (i + k) % VISITS) for i in range(VISITS)])  21.1 us
    pallas_call x2, Pallas kernels, strip(): pl.pallas_call(strip_body, in_specs=[SMEM, SMEM, pl.BlockSpec(memory_spac...  21 us
    pallas_call x2, Pallas kernels, spread(): pl.pallas_call(spread_body, grid=(3,), in_specs=[pl.BlockSpec((PATCHES, r...  9.81 us
    all_to_all x1, starting transfers between devices, shards(): lax.all_to_all(packed, 'fp', split_axis=0, concat_axis=0, tiled=True)  8.13 us
    pallas_call x1, Pallas kernels, send_flux(): pl.pallas_call(flux_body, grid=(STEPS,), in_specs=[SMEM] * 2 + window_spe...  6.38 us
    ppermute x7, starting transfers between devices, strip_rows(): lax.ppermute(first, 'visit', [(i, (i + k) % VISITS) for i in range(VISITS)])  5.86 us
  transfers between devices with their start and end apart: 12, of which 7 were waited for; matrix products, arithmetic and copies ran while one was open for 0% of the time, Pallas kernels for 23%

profile of v5, /device:TPU:0, one launch (start us, length us, event | category | flops | bytes accessed | tf_op | source)
XLA Modules:
  0.0 162.2 jit_solution(12174443447579699665)
XLA Ops:
  1.3 1.6 pack.1
  2.9 8.1 %all-to-all-start = ((f32[16,24,128]{2,1,0:T(8,128)}), f32[16,24,128]{2,1,0:T(8,128)S(1)}, u32[]{:S(2)}, u32[]{:S(2)}) async-start(f32[16,24,128]{2,1,0:T(8,128)} %get-tuple-element.11), calls=%async_computation | async-start | bytes 393216 | tf_op jit(solution)/shard_map/all_to_all | solution.py:404
  11.0 4.8 %send_weight.1 = (bf16[128,64,128]{2,1,0:T(8,128)(2,1)}, bf16[8,256,512]{2,1,0:T(8,128)(2,1)}) custom-call(s32[1,128]{1,0:T(1,128)} %get-tuple-element.9.table_ref, f32[1,128]{1,0:T(1,128)} %get-tuple-element.10.psf_ref, bf16[1,256,4096]{2,1,0:T(8,128)(2,1)} %right_ref.2, bf16[1,256,4096]{2,1,0:T(8,128)(2,1)} %right_ref.2, bf16[1,256,4096]{2,1,0:T(8,128)(2,1)} %right_ref.2), custom_call_target="tpu_custom_call" | custom-call | tf_op jit(solution)/shard_map/send_weight/pallas_call | solution.py:299
  15.8 3.3 %all-to-all-done.packed_ref = f32[16,24,128]{2,1,0:T(8,128)S(1)} async-done(((f32[16,24,128]{2,1,0:T(8,128)}), f32[16,24,128]{2,1,0:T(8,128)S(1)}, u32[]{:S(2)}, u32[]{:S(2)}) %all-to-all-start) | async-done | bytes 196640 | tf_op jit(solution)/shard_map/all_to_all | solution.py:404
  19.2 6.9 %all-to-all-start.3 = ((bf16[128,64,128]{2,1,0:T(8,128)(2,1)}), bf16[128,64,128]{2,1,0:T(8,128)(2,1)S(1)}, u32[]{:S(2)}, u32[]{:S(2)}) async-start(bf16[128,64,128]{2,1,0:T(8,128)(2,1)} %get-tuple-element.15), calls=%async_computation.3 | async-start | bytes 4194304 | tf_op jit(solution)/shard_map/all_to_all | solution.py:346
  26.2 1.9 %collective-permute-start.6 = (f32[1,256]{1,0:T(1,128)S(1)}, f32[1,256]{1,0:T(1,128)S(1)}, u32[]{:S(2)}, u32[]{:S(2)}) collective-permute-start(f32[1,256]{1,0:T(1,128)S(1)} %reshape_squeeze.3), channel_id=1, source_target_pairs={{0,112},{16,0},{32,16},{48,32},{64,48},{80,64},{96,80},{112,96},{1... | collective-permute-start | bytes 3080 | tf_op jit(solution)/shard_map/ppermute | solution.py:378
  28.2 0.9 collective-permute-start.5
  29.1 2.6 %collective-permute-start.3 = (f32[1,256]{1,0:T(1,128)S(1)}, f32[1,256]{1,0:T(1,128)S(1)}, u32[]{:S(2)}, u32[]{:S(2)}) collective-permute-start(f32[1,256]{1,0:T(1,128)S(1)} %reshape_squeeze.3), channel_id=1, source_target_pairs={{0,64},{16,80},{32,96},{48,112},{64,0},{80,16},{96,32},{112,48},{1... | collective-permute-start | bytes 3080 | tf_op jit(solution)/shard_map/ppermute | solution.py:378
  32.2 6.4 %send_flux.1 = bf16[128,64,128]{2,1,0:T(8,128)(2,1)} custom-call(s32[1,128]{1,0:T(1,128)} %get-tuple-element.9.table_ref, f32[1,128]{1,0:T(1,128)} %get-tuple-element.10.psf_ref, bf16[1,256,4096]{2,1,0:T(8,128)(2,1)} %right_ref.3, bf16[1,256,4096]{2,1,0:T(8,128)(2,1)} %right_ref.3, bf16[1,256,4096]{2,1,0:T(8,128)(2,1)} %right_ref.3, ...), custom_call_target="tpu_custom_call" | custom-call | tf_op jit(solution)/shard_map/send_flux/pallas_call | solution.py:329
  38.6 11.8 %collective-permute-done = f32[1,256]{1,0:T(1,128)S(1)} collective-permute-done((f32[1,256]{1,0:T(1,128)S(1)}, f32[1,256]{1,0:T(1,128)S(1)}, u32[]{:S(2)}, u32[]{:S(2)}) %collective-permute-start) | collective-permute-done | bytes 1056 | tf_op jit(solution)/shard_map/ppermute | solution.py:378
  50.4 4.8 %collective-permute-done.1 = f32[1,256]{1,0:T(1,128)S(1)} collective-permute-done((f32[1,256]{1,0:T(1,128)S(1)}, f32[1,256]{1,0:T(1,128)S(1)}, u32[]{:S(2)}, u32[]{:S(2)}) %collective-permute-start.1) | collective-permute-done | bytes 1056 | tf_op jit(solution)/shard_map/ppermute | solution.py:378
  55.2 4.5 %collective-permute-done.2 = f32[1,256]{1,0:T(1,128)S(1)} collective-permute-done((f32[1,256]{1,0:T(1,128)S(1)}, f32[1,256]{1,0:T(1,128)S(1)}, u32[]{:S(2)}, u32[]{:S(2)}) %collective-permute-start.2) | collective-permute-done | bytes 1056 | tf_op jit(solution)/shard_map/ppermute | solution.py:378
  59.8 8.0 %all-to-all-start.1 = ((bf16[128,64,128]{2,1,0:T(8,128)(2,1)}), bf16[128,64,128]{2,1,0:T(8,128)(2,1)}, u32[]{:S(2)}, u32[]{:S(2)}) async-start(bf16[128,64,128]{2,1,0:T(8,128)(2,1)} %send_flux.1), calls=%async_computation.1 | async-start | bytes 4194304 | tf_op jit(solution)/shard_map/all_to_all | solution.py:346
  67.8 10.1 %strip.3 = bf16[16,456,128]{2,1,0:T(8,128)(2,1)S(1)} custom-call(s32[1,128]{1,0:T(1,128)S(1)} %copy-done.2, s32[2048]{0:T(1024)S(1)} %convert_element_type.6.rows_ref, bf16[512,16,128]{2,1,0:T(8,128)(2,1)S(1)} %bitcast.17), custom_call_target="tpu_custom_call" | custom-call | tf_op jit(solution)/shard_map/strip/pallas_call | solution.py:350
  77.9 1.2 copy-done
  79.1 18.0 %all-to-all-done.1 = bf16[128,64,128]{2,1,0:T(8,128)(2,1)} async-done(((bf16[128,64,128]{2,1,0:T(8,128)(2,1)}), bf16[128,64,128]{2,1,0:T(8,128)(2,1)}, u32[]{:S(2)}, u32[]{:S(2)}) %all-to-all-start.1) | async-done | bytes 2097184 | tf_op jit(solution)/shard_map/all_to_all | solution.py:346
  97.1 4.6 %all-to-all-start.4 = ((bf16[16,456,128]{2,1,0:T(8,128)(2,1)}), bf16[16,456,128]{2,1,0:T(8,128)(2,1)}, u32[]{:S(2)}, u32[]{:S(2)}) async-start(bf16[16,456,128]{2,1,0:T(8,128)(2,1)} %copy-done), calls=%async_computation.4 | async-start | bytes 3735552 | tf_op jit(solution)/shard_map/all_to_all | solution.py:346
  101.7 11.0 %strip.2 = bf16[16,456,128]{2,1,0:T(8,128)(2,1)S(1)} custom-call(s32[1,128]{1,0:T(1,128)S(1)} %copy-done.2, s32[2048]{0:T(1024)S(1)} %convert_element_type.6.rows_ref, bf16[512,16,128]{2,1,0:T(8,128)(2,1)} %bitcast.8.received_ref), custom_call_target="tpu_custom_call" | custom-call | tf_op jit(solution)/shard_map/strip/pallas_call | solution.py:350
  112.7 1.2 copy-done.1
  113.9 14.4 %all-to-all-done.4.received_ref = bf16[16,456,128]{2,1,0:T(8,128)(2,1)} async-done(((bf16[16,456,128]{2,1,0:T(8,128)(2,1)}), bf16[16,456,128]{2,1,0:T(8,128)(2,1)}, u32[]{:S(2)}, u32[]{:S(2)}) %all-to-all-start.4) | async-done | bytes 1867808 | tf_op jit(solution)/shard_map/all_to_all | solution.py:346
  128.3 4.4 %all-to-all-start.2 = ((bf16[16,456,128]{2,1,0:T(8,128)(2,1)}), bf16[16,456,128]{2,1,0:T(8,128)(2,1)}, u32[]{:S(2)}, u32[]{:S(2)}) async-start(bf16[16,456,128]{2,1,0:T(8,128)(2,1)} %copy-done.1), calls=%async_computation.2 | async-start | bytes 3735552 | tf_op jit(solution)/shard_map/all_to_all | solution.py:346
  132.8 4.9 %spread.3 = f32[4,456,512]{2,1,0:T(8,128)} custom-call(bf16[16,456,128]{2,1,0:T(8,128)(2,1)} %all-to-all-done.4.received_ref), custom_call_target="tpu_custom_call" | custom-call | tf_op jit(solution)/shard_map/spread/pallas_call | solution.py:363
  137.7 19.6 %all-to-all-done.2.received_ref = bf16[16,456,128]{2,1,0:T(8,128)(2,1)} async-done(((bf16[16,456,128]{2,1,0:T(8,128)(2,1)}), bf16[16,456,128]{2,1,0:T(8,128)(2,1)}, u32[]{:S(2)}, u32[]{:S(2)}) %all-to-all-start.2) | async-done | bytes 1867808 | tf_op jit(solution)/shard_map/all_to_all | solution.py:346
  157.3 4.9 %spread.2 = f32[4,456,512]{2,1,0:T(8,128)} custom-call(bf16[16,456,128]{2,1,0:T(8,128)(2,1)} %all-to-all-done.2.received_ref), custom_call_target="tpu_custom_call" | custom-call | tf_op jit(solution)/shard_map/spread/pallas_call | solution.py:363
  (28 shorter events, 0.7 us)
Async XLA Ops:
  2.9 16.3 %all-to-all-start = ((f32[16,24,128]{2,1,0:T(8,128)}), f32[16,24,128]{2,1,0:T(8,128)S(1)}, u32[]{:S(2)}, u32[]{:S(2)}) async-start(f32[16,24,128]{2,1,0:T(8,128)} %get-tuple-element.11), calls=%async_computation | async-start | bytes 393216 | tf_op jit(solution)/shard_map/all_to_all | solution.py:404
  19.2 6.9 %copy-start.3 = (f32[16,24,128]{2,1,0:T(8,128)}, f32[16,24,128]{2,1,0:T(8,128)S(1)}, u32[]{:S(2)}) copy-start(f32[16,24,128]{2,1,0:T(8,128)S(1)} %all-to-all-done.packed_ref) | copy-start | bytes 589828
  19.2 40.6 %all-to-all-start.3 = ((bf16[128,64,128]{2,1,0:T(8,128)(2,1)}), bf16[128,64,128]{2,1,0:T(8,128)(2,1)S(1)}, u32[]{:S(2)}, u32[]{:S(2)}) async-start(bf16[128,64,128]{2,1,0:T(8,128)(2,1)} %get-tuple-element.15), calls=%async_computation.3 | async-start | bytes 4194304 | tf_op jit(solution)/shard_map/all_to_all | solution.py:346
  26.2 33.5 %collective-permute-start.6 = (f32[1,256]{1,0:T(1,128)S(1)}, f32[1,256]{1,0:T(1,128)S(1)}, u32[]{:S(2)}, u32[]{:S(2)}) collective-permute-start(f32[1,256]{1,0:T(1,128)S(1)} %reshape_squeeze.3), channel_id=1, source_target_pairs={{0,112},{16,0},{32,16},{48,32},{64,48},{80,64},{96,80},{112,96},{1... | collective-permute-start | bytes 3080 | tf_op jit(solution)/shard_map/ppermute | solution.py:378
  28.2 31.6 %collective-permute-start.5 = (f32[1,256]{1,0:T(1,128)S(1)}, f32[1,256]{1,0:T(1,128)S(1)}, u32[]{:S(2)}, u32[]{:S(2)}) collective-permute-start(f32[1,256]{1,0:T(1,128)S(1)} %reshape_squeeze.3), channel_id=1, source_target_pairs={{0,96},{16,112},{32,0},{48,16},{64,32},{80,48},{96,64},{112,80},{1... | collective-permute-start | bytes 3080 | tf_op jit(solution)/shard_map/ppermute | solution.py:378
  29.0 30.7 %collective-permute-start.4 = (f32[1,256]{1,0:T(1,128)S(1)}, f32[1,256]{1,0:T(1,128)S(1)}, u32[]{:S(2)}, u32[]{:S(2)}) collective-permute-start(f32[1,256]{1,0:T(1,128)S(1)} %reshape_squeeze.3), channel_id=1, source_target_pairs={{0,80},{16,96},{32,112},{48,0},{64,16},{80,32},{96,48},{112,64},{1... | collective-permute-start | bytes 3080 | tf_op jit(solution)/shard_map/ppermute | solution.py:378
  29.1 30.5 %collective-permute-start.3 = (f32[1,256]{1,0:T(1,128)S(1)}, f32[1,256]{1,0:T(1,128)S(1)}, u32[]{:S(2)}, u32[]{:S(2)}) collective-permute-start(f32[1,256]{1,0:T(1,128)S(1)} %reshape_squeeze.3), channel_id=1, source_target_pairs={{0,64},{16,80},{32,96},{48,112},{64,0},{80,16},{96,32},{112,48},{1... | collective-permute-start | bytes 3080 | tf_op jit(solution)/shard_map/ppermute | solution.py:378
  31.8 18.6 %collective-permute-start = (f32[1,256]{1,0:T(1,128)S(1)}, f32[1,256]{1,0:T(1,128)S(1)}, u32[]{:S(2)}, u32[]{:S(2)}) collective-permute-start(f32[1,256]{1,0:T(1,128)S(1)} %reshape_squeeze.3), channel_id=1, source_target_pairs={{0,16},{16,32},{32,48},{48,64},{64,80},{80,96},{96,112},{112,0},{1... | collective-permute-start | bytes 3080 | tf_op jit(solution)/shard_map/ppermute | solution.py:378
  50.4 4.8 %collective-permute-start.1 = (f32[1,256]{1,0:T(1,128)S(1)}, f32[1,256]{1,0:T(1,128)S(1)}, u32[]{:S(2)}, u32[]{:S(2)}) collective-permute-start(f32[1,256]{1,0:T(1,128)S(1)} %reshape_squeeze.3), channel_id=1, source_target_pairs={{0,32},{16,48},{32,64},{48,80},{64,96},{80,112},{96,0},{112,16},{1... | collective-permute-start | bytes 3080 | tf_op jit(solution)/shard_map/ppermute | solution.py:378
  55.2 4.5 %collective-permute-start.2 = (f32[1,256]{1,0:T(1,128)S(1)}, f32[1,256]{1,0:T(1,128)S(1)}, u32[]{:S(2)}, u32[]{:S(2)}) collective-permute-start(f32[1,256]{1,0:T(1,128)S(1)} %reshape_squeeze.3), channel_id=1, source_target_pairs={{0,48},{16,64},{32,80},{48,96},{64,112},{80,0},{96,16},{112,32},{1... | collective-permute-start | bytes 3080 | tf_op jit(solution)/shard_map/ppermute | solution.py:378
  59.8 8.0 %copy-start.2 = (s32[1,128]{1,0:T(1,128)S(1)}, s32[1,128]{1,0:T(1,128)}, u32[]{:S(2)}) copy-start(s32[1,128]{1,0:T(1,128)} %get-tuple-element.9.table_ref) | copy-start | bytes 1540
  59.8 37.3 %all-to-all-start.1 = ((bf16[128,64,128]{2,1,0:T(8,128)(2,1)}), bf16[128,64,128]{2,1,0:T(8,128)(2,1)}, u32[]{:S(2)}, u32[]{:S(2)}) async-start(bf16[128,64,128]{2,1,0:T(8,128)(2,1)} %send_flux.1), calls=%async_computation.1 | async-start | bytes 4194304 | tf_op jit(solution)/shard_map/all_to_all | solution.py:346
  77.9 1.2 copy-start
  97.1 31.3 %all-to-all-start.4 = ((bf16[16,456,128]{2,1,0:T(8,128)(2,1)}), bf16[16,456,128]{2,1,0:T(8,128)(2,1)}, u32[]{:S(2)}, u32[]{:S(2)}) async-start(bf16[16,456,128]{2,1,0:T(8,128)(2,1)} %copy-done), calls=%async_computation.4 | async-start | bytes 3735552 | tf_op jit(solution)/shard_map/all_to_all | solution.py:346
  112.7 1.2 copy-start.1
  128.3 28.9 %all-to-all-start.2 = ((bf16[16,456,128]{2,1,0:T(8,128)(2,1)}), bf16[16,456,128]{2,1,0:T(8,128)(2,1)}, u32[]{:S(2)}, u32[]{:S(2)}) async-start(bf16[16,456,128]{2,1,0:T(8,128)(2,1)} %copy-done.1), calls=%async_computation.2 | async-start | bytes 3735552 | tf_op jit(solution)/shard_map/all_to_all | solution.py:346

commit v6 on v5

--- a/solution.py
+++ b/solution.py
@@ -29,6 +29,7 @@
 SPAN = ROW_PIX // VISITS
 PER = 4
 PARTS = 4
+THIRDS = 3
 LANES = 128
 SHARE = LANES // PARTS
 PART_ROWS = CCD_ROWS // PARTS
@@ -234,7 +235,9 @@
         for band, strip_ref in enumerate(strips):
             visit = table_ref[0, AT_ORDER + TURNS * band + turn]
             value = received_ref[(visit * GROUPS + group) * blocks + block].astype(jnp.float32)
-            base = (((table_ref[0, AT_VISIT] - visit) & (VISITS - 1)) * GROUPS + group) * PIECES
+            own = table_ref[0, AT_VISIT]
+            place = (((own >> 1) - (visit >> 1)) & (VISITS // 2 - 1)) * 2 + ((own ^ visit) & 1)
+            base = (place * GROUPS + group) * PIECES
             for m in range(PARTS):
                 row = rows_ref[base + blocks * m + block]
                 work.append((strip_ref.at[pl.ds(row, PIECE_ROWS), :], value, masks[m]))
@@ -258,11 +261,31 @@
         out_ref[patch] = fold(first, second, low, 2 * SHARE).astype(jnp.bfloat16)
 
 
-def spread_body(received_ref, out_ref):
-    for tile in range(SPAN // LANES):
-        blocks = [received_ref[PARTS * tile + m].astype(jnp.float32) for m in range(PARTS)]
-        for band, block in enumerate(swap_parts(blocks)):
-            out_ref[band, :, LANES * tile : LANES * (tile + 1)] = block
+def spread_body(received_ref, out_ref, taken_ref, given_ref, in_sems, out_sems):
+    rows = FRAME // THIRDS
+    reads = [
+        pltpu.make_async_copy(
+            received_ref.at[:, pl.ds(rows * n, rows)], taken_ref.at[n], in_sems.at[n]
+        )
+        for n in range(THIRDS)
+    ]
+    writes = [
+        pltpu.make_async_copy(
+            given_ref.at[n], out_ref.at[:, pl.ds(rows * n, rows)], out_sems.at[n]
+        )
+        for n in range(THIRDS)
+    ]
+    for read in reads:
+        read.start()
+    for n in range(THIRDS):
+        reads[n].wait()
+        for tile in range(SPAN // LANES):
+            blocks = [taken_ref[n, PARTS * tile + m].astype(jnp.float32) for m in range(PARTS)]
+            for band, block in enumerate(swap_parts(blocks)):
+                given_ref[n, band, :, LANES * tile : LANES * (tile + 1)] = block
+        writes[n].start()
+    for write in writes:
+        write.wait()
 
 
 SMEM = pl.BlockSpec(memory_space=pltpu.SMEM)
@@ -359,23 +382,31 @@
 
 
 def spread(received):
-    rows = FRAME // 3
+    rows = FRAME // THIRDS
+    anywhere = pl.BlockSpec(memory_space=pl.ANY)
     return pl.pallas_call(
         spread_body,
-        grid=(3,),
-        in_specs=[pl.BlockSpec((PATCHES, rows, LANES), lambda i: (0, i, 0))],
-        out_specs=pl.BlockSpec((BANDS, rows, SPAN), lambda i: (0, i, 0)),
+        in_specs=[anywhere],
+        out_specs=anywhere,
         out_shape=jax.ShapeDtypeStruct((BANDS, FRAME, SPAN), jnp.float32),
-        compiler_params=params(24),
+        scratch_shapes=[
+            pltpu.VMEM((THIRDS, PATCHES, rows, LANES), jnp.bfloat16),
+            pltpu.VMEM((THIRDS, BANDS, rows, SPAN), jnp.float32),
+            pltpu.SemaphoreType.DMA((THIRDS,)),
+            pltpu.SemaphoreType.DMA((THIRDS,)),
+        ],
+        compiler_params=pltpu.CompilerParams(vmem_limit_bytes=24 << 20),
         name="spread",
     )(received)
 
 
 def strip_rows(first):
     first = first.reshape(1, GROUPS * PIECES)
-    blocks = [first]
-    for k in range(1, VISITS):
-        blocks.append(lax.ppermute(first, "visit", [(i, (i + k) % VISITS) for i in range(VISITS)]))
+    other = lax.ppermute(first, "visit", [(i, i ^ 1) for i in range(VISITS)])
+    pair = jnp.concatenate([first, other], axis=1)
+    blocks = [pair]
+    for k in range(2, VISITS, 2):
+        blocks.append(lax.ppermute(pair, "visit", [(i, (i + k) % VISITS) for i in range(VISITS)]))
     return jnp.concatenate(blocks, axis=1).astype(jnp.int32).reshape(-1)
 
 

time: 163 us -> 156 us (0.957)
  starting transfers between devices: 37.9 us -> 33.9 us
  waiting for transfers between devices: 76.4 us -> 73.4 us
    ppermute x7 -> x4, waiting for transfers between devices: 21.1 us -> 14.6 us  [the longest x3 14.6 us: strip_rows(): lax.ppermute(pair, 'visit', [(i, (i + k) % VISITS) for i in range(VISITS)])]
    all_to_all x4, waiting for transfers between devices: 52 us -> 55.5 us  [exchange(): return lax.all_to_all(pieces, axes, split_axis=0, concat_axis=0, tiled=True)]
    all_to_all x4, starting transfers between devices: 23.9 us -> 21.7 us  [exchange(): return lax.all_to_all(pieces, axes, split_axis=0, concat_axis=0, tiled=True)]
    ppermute x7 -> x4, starting transfers between devices: 5.86 us -> 4.09 us  [the longest x3 4.06 us: strip_rows(): lax.ppermute(pair, 'visit', [(i, (i + k) % VISITS) for i in range(VISITS)])]
    pallas_call x2, Pallas kernels: 9.81 us -> 8.05 us  [spread(): pl.pallas_call(spread_body, in_specs=[anywhere], out_specs=anywhere, out_...]
    pallas_call x2, Pallas kernels: 21 us -> 22.7 us  [strip(): pl.pallas_call(strip_body, in_specs=[SMEM, SMEM, pl.BlockSpec(memory_spac...]
  transfers between devices with their start and end apart: 12 -> 9, of which waited for: 7 -> 7; matrix products, arithmetic and copies ran while one was open for 0% -> 0% of each run, Pallas kernels for 23% -> 24%
where the time goes in v6:
time: 156 us; the launch traced here: 155 us
  waiting for transfers between devices  73.4 us (47%)
  Pallas kernels  43.6 us (28%)
  starting transfers between devices  33.9 us (22%)
  local copies, waits for them, and re-layouts  2.7 us (2%)
  between operations  1.6 us (1%)
    all_to_all x4, waiting for transfers between devices, exchange(): return lax.all_to_all(pieces, axes, split_axis=0, concat_axis=0, tiled=True)  55.5 us
    pallas_call x2, Pallas kernels, strip(): pl.pallas_call(strip_body, in_specs=[SMEM, SMEM, pl.BlockSpec(memory_spac...  22.7 us
    all_to_all x4, starting transfers between devices, exchange(): return lax.all_to_all(pieces, axes, split_axis=0, concat_axis=0, tiled=True)  21.7 us
    ppermute x3, waiting for transfers between devices, strip_rows(): lax.ppermute(pair, 'visit', [(i, (i + k) % VISITS) for i in range(VISITS)])  14.6 us
    all_to_all x1, starting transfers between devices, shards(): lax.all_to_all(packed, 'fp', split_axis=0, concat_axis=0, tiled=True)  8.13 us
    pallas_call x2, Pallas kernels, spread(): pl.pallas_call(spread_body, in_specs=[anywhere], out_specs=anywhere, out_...  8.05 us
    pallas_call x1, Pallas kernels, send_flux(): pl.pallas_call(flux_body, grid=(STEPS,), in_specs=[SMEM] * 2 + window_spe...  6.42 us
    pallas_call x1, Pallas kernels, send_weight(): pl.pallas_call(weight_body, grid=(STEPS,), in_specs=[SMEM] * 2 + window_s...  4.83 us
  transfers between devices with their start and end apart: 9, of which 7 were waited for; matrix products, arithmetic and copies ran while one was open for 0% of the time, Pallas kernels for 24%

profile of v6, /device:TPU:0, one launch (start us, length us, event | category | flops | bytes accessed | tf_op | source)
XLA Modules:
  0.0 155.3 jit_solution(17148213469526821573)
XLA Ops:
  1.3 1.6 %pack.1 = (f32[16,24,128]{2,1,0:T(8,128)}, s32[1,128]{1,0:T(1,128)}, f32[1,128]{1,0:T(1,128)}) custom-call(f32[16,16]{1,0:T(8,128)} %mix_ref.1, s32[16]{0:T(128)} %bitcast.22, s32[1,16]{1,0:T(1,128)} %pos_ref.1, f32[1,1,21]{2,1,0:T(1,128)} %psf_ref.1, s32[1,1]{1,0:T(1,128)S(6)} %copy.20.shift_ref, s32[1,32]{1,0:T(1,128)} %bad_ref.1, s32[8]{0:T(128)} %band_ref.1, ...), custom_call_target="tpu_custom_call" | custom-call | tf_op jit(solution)/shard_map/pack/pallas_call | solution.py:338
  2.9 8.1 %all-to-all-start = ((f32[16,24,128]{2,1,0:T(8,128)}), f32[16,24,128]{2,1,0:T(8,128)S(1)}, u32[]{:S(2)}, u32[]{:S(2)}) async-start(f32[16,24,128]{2,1,0:T(8,128)} %get-tuple-element.11), calls=%async_computation | async-start | bytes 393216 | tf_op jit(solution)/shard_map/all_to_all | solution.py:435
  11.0 4.8 %send_weight.1 = (bf16[128,64,128]{2,1,0:T(8,128)(2,1)}, bf16[8,256,512]{2,1,0:T(8,128)(2,1)}) custom-call(s32[1,128]{1,0:T(1,128)} %get-tuple-element.9.table_ref, f32[1,128]{1,0:T(1,128)} %get-tuple-element.10.psf_ref, bf16[1,256,4096]{2,1,0:T(8,128)(2,1)} %right_ref.2, bf16[1,256,4096]{2,1,0:T(8,128)(2,1)} %right_ref.2, bf16[1,256,4096]{2,1,0:T(8,128)(2,1)} %right_ref.2), custom_call_target="tpu_custom_call" | custom-call | tf_op jit(solution)/shard_map/send_weight/pallas_call | solution.py:322
  15.9 3.3 %all-to-all-done.packed_ref = f32[16,24,128]{2,1,0:T(8,128)S(1)} async-done(((f32[16,24,128]{2,1,0:T(8,128)}), f32[16,24,128]{2,1,0:T(8,128)S(1)}, u32[]{:S(2)}, u32[]{:S(2)}) %all-to-all-start) | async-done | bytes 196640 | tf_op jit(solution)/shard_map/all_to_all | solution.py:435
  19.2 6.9 %all-to-all-start.3 = ((bf16[128,64,128]{2,1,0:T(8,128)(2,1)}), bf16[128,64,128]{2,1,0:T(8,128)(2,1)S(1)}, u32[]{:S(2)}, u32[]{:S(2)}) async-start(bf16[128,64,128]{2,1,0:T(8,128)(2,1)} %get-tuple-element.15), calls=%async_computation.3 | async-start | bytes 4194304 | tf_op jit(solution)/shard_map/all_to_all | solution.py:369
  26.4 6.4 %send_flux.1 = bf16[128,64,128]{2,1,0:T(8,128)(2,1)} custom-call(s32[1,128]{1,0:T(1,128)} %get-tuple-element.9.table_ref, f32[1,128]{1,0:T(1,128)} %get-tuple-element.10.psf_ref, bf16[1,256,4096]{2,1,0:T(8,128)(2,1)} %right_ref.3, bf16[1,256,4096]{2,1,0:T(8,128)(2,1)} %right_ref.3, bf16[1,256,4096]{2,1,0:T(8,128)(2,1)} %right_ref.3, ...), custom_call_target="tpu_custom_call" | custom-call | tf_op jit(solution)/shard_map/send_flux/pallas_call | solution.py:352
  32.8 2.4 %collective-permute-start.3 = (f32[1,512]{1,0:T(1,128)S(1)}, f32[1,512]{1,0:T(1,128)S(1)}, u32[]{:S(2)}, u32[]{:S(2)}) collective-permute-start(f32[1,512]{1,0:T(1,128)S(1)} %constant_dynamic-update-slice_fusion), channel_id=1, source_target_pairs={{0,96},{16,112},{32,0},{48,16},{64,32},{80,48},{96,64},{112,80},{1... | collective-permute-start | bytes 6152 | tf_op jit(solution)/shard_map/ppermute | solution.py:409
  35.2 0.8 collective-permute-start.2
  36.0 0.9 collective-permute-start.1
  36.9 13.9 %collective-permute-done.1 = f32[1,512]{1,0:T(1,128)S(1)} collective-permute-done((f32[1,512]{1,0:T(1,128)S(1)}, f32[1,512]{1,0:T(1,128)S(1)}, u32[]{:S(2)}, u32[]{:S(2)}) %collective-permute-start.1) | collective-permute-done | bytes 2080 | tf_op jit(solution)/shard_map/ppermute | solution.py:409
  50.8 0.7 collective-permute-done.2
  51.5 4.3 %all-to-all-done.3 = bf16[128,64,128]{2,1,0:T(8,128)(2,1)S(1)} async-done(((bf16[128,64,128]{2,1,0:T(8,128)(2,1)}), bf16[128,64,128]{2,1,0:T(8,128)(2,1)S(1)}, u32[]{:S(2)}, u32[]{:S(2)}) %all-to-all-start.3) | async-done | bytes 2097184 | tf_op jit(solution)/shard_map/all_to_all | solution.py:369
  55.8 5.8 %all-to-all-start.1 = ((bf16[128,64,128]{2,1,0:T(8,128)(2,1)}), bf16[128,64,128]{2,1,0:T(8,128)(2,1)}, u32[]{:S(2)}, u32[]{:S(2)}) async-start(bf16[128,64,128]{2,1,0:T(8,128)(2,1)} %send_flux.1), calls=%async_computation.1 | async-start | bytes 4194304 | tf_op jit(solution)/shard_map/all_to_all | solution.py:369
  61.6 10.9 %strip.3 = bf16[16,456,128]{2,1,0:T(8,128)(2,1)S(1)} custom-call(s32[1,128]{1,0:T(1,128)S(1)} %copy-done.2, s32[2048]{0:T(1024)S(1)} %convert_element_type.6.rows_ref, bf16[512,16,128]{2,1,0:T(8,128)(2,1)S(1)} %bitcast.14), custom_call_target="tpu_custom_call" | custom-call | tf_op jit(solution)/shard_map/strip/pallas_call | solution.py:373
  72.6 1.2 copy-done
  73.8 17.1 %all-to-all-done.1 = bf16[128,64,128]{2,1,0:T(8,128)(2,1)} async-done(((bf16[128,64,128]{2,1,0:T(8,128)(2,1)}), bf16[128,64,128]{2,1,0:T(8,128)(2,1)}, u32[]{:S(2)}, u32[]{:S(2)}) %all-to-all-start.1) | async-done | bytes 2097184 | tf_op jit(solution)/shard_map/all_to_all | solution.py:369
  90.9 4.6 %all-to-all-start.4 = ((bf16[16,456,128]{2,1,0:T(8,128)(2,1)}), bf16[16,456,128]{2,1,0:T(8,128)(2,1)}, u32[]{:S(2)}, u32[]{:S(2)}) async-start(bf16[16,456,128]{2,1,0:T(8,128)(2,1)} %copy-done), calls=%async_computation.4 | async-start | bytes 3735552 | tf_op jit(solution)/shard_map/all_to_all | solution.py:369
  95.5 11.8 %strip.2 = bf16[16,456,128]{2,1,0:T(8,128)(2,1)S(1)} custom-call(s32[1,128]{1,0:T(1,128)S(1)} %copy-done.2, s32[2048]{0:T(1024)S(1)} %convert_element_type.6.rows_ref, bf16[512,16,128]{2,1,0:T(8,128)(2,1)} %bitcast.5.received_ref), custom_call_target="tpu_custom_call" | custom-call | tf_op jit(solution)/shard_map/strip/pallas_call | solution.py:373
  107.3 1.2 copy-done.1
  108.5 13.6 %all-to-all-done.4.received_ref = bf16[16,456,128]{2,1,0:T(8,128)(2,1)} async-done(((bf16[16,456,128]{2,1,0:T(8,128)(2,1)}), bf16[16,456,128]{2,1,0:T(8,128)(2,1)}, u32[]{:S(2)}, u32[]{:S(2)}) %all-to-all-start.4) | async-done | bytes 1867808 | tf_op jit(solution)/shard_map/all_to_all | solution.py:369
  122.2 4.4 %all-to-all-start.2 = ((bf16[16,456,128]{2,1,0:T(8,128)(2,1)}), bf16[16,456,128]{2,1,0:T(8,128)(2,1)}, u32[]{:S(2)}, u32[]{:S(2)}) async-start(bf16[16,456,128]{2,1,0:T(8,128)(2,1)} %copy-done.1), calls=%async_computation.2 | async-start | bytes 3735552 | tf_op jit(solution)/shard_map/all_to_all | solution.py:369
  126.6 4.0 %spread.3 = f32[4,456,512]{2,1,0:T(8,128)} custom-call(bf16[16,456,128]{2,1,0:T(8,128)(2,1)} %all-to-all-done.4.received_ref), custom_call_target="tpu_custom_call" | custom-call | tf_op jit(solution)/shard_map/spread/pallas_call | solution.py:387
  130.6 20.5 %all-to-all-done.2.received_ref = bf16[16,456,128]{2,1,0:T(8,128)(2,1)} async-done(((bf16[16,456,128]{2,1,0:T(8,128)(2,1)}), bf16[16,456,128]{2,1,0:T(8,128)(2,1)}, u32[]{:S(2)}, u32[]{:S(2)}) %all-to-all-start.2) | async-done | bytes 1867808 | tf_op jit(solution)/shard_map/all_to_all | solution.py:369
  151.1 4.0 %spread.2 = f32[4,456,512]{2,1,0:T(8,128)} custom-call(bf16[16,456,128]{2,1,0:T(8,128)(2,1)} %all-to-all-done.2.received_ref), custom_call_target="tpu_custom_call" | custom-call | tf_op jit(solution)/shard_map/spread/pallas_call | solution.py:387
  (21 shorter events, 0.3 us)
Async XLA Ops:
  2.9 16.3 %all-to-all-start = ((f32[16,24,128]{2,1,0:T(8,128)}), f32[16,24,128]{2,1,0:T(8,128)S(1)}, u32[]{:S(2)}, u32[]{:S(2)}) async-start(f32[16,24,128]{2,1,0:T(8,128)} %get-tuple-element.11), calls=%async_computation | async-start | bytes 393216 | tf_op jit(solution)/shard_map/all_to_all | solution.py:435
  19.2 6.9 %copy-start.3 = (f32[16,24,128]{2,1,0:T(8,128)}, f32[16,24,128]{2,1,0:T(8,128)S(1)}, u32[]{:S(2)}) copy-start(f32[16,24,128]{2,1,0:T(8,128)S(1)} %all-to-all-done.packed_ref) | copy-start | bytes 589828
  19.2 36.6 %all-to-all-start.3 = ((bf16[128,64,128]{2,1,0:T(8,128)(2,1)}), bf16[128,64,128]{2,1,0:T(8,128)(2,1)S(1)}, u32[]{:S(2)}, u32[]{:S(2)}) async-start(bf16[128,64,128]{2,1,0:T(8,128)(2,1)} %get-tuple-element.15), calls=%async_computation.3 | async-start | bytes 4194304 | tf_op jit(solution)/shard_map/all_to_all | solution.py:369
  26.3 6.5 %collective-permute-start = (f32[1,256]{1,0:T(1,128)S(1)}, f32[1,256]{1,0:T(1,128)S(1)}, u32[]{:S(2)}, u32[]{:S(2)}) collective-permute-start(f32[1,256]{1,0:T(1,128)S(1)} %reshape_squeeze.3), channel_id=1, source_target_pairs={{0,16},{16,0},{32,48},{48,32},{64,80},{80,64},{96,112},{112,96},{1... | collective-permute-start | bytes 3080 | tf_op jit(solution)/shard_map/ppermute | solution.py:405
  32.8 18.6 %collective-permute-start.3 = (f32[1,512]{1,0:T(1,128)S(1)}, f32[1,512]{1,0:T(1,128)S(1)}, u32[]{:S(2)}, u32[]{:S(2)}) collective-permute-start(f32[1,512]{1,0:T(1,128)S(1)} %constant_dynamic-update-slice_fusion), channel_id=1, source_target_pairs={{0,96},{16,112},{32,0},{48,16},{64,32},{80,48},{96,64},{112,80},{1... | collective-permute-start | bytes 6152 | tf_op jit(solution)/shard_map/ppermute | solution.py:409
  35.2 16.3 %collective-permute-start.2 = (f32[1,512]{1,0:T(1,128)S(1)}, f32[1,512]{1,0:T(1,128)S(1)}, u32[]{:S(2)}, u32[]{:S(2)}) collective-permute-start(f32[1,512]{1,0:T(1,128)S(1)} %constant_dynamic-update-slice_fusion), channel_id=1, source_target_pairs={{0,64},{16,80},{32,96},{48,112},{64,0},{80,16},{96,32},{112,48},{1... | collective-permute-start | bytes 6152 | tf_op jit(solution)/shard_map/ppermute | solution.py:409
  36.0 14.8 %collective-permute-start.1 = (f32[1,512]{1,0:T(1,128)S(1)}, f32[1,512]{1,0:T(1,128)S(1)}, u32[]{:S(2)}, u32[]{:S(2)}) collective-permute-start(f32[1,512]{1,0:T(1,128)S(1)} %constant_dynamic-update-slice_fusion), channel_id=1, source_target_pairs={{0,32},{16,48},{32,64},{48,80},{64,96},{80,112},{96,0},{112,16},{1... | collective-permute-start | bytes 6152 | tf_op jit(solution)/shard_map/ppermute | solution.py:409
  51.5 10.1 %copy-start.2 = (s32[1,128]{1,0:T(1,128)S(1)}, s32[1,128]{1,0:T(1,128)}, u32[]{:S(2)}) copy-start(s32[1,128]{1,0:T(1,128)} %get-tuple-element.9.table_ref) | copy-start | bytes 1540
  55.8 35.1 %all-to-all-start.1 = ((bf16[128,64,128]{2,1,0:T(8,128)(2,1)}), bf16[128,64,128]{2,1,0:T(8,128)(2,1)}, u32[]{:S(2)}, u32[]{:S(2)}) async-start(bf16[128,64,128]{2,1,0:T(8,128)(2,1)} %send_flux.1), calls=%async_computation.1 | async-start | bytes 4194304 | tf_op jit(solution)/shard_map/all_to_all | solution.py:369
  72.5 1.2 copy-start
  90.9 31.3 %all-to-all-start.4 = ((bf16[16,456,128]{2,1,0:T(8,128)(2,1)}), bf16[16,456,128]{2,1,0:T(8,128)(2,1)}, u32[]{:S(2)}, u32[]{:S(2)}) async-start(bf16[16,456,128]{2,1,0:T(8,128)(2,1)} %copy-done), calls=%async_computation.4 | async-start | bytes 3735552 | tf_op jit(solution)/shard_map/all_to_all | solution.py:369
  107.3 1.2 copy-start.1
  122.2 28.9 %all-to-all-start.2 = ((bf16[16,456,128]{2,1,0:T(8,128)(2,1)}), bf16[16,456,128]{2,1,0:T(8,128)(2,1)}, u32[]{:S(2)}, u32[]{:S(2)}) async-start(bf16[16,456,128]{2,1,0:T(8,128)(2,1)} %copy-done.1), calls=%async_computation.2 | async-start | bytes 3735552 | tf_op jit(solution)/shard_map/all_to_all | solution.py:369

commit v7 on v6

--- a/solution.py
+++ b/solution.py
@@ -120,7 +120,7 @@
 
 
 def pack_body(
-    mix_ref, patch_ref, pos_ref, psf_ref, shift_ref, bad_ref, band_ref, grid_ref, out_ref, table_ref, taps_ref
+    mix_ref, patch_ref, pos_ref, psf_ref, bad_ref, band_ref, shift_ref, grid_ref, out_ref, table_ref, taps_ref
 ):
     group = lax.axis_index("fp")
     lane = lax.broadcasted_iota(jnp.int32, (1, BINS), 1)
@@ -134,7 +134,7 @@
         out_ref[q, GRID_ROWS:] = jnp.broadcast_to(first, (PACKED - GRID_ROWS, BINS))
     for k in range(BAD_COUNT):
         table = jnp.where(lane == AT_BAD + k, bad_ref[0, k], table)
-    table = jnp.where(lane == AT_SHIFT, shift_ref[0, 0], table)
+    table = jnp.where(lane == AT_SHIFT, shift_ref[...], table)
     table = jnp.where(lane == AT_VISIT, lax.axis_index("visit"), table)
     bands = [band_ref[v] for v in range(VISITS)]
     for v in range(VISITS):
@@ -261,28 +261,32 @@
         out_ref[patch] = fold(first, second, low, 2 * SHARE).astype(jnp.bfloat16)
 
 
-def spread_body(received_ref, out_ref, taken_ref, given_ref, in_sems, out_sems):
+def spread_body(received_ref, out_ref, taken_ref, given_ref, in_sem, out_sems):
     rows = FRAME // THIRDS
-    reads = [
-        pltpu.make_async_copy(
-            received_ref.at[:, pl.ds(rows * n, rows)], taken_ref.at[n], in_sems.at[n]
-        )
-        for n in range(THIRDS)
-    ]
+    read = pltpu.make_async_copy(received_ref, taken_ref, in_sem)
     writes = [
         pltpu.make_async_copy(
             given_ref.at[n], out_ref.at[:, pl.ds(rows * n, rows)], out_sems.at[n]
         )
         for n in range(THIRDS)
     ]
-    for read in reads:
-        read.start()
+    read.start()
+    shape = (PARTS * LANES, PARTS * LANES)
+    lane = lax.broadcasted_iota(jnp.int32, shape, 0)
+    column = lax.broadcasted_iota(jnp.int32, shape, 1)
+    source = (column // SHARE % PARTS) * LANES + (column // LANES) * SHARE + column % SHARE
+    order = (lane == source).astype(jnp.bfloat16)
+    read.wait()
     for n in range(THIRDS):
-        reads[n].wait()
         for tile in range(SPAN // LANES):
-            blocks = [taken_ref[n, PARTS * tile + m].astype(jnp.float32) for m in range(PARTS)]
-            for band, block in enumerate(swap_parts(blocks)):
-                given_ref[n, band, :, LANES * tile : LANES * (tile + 1)] = block
+            blocks = [taken_ref[PARTS * tile + m, rows * n : rows * (n + 1)] for m in range(PARTS)]
+            mixed = jnp.dot(
+                jnp.concatenate(blocks, axis=1), order, preferred_element_type=jnp.float32
+            )
+            for band in range(BANDS):
+                given_ref[n, band, :, LANES * tile : LANES * (tile + 1)] = mixed[
+                    :, LANES * band : LANES * (band + 1)
+                ]
         writes[n].start()
     for write in writes:
         write.wait()
@@ -337,7 +341,7 @@
 def pack(*smalls):
     return pl.pallas_call(
         pack_body,
-        in_specs=[SMEM] * (len(smalls) - 1) + [pl.BlockSpec(memory_space=pltpu.VMEM)],
+        in_specs=[SMEM] * (len(smalls) - 2) + [pl.BlockSpec(memory_space=pltpu.VMEM)] * 2,
         out_specs=[pl.BlockSpec(memory_space=pltpu.VMEM)] * 3,
         out_shape=[
             jax.ShapeDtypeStruct((PATCHES, PACKED, BINS), jnp.float32),
@@ -390,9 +394,9 @@
         out_specs=anywhere,
         out_shape=jax.ShapeDtypeStruct((BANDS, FRAME, SPAN), jnp.float32),
         scratch_shapes=[
-            pltpu.VMEM((THIRDS, PATCHES, rows, LANES), jnp.bfloat16),
+            pltpu.VMEM((PATCHES, FRAME, LANES), jnp.bfloat16),
             pltpu.VMEM((THIRDS, BANDS, rows, SPAN), jnp.float32),
-            pltpu.SemaphoreType.DMA((THIRDS,)),
+            pltpu.SemaphoreType.DMA,
             pltpu.SemaphoreType.DMA((THIRDS,)),
         ],
         compiler_params=pltpu.CompilerParams(vmem_limit_bytes=24 << 20),
@@ -427,9 +431,9 @@
         piece_patch[0, :, 0],
         piece_pos,
         psf_taps,
-        warp_shift,
         bad_cols,
         band_of_visit,
+        warp_shift,
         bg_grid,
     )
     packed = lax.all_to_all(packed, "fp", split_axis=0, concat_axis=0, tiled=True)

time: 156 us -> 156 us (level)
  no operation moved by 1% of the time
where the time goes in v7:
time: 156 us; the launch traced here: 155 us
  waiting for transfers between devices  73.5 us (47%)
  Pallas kernels  43.4 us (28%)
  starting transfers between devices  33.9 us (22%)
  local copies, waits for them, and re-layouts  2.7 us (2%)
  between operations  1.6 us (1%)
    all_to_all x4, waiting for transfers between devices, exchange(): return lax.all_to_all(pieces, axes, split_axis=0, concat_axis=0, tiled=True)  55.6 us
    pallas_call x2, Pallas kernels, strip(): pl.pallas_call(strip_body, in_specs=[SMEM, SMEM, pl.BlockSpec(memory_spac...  22.7 us
    all_to_all x4, starting transfers between devices, exchange(): return lax.all_to_all(pieces, axes, split_axis=0, concat_axis=0, tiled=True)  21.7 us
    ppermute x3, waiting for transfers between devices, strip_rows(): lax.ppermute(pair, 'visit', [(i, (i + k) % VISITS) for i in range(VISITS)])  14.6 us
    all_to_all x1, starting transfers between devices, shards(): lax.all_to_all(packed, 'fp', split_axis=0, concat_axis=0, tiled=True)  8.13 us
    pallas_call x2, Pallas kernels, spread(): pl.pallas_call(spread_body, in_specs=[anywhere], out_specs=anywhere, out_...  7.81 us
    pallas_call x1, Pallas kernels, send_flux(): pl.pallas_call(flux_body, grid=(STEPS,), in_specs=[SMEM] * 2 + window_spe...  6.42 us
    pallas_call x1, Pallas kernels, send_weight(): pl.pallas_call(weight_body, grid=(STEPS,), in_specs=[SMEM] * 2 + window_s...  4.83 us
  transfers between devices with their start and end apart: 9, of which 7 were waited for; matrix products, arithmetic and copies ran while one was open for 0% of the time, Pallas kernels for 24%

profile of v7, /device:TPU:0, one launch (start us, length us, event | category | flops | bytes accessed | tf_op | source)
XLA Modules:
  0.0 155.2 jit_solution(13012960534359769766)
XLA Ops:
  1.3 1.6 %pack.1 = (f32[16,24,128]{2,1,0:T(8,128)}, s32[1,128]{1,0:T(1,128)}, f32[1,128]{1,0:T(1,128)}) custom-call(f32[16,16]{1,0:T(8,128)} %mix_ref.1, s32[16]{0:T(128)} %bitcast.22, s32[1,16]{1,0:T(1,128)} %pos_ref.1, f32[1,1,21]{2,1,0:T(1,128)} %psf_ref.1, s32[1,32]{1,0:T(1,128)} %bad_ref.1, s32[8]{0:T(128)} %band_ref.1, s32[1,1]{1,0:T(1,128)S(6)} %copy.20.shift_ref, ...), custom_call_target="tpu_custom_call" | custom-call | tf_op jit(solution)/shard_map/pack/pallas_call | solution.py:342
  2.9 8.1 %all-to-all-start = ((f32[16,24,128]{2,1,0:T(8,128)}), f32[16,24,128]{2,1,0:T(8,128)S(1)}, u32[]{:S(2)}, u32[]{:S(2)}) async-start(f32[16,24,128]{2,1,0:T(8,128)} %get-tuple-element.11), calls=%async_computation | async-start | bytes 393216 | tf_op jit(solution)/shard_map/all_to_all | solution.py:439
  11.0 4.8 %send_weight.1 = (bf16[128,64,128]{2,1,0:T(8,128)(2,1)}, bf16[8,256,512]{2,1,0:T(8,128)(2,1)}) custom-call(s32[1,128]{1,0:T(1,128)} %get-tuple-element.9.table_ref, f32[1,128]{1,0:T(1,128)} %get-tuple-element.10.psf_ref, bf16[1,256,4096]{2,1,0:T(8,128)(2,1)} %right_ref.2, bf16[1,256,4096]{2,1,0:T(8,128)(2,1)} %right_ref.2, bf16[1,256,4096]{2,1,0:T(8,128)(2,1)} %right_ref.2), custom_call_target="tpu_custom_call" | custom-call | tf_op jit(solution)/shard_map/send_weight/pallas_call | solution.py:326
  15.9 3.3 %all-to-all-done.packed_ref = f32[16,24,128]{2,1,0:T(8,128)S(1)} async-done(((f32[16,24,128]{2,1,0:T(8,128)}), f32[16,24,128]{2,1,0:T(8,128)S(1)}, u32[]{:S(2)}, u32[]{:S(2)}) %all-to-all-start) | async-done | bytes 196640 | tf_op jit(solution)/shard_map/all_to_all | solution.py:439
  19.2 6.9 %all-to-all-start.3 = ((bf16[128,64,128]{2,1,0:T(8,128)(2,1)}), bf16[128,64,128]{2,1,0:T(8,128)(2,1)S(1)}, u32[]{:S(2)}, u32[]{:S(2)}) async-start(bf16[128,64,128]{2,1,0:T(8,128)(2,1)} %get-tuple-element.15), calls=%async_computation.3 | async-start | bytes 4194304 | tf_op jit(solution)/shard_map/all_to_all | solution.py:373
  26.4 6.4 %send_flux.1 = bf16[128,64,128]{2,1,0:T(8,128)(2,1)} custom-call(s32[1,128]{1,0:T(1,128)} %get-tuple-element.9.table_ref, f32[1,128]{1,0:T(1,128)} %get-tuple-element.10.psf_ref, bf16[1,256,4096]{2,1,0:T(8,128)(2,1)} %right_ref.3, bf16[1,256,4096]{2,1,0:T(8,128)(2,1)} %right_ref.3, bf16[1,256,4096]{2,1,0:T(8,128)(2,1)} %right_ref.3, ...), custom_call_target="tpu_custom_call" | custom-call | tf_op jit(solution)/shard_map/send_flux/pallas_call | solution.py:356
  32.8 2.4 %collective-permute-start.3 = (f32[1,512]{1,0:T(1,128)S(1)}, f32[1,512]{1,0:T(1,128)S(1)}, u32[]{:S(2)}, u32[]{:S(2)}) collective-permute-start(f32[1,512]{1,0:T(1,128)S(1)} %constant_dynamic-update-slice_fusion), channel_id=1, source_target_pairs={{0,96},{16,112},{32,0},{48,16},{64,32},{80,48},{96,64},{112,80},{1... | collective-permute-start | bytes 6152 | tf_op jit(solution)/shard_map/ppermute | solution.py:413
  35.2 0.8 collective-permute-start.2
  36.0 0.9 collective-permute-start.1
  36.9 13.9 %collective-permute-done.1 = f32[1,512]{1,0:T(1,128)S(1)} collective-permute-done((f32[1,512]{1,0:T(1,128)S(1)}, f32[1,512]{1,0:T(1,128)S(1)}, u32[]{:S(2)}, u32[]{:S(2)}) %collective-permute-start.1) | collective-permute-done | bytes 2080 | tf_op jit(solution)/shard_map/ppermute | solution.py:413
  50.8 0.7 collective-permute-done.2
  51.5 4.3 %all-to-all-done.3 = bf16[128,64,128]{2,1,0:T(8,128)(2,1)S(1)} async-done(((bf16[128,64,128]{2,1,0:T(8,128)(2,1)}), bf16[128,64,128]{2,1,0:T(8,128)(2,1)S(1)}, u32[]{:S(2)}, u32[]{:S(2)}) %all-to-all-start.3) | async-done | bytes 2097184 | tf_op jit(solution)/shard_map/all_to_all | solution.py:373
  55.8 5.8 %all-to-all-start.1 = ((bf16[128,64,128]{2,1,0:T(8,128)(2,1)}), bf16[128,64,128]{2,1,0:T(8,128)(2,1)}, u32[]{:S(2)}, u32[]{:S(2)}) async-start(bf16[128,64,128]{2,1,0:T(8,128)(2,1)} %send_flux.1), calls=%async_computation.1 | async-start | bytes 4194304 | tf_op jit(solution)/shard_map/all_to_all | solution.py:373
  61.6 10.9 %strip.3 = bf16[16,456,128]{2,1,0:T(8,128)(2,1)S(1)} custom-call(s32[1,128]{1,0:T(1,128)S(1)} %copy-done.2, s32[2048]{0:T(1024)S(1)} %convert_element_type.6.rows_ref, bf16[512,16,128]{2,1,0:T(8,128)(2,1)S(1)} %bitcast.14), custom_call_target="tpu_custom_call" | custom-call | tf_op jit(solution)/shard_map/strip/pallas_call | solution.py:377
  72.6 1.2 copy-done
  73.8 17.1 %all-to-all-done.1 = bf16[128,64,128]{2,1,0:T(8,128)(2,1)} async-done(((bf16[128,64,128]{2,1,0:T(8,128)(2,1)}), bf16[128,64,128]{2,1,0:T(8,128)(2,1)}, u32[]{:S(2)}, u32[]{:S(2)}) %all-to-all-start.1) | async-done | bytes 2097184 | tf_op jit(solution)/shard_map/all_to_all | solution.py:373
  90.9 4.6 %all-to-all-start.4 = ((bf16[16,456,128]{2,1,0:T(8,128)(2,1)}), bf16[16,456,128]{2,1,0:T(8,128)(2,1)}, u32[]{:S(2)}, u32[]{:S(2)}) async-start(bf16[16,456,128]{2,1,0:T(8,128)(2,1)} %copy-done), calls=%async_computation.4 | async-start | bytes 3735552 | tf_op jit(solution)/shard_map/all_to_all | solution.py:373
  95.5 11.8 %strip.2 = bf16[16,456,128]{2,1,0:T(8,128)(2,1)S(1)} custom-call(s32[1,128]{1,0:T(1,128)S(1)} %copy-done.2, s32[2048]{0:T(1024)S(1)} %convert_element_type.6.rows_ref, bf16[512,16,128]{2,1,0:T(8,128)(2,1)} %bitcast.5.received_ref), custom_call_target="tpu_custom_call" | custom-call | tf_op jit(solution)/shard_map/strip/pallas_call | solution.py:377
  107.3 1.2 copy-done.1
  108.6 13.6 %all-to-all-done.4.received_ref = bf16[16,456,128]{2,1,0:T(8,128)(2,1)} async-done(((bf16[16,456,128]{2,1,0:T(8,128)(2,1)}), bf16[16,456,128]{2,1,0:T(8,128)(2,1)}, u32[]{:S(2)}, u32[]{:S(2)}) %all-to-all-start.4) | async-done | bytes 1867808 | tf_op jit(solution)/shard_map/all_to_all | solution.py:373
  122.2 4.4 %all-to-all-start.2 = ((bf16[16,456,128]{2,1,0:T(8,128)(2,1)}), bf16[16,456,128]{2,1,0:T(8,128)(2,1)}, u32[]{:S(2)}, u32[]{:S(2)}) async-start(bf16[16,456,128]{2,1,0:T(8,128)(2,1)} %copy-done.1), calls=%async_computation.2 | async-start | bytes 3735552 | tf_op jit(solution)/shard_map/all_to_all | solution.py:373
  126.6 3.9 %spread.3 = f32[4,456,512]{2,1,0:T(8,128)} custom-call(bf16[16,456,128]{2,1,0:T(8,128)(2,1)} %all-to-all-done.4.received_ref), custom_call_target="tpu_custom_call" | custom-call | tf_op jit(solution)/shard_map/spread/pallas_call | solution.py:391
  130.5 20.6 %all-to-all-done.2.received_ref = bf16[16,456,128]{2,1,0:T(8,128)(2,1)} async-done(((bf16[16,456,128]{2,1,0:T(8,128)(2,1)}), bf16[16,456,128]{2,1,0:T(8,128)(2,1)}, u32[]{:S(2)}, u32[]{:S(2)}) %all-to-all-start.2) | async-done | bytes 1867808 | tf_op jit(solution)/shard_map/all_to_all | solution.py:373
  151.1 3.9 %spread.2 = f32[4,456,512]{2,1,0:T(8,128)} custom-call(bf16[16,456,128]{2,1,0:T(8,128)(2,1)} %all-to-all-done.2.received_ref), custom_call_target="tpu_custom_call" | custom-call | tf_op jit(solution)/shard_map/spread/pallas_call | solution.py:391
  (21 shorter events, 0.3 us)
Async XLA Ops:
  2.9 16.3 %all-to-all-start = ((f32[16,24,128]{2,1,0:T(8,128)}), f32[16,24,128]{2,1,0:T(8,128)S(1)}, u32[]{:S(2)}, u32[]{:S(2)}) async-start(f32[16,24,128]{2,1,0:T(8,128)} %get-tuple-element.11), calls=%async_computation | async-start | bytes 393216 | tf_op jit(solution)/shard_map/all_to_all | solution.py:439
  19.2 6.9 %copy-start.3 = (f32[16,24,128]{2,1,0:T(8,128)}, f32[16,24,128]{2,1,0:T(8,128)S(1)}, u32[]{:S(2)}) copy-start(f32[16,24,128]{2,1,0:T(8,128)S(1)} %all-to-all-done.packed_ref) | copy-start | bytes 589828
  19.2 36.6 %all-to-all-start.3 = ((bf16[128,64,128]{2,1,0:T(8,128)(2,1)}), bf16[128,64,128]{2,1,0:T(8,128)(2,1)S(1)}, u32[]{:S(2)}, u32[]{:S(2)}) async-start(bf16[128,64,128]{2,1,0:T(8,128)(2,1)} %get-tuple-element.15), calls=%async_computation.3 | async-start | bytes 4194304 | tf_op jit(solution)/shard_map/all_to_all | solution.py:373
  26.3 6.5 %collective-permute-start = (f32[1,256]{1,0:T(1,128)S(1)}, f32[1,256]{1,0:T(1,128)S(1)}, u32[]{:S(2)}, u32[]{:S(2)}) collective-permute-start(f32[1,256]{1,0:T(1,128)S(1)} %reshape_squeeze.3), channel_id=1, source_target_pairs={{0,16},{16,0},{32,48},{48,32},{64,80},{80,64},{96,112},{112,96},{1... | collective-permute-start | bytes 3080 | tf_op jit(solution)/shard_map/ppermute | solution.py:409
  32.8 18.6 %collective-permute-start.3 = (f32[1,512]{1,0:T(1,128)S(1)}, f32[1,512]{1,0:T(1,128)S(1)}, u32[]{:S(2)}, u32[]{:S(2)}) collective-permute-start(f32[1,512]{1,0:T(1,128)S(1)} %constant_dynamic-update-slice_fusion), channel_id=1, source_target_pairs={{0,96},{16,112},{32,0},{48,16},{64,32},{80,48},{96,64},{112,80},{1... | collective-permute-start | bytes 6152 | tf_op jit(solution)/shard_map/ppermute | solution.py:413
  35.2 16.3 %collective-permute-start.2 = (f32[1,512]{1,0:T(1,128)S(1)}, f32[1,512]{1,0:T(1,128)S(1)}, u32[]{:S(2)}, u32[]{:S(2)}) collective-permute-start(f32[1,512]{1,0:T(1,128)S(1)} %constant_dynamic-update-slice_fusion), channel_id=1, source_target_pairs={{0,64},{16,80},{32,96},{48,112},{64,0},{80,16},{96,32},{112,48},{1... | collective-permute-start | bytes 6152 | tf_op jit(solution)/shard_map/ppermute | solution.py:413
  36.0 14.8 %collective-permute-start.1 = (f32[1,512]{1,0:T(1,128)S(1)}, f32[1,512]{1,0:T(1,128)S(1)}, u32[]{:S(2)}, u32[]{:S(2)}) collective-permute-start(f32[1,512]{1,0:T(1,128)S(1)} %constant_dynamic-update-slice_fusion), channel_id=1, source_target_pairs={{0,32},{16,48},{32,64},{48,80},{64,96},{80,112},{96,0},{112,16},{1... | collective-permute-start | bytes 6152 | tf_op jit(solution)/shard_map/ppermute | solution.py:413
  51.5 10.1 %copy-start.2 = (s32[1,128]{1,0:T(1,128)S(1)}, s32[1,128]{1,0:T(1,128)}, u32[]{:S(2)}) copy-start(s32[1,128]{1,0:T(1,128)} %get-tuple-element.9.table_ref) | copy-start | bytes 1540
  55.8 35.1 %all-to-all-start.1 = ((bf16[128,64,128]{2,1,0:T(8,128)(2,1)}), bf16[128,64,128]{2,1,0:T(8,128)(2,1)}, u32[]{:S(2)}, u32[]{:S(2)}) async-start(bf16[128,64,128]{2,1,0:T(8,128)(2,1)} %send_flux.1), calls=%async_computation.1 | async-start | bytes 4194304 | tf_op jit(solution)/shard_map/all_to_all | solution.py:373
  72.6 1.2 copy-start
  90.9 31.3 %all-to-all-start.4 = ((bf16[16,456,128]{2,1,0:T(8,128)(2,1)}), bf16[16,456,128]{2,1,0:T(8,128)(2,1)}, u32[]{:S(2)}, u32[]{:S(2)}) async-start(bf16[16,456,128]{2,1,0:T(8,128)(2,1)} %copy-done), calls=%async_computation.4 | async-start | bytes 3735552 | tf_op jit(solution)/shard_map/all_to_all | solution.py:373
  107.3 1.2 copy-start.1
  122.2 28.9 %all-to-all-start.2 = ((bf16[16,456,128]{2,1,0:T(8,128)(2,1)}), bf16[16,456,128]{2,1,0:T(8,128)(2,1)}, u32[]{:S(2)}, u32[]{:S(2)}) async-start(bf16[16,456,128]{2,1,0:T(8,128)(2,1)} %copy-done.1), calls=%async_computation.2 | async-start | bytes 3735552 | tf_op jit(solution)/shard_map/all_to_all | solution.py:373
